TPU v7x, 256 devices: a whole 4x4x8 slice. The times are simulated.
256 devices in a mesh: strip: 16 (over x, y), tile: 16 (over z, core).
Axes of the slice: x: 4, y: 4, z: 8, core: 2. Of those that a mesh axis runs over, the one named last changes fastest.
Arguments:
- object_field: float32 [2, 2, 2048, 2048], P(None, None, 'strip', 'tile'), may hold values from -1 to 1
- probe_modes: float32 [2, 4, 256, 256], replicated, may hold values from -6 to 6
- offsets: int32 [512, 2], P(('strip', 'tile')), may hold values from 0 to 2047, as said below
- measured: float32 [512, 256, 256], P(('strip', 'tile')), may hold values from 0.5 to 6
Outputs:
- object_grad: float32 [2, 2, 2048, 2048], P(None, None, 'strip', 'tile')
- probe_grad: float32 [2, 4, 256, 256], replicated
Inputs may be any that keep to these rules, and one draw needn't show every extreme that they name: `offsets`: column 0 is a window's row offset, column 1 its column offset. A window held by the device with strip index s and tile index t has its row offset between s * 128 and (s + 1) * 128 - 1 and its column offset between t * 128 and (t + 1) * 128 - 1.
All inputs are finite; a program needn't handle non-finite values.
Results may differ from a plain program's by a relative error of at most 0.0003.
Values sent between devices are 32-bit elements; how exact they have to be, the bound alone decides.
No kernel may reach another device: no remote copies, remote signals or barrier semaphores. Data moves between devices by JAX's collectives and lax.ppermute only.
A program may use at most 64 MiB of HBM per device.

v0:
```python
import math

import jax
import jax.numpy as jnp
from jax import lax
from jax.sharding import PartitionSpec as P

TWO_PI = 6.283185307179586
FRESNEL = 0.5


def passed_along(value, axis, steps):
    count = lax.axis_size(axis)
    pairs = [(source, (source + steps) % count) for source in range(count)]
    return lax.ppermute(value, axis, pairs)


def product_left(matrix, field):
    return jnp.einsum("ij,...jk->...ik", matrix, field, precision=lax.Precision.HIGHEST)


def product_right(field, matrix):
    return jnp.einsum("...ij,jk->...ik", field, matrix, precision=lax.Precision.HIGHEST)


def sandwich(matrix_re, matrix_im, field_re, field_im):
    inner_re = product_left(matrix_re, field_re) - product_left(matrix_im, field_im)
    inner_im = product_left(matrix_re, field_im) + product_left(matrix_im, field_re)
    outer_re = product_right(inner_re, matrix_re) - product_right(inner_im, matrix_im)
    outer_im = product_right(inner_re, matrix_im) + product_right(inner_im, matrix_re)
    return (outer_re, outer_im)


def make_tables(length):
    counter = jnp.arange(length, dtype=jnp.int32)
    product = counter[:, None] * counter[None, :] % length
    angles = product.astype(jnp.float32) * (TWO_PI / length)
    factor = 1.0 / math.sqrt(length)
    four_re = jnp.cos(angles) * factor
    four_im = -jnp.sin(angles) * factor
    centred = (counter + length // 2) % length - length // 2
    phases = -0.5 * TWO_PI * FRESNEL * (centred * centred).astype(jnp.float32) / length
    kernel_re = jnp.cos(phases)
    kernel_im = jnp.sin(phases)
    left_re = four_re * kernel_re[None, :] + four_im * kernel_im[None, :]
    left_im = four_re * kernel_im[None, :] - four_im * kernel_re[None, :]
    highest = lax.Precision.HIGHEST
    prop_re = jnp.dot(left_re, four_re, precision=highest) - jnp.dot(
        left_im, four_im, precision=highest
    )
    prop_im = jnp.dot(left_re, four_im, precision=highest) + jnp.dot(
        left_im, four_re, precision=highest
    )
    return (four_re, four_im, prop_re, prop_im)


def window_grads(window, probe_modes, amplitude, tables):
    four_re, four_im, prop_re, prop_im = tables
    top_re, top_im = (window[0, 0], window[1, 0])
    low_re, low_im = (window[0, 1], window[1, 1])
    probe_re, probe_im = (probe_modes[0], probe_modes[1])
    entry_re = probe_re * top_re - probe_im * top_im
    entry_im = probe_re * top_im + probe_im * top_re
    moved_re, moved_im = sandwich(prop_re, prop_im, entry_re, entry_im)
    exit_re = moved_re * low_re - moved_im * low_im
    exit_im = moved_re * low_im + moved_im * low_re
    far_re, far_im = sandwich(four_re, four_im, exit_re, exit_im)
    intensity = jnp.sum(far_re * far_re + far_im * far_im, axis=0)
    scaling = 1.0 - amplitude / jnp.sqrt(intensity + 1.0)
    misfit_re = scaling * far_re
    misfit_im = scaling * far_im
    back_re, back_im = sandwich(four_re, -four_im, misfit_re, misfit_im)
    grad_low_re = jnp.sum(moved_re * back_re + moved_im * back_im, axis=0)
    grad_low_im = jnp.sum(moved_re * back_im - moved_im * back_re, axis=0)
    behind_re = low_re * back_re + low_im * back_im
    behind_im = low_re * back_im - low_im * back_re
    source_re, source_im = sandwich(prop_re, -prop_im, behind_re, behind_im)
    grad_top_re = jnp.sum(probe_re * source_re + probe_im * source_im, axis=0)
    grad_top_im = jnp.sum(probe_re * source_im - probe_im * source_re, axis=0)
    grad_probe_re = top_re * source_re + top_im * source_im
    grad_probe_im = top_re * source_im - top_im * source_re
    window_grad = jnp.stack(
        [jnp.stack([grad_top_re, grad_low_re]), jnp.stack([grad_top_im, grad_low_im])]
    )
    probe_grad = jnp.stack([grad_probe_re, grad_probe_im])
    return (window_grad, probe_grad)


def per_device(object_field, probe_modes, offsets, measured):
    tile_size = object_field.shape[2]
    slices = object_field.shape[1]
    window_size = probe_modes.shape[3]
    strip_count = lax.axis_size("strip")
    tile_count = lax.axis_size("tile")
    full_rows = tile_size * strip_count
    full_cols = tile_size * tile_count
    bands_below = (window_size + tile_size - 1) // tile_size
    ext_rows = (bands_below + 1) * tile_size
    rows_local = (offsets[:, 0] - lax.axis_index("strip") * tile_size) % full_rows
    cols_local = (offsets[:, 1] - lax.axis_index("tile") * tile_size) % full_cols
    tables = make_tables(window_size)
    right_tiles = [
        passed_along(object_field, "tile", -distance) for distance in range(1, bands_below + 1)
    ]
    tile_row = jnp.concatenate([object_field] + right_tiles, axis=3)
    lower_rows = [
        passed_along(tile_row, "strip", -distance) for distance in range(1, bands_below + 1)
    ]
    local_block = jnp.concatenate([tile_row] + lower_rows, axis=2)

    def single_cut(pair):
        corner = (jnp.int32(0), jnp.int32(0), pair[0], pair[1])
        return lax.dynamic_slice(local_block, corner, (2, slices, window_size, window_size))

    windows = lax.map(single_cut, jnp.stack([rows_local, cols_local], axis=1))
    grads_window, grads_probe = jax.vmap(window_grads, in_axes=(0, None, 0, None))(
        windows, probe_modes, measured, tables
    )
    probe_grad = lax.psum(jnp.sum(grads_probe, axis=0), ("strip", "tile"))

    def single_add(position, running):
        corner = (jnp.int32(0), jnp.int32(0), rows_local[position], cols_local[position])
        current = lax.dynamic_slice(running, corner, grads_window.shape[1:])
        return lax.dynamic_update_slice(running, current + grads_window[position], corner)

    grad_block = lax.fori_loop(
        0,
        grads_window.shape[0],
        single_add,
        jnp.zeros((2, slices, ext_rows, ext_rows), jnp.float32),
    )
    band_part = grad_block[:, :, :tile_size, :]
    for distance in range(1, bands_below + 1):
        band_part = band_part + passed_along(
            grad_block[:, :, distance * tile_size : (distance + 1) * tile_size, :],
            "strip",
            distance,
        )
    object_grad = band_part[..., :tile_size]
    for distance in range(1, bands_below + 1):
        object_grad = object_grad + passed_along(
            band_part[..., distance * tile_size : (distance + 1) * tile_size], "tile", distance
        )
    return (object_grad, probe_grad)


def solution(mesh):
    in_specs = (
        P(None, None, "strip", "tile"),
        P(),
        P(("strip", "tile"), None),
        P(("strip", "tile"), None, None),
    )
    out_specs = (P(None, None, "strip", "tile"), P())
    return jax.shard_map(
        per_device, mesh=mesh, in_specs=in_specs, out_specs=out_specs, check_vma=False
    )
```

profile of v0, /device:TPU:1, one launch (start us, length us, event | category | flops | bytes accessed | tf_op | source)
XLA Modules:
  0.0 565.4 jit_solution(2427298918894452596)
XLA Ops:
  20.8 5.0 collective-permute-start.2
  29.3 21.3 %collective-permute-done.2 = f32[2,2,128,384]{3,2,1,0:T(8,128)} collective-permute-done((f32[2,2,128,384]{3,2,1,0:T(8,128)S(1)}, f32[2,2,128,384]{3,2,1,0:T(8,128)}, u32[]{:S(2)}, u32[]{:S(2)}) %collective-permute-start.2) | collective-permute-done | bytes 786464 | tf_op jit(solution)/shard_map/ppermute | solution.py:15
  50.6 16.0 %collective-permute-done.3 = f32[2,2,128,384]{3,2,1,0:T(8,128)} collective-permute-done((f32[2,2,128,384]{3,2,1,0:T(8,128)S(1)}, f32[2,2,128,384]{3,2,1,0:T(8,128)}, u32[]{:S(2)}, u32[]{:S(2)}) %collective-permute-start.3) | collective-permute-done | bytes 786464 | tf_op jit(solution)/shard_map/ppermute | solution.py:15
  69.6 14.6 %while.23 = (s32[]{:T(128)}, f32[2,2,2,256,256]{4,3,2,1,0:T(8,128)}, s32[2,2]{1,0:T(2,128)S(1)}, f32[2,2,384,384]{3,2,1,0:T(8,128)}, s32[]{:T(128)}, /*index=5*/s32[]{:T(128)}, s32[]{:T(128)}) while((s32[]{:T(128)}, f32[2,2,2,256,256]{4,3,2,1,0:T(8,128)}, s32[2,2]{1,0:T(2,128)S(1)}, f32[2,2,384,384]{3,2,1,0:T(8,128)}, s32[]{:T(128)}, ...), condition=%wide.region_1.2_spmd, body=%wide.region_0.1_spmd.sunk | while | flops 8 | bytes 2097853 | solution.py:115
  115.3 4.6 fusion.121
  119.9 5.0 fusion.118
  124.9 4.6 convolution_add_fusion.1
  134.1 4.6 fusion.16
  138.8 4.7 convolution_subtract_fusion.1
  143.4 4.6 fusion.56
  148.0 5.0 add_reduce_fusion.2
  157.6 4.9 fusion.36
  162.5 4.5 fusion.47
  167.1 4.5 fusion.10
  171.6 4.6 fusion.8
  185.3 5.5 add_reduce_fusion
  216.9 7.1 %add_bitcast_fusion = (f32[1,2,4,256,256]{4,3,2,1,0:T(8,128)}, f32[1,2,4,256,256]{4,3,2,1,0:T(8,128)}, f32[2,256,256]{2,1,0:T(8,128)S(1)}, f32[2,256,256]{2,1,0:T(8,128)S(1)}) fusion(f32[2,4,256,256]{3,2,1,0:T(8,128)S(1)} %fusion.71, f32[2,256,256]{2,1,0:T(8,128)S(1)} %get-tuple-element.154, f32[2,256,256]{2,1,0:T(8,128)S(1)} %get-tuple-element.155, ...), kind=kOutput, calls=%fused_computation.39 | convolution fusion | flops 1618214912 | bytes 14942208 | tf_op jit(solution)/shard_map/vmap(...ij,jk->...ik)/dot_general | solution.py:23
  225.8 44.0 %while.24 = (s32[]{:T(128)}, f32[2,2,384,384]{3,2,1,0:T(8,128)S(1)}, s32[2]{0:T(128)S(1)}, s32[2]{0:T(128)S(1)}, f32[2,2,2,256,256]{4,3,2,1,0:T(8,128)}, /*index=5*/s32[]{:T(128)}, s32[]{:T(128)}, s32[]{:T(128)}) while((s32[]{:T(128)}, f32[2,2,384,384]{3,2,1,0:T(8,128)S(1)}, s32[2]{0:T(128)S(1)}, s32[2]{0:T(128)S(1)}, ...), condition=%wide.region_8.9_spmd, body=%wide.region_7.8_spmd.sunk | while | flops 262152 | bytes 5243073 | solution.py:126
  231.9 15.7 %dynamic_update_slice.15 = f32[2,2,384,384]{3,2,1,0:T(8,128)S(1)} dynamic-update-slice(f32[2,2,384,384]{3,2,1,0:T(8,128)S(1)} %get-tuple-element.259, f32[2,2,256,256]{3,2,1,0:T(8,128)S(1)} %bitcast_add_fusion.2, s32[]{:T(128)} %constant.100.clone.1..sunk.1, s32[]{:T(128)} %constant.100.clone.1..sunk.1, s32[]{:T(128)S(6)} %select_n.225, s32[]{:T(128)S(6)} %select_n.226) | dynamic-update-slice | bytes 2097156 | tf_op jit(solution)/shard_map/while/body/eval_jaxpr/dynamic_update_slice | solution.py:124
  253.8 16.0 %dynamic_update_slice.15 = f32[2,2,384,384]{3,2,1,0:T(8,128)S(1)} dynamic-update-slice(f32[2,2,384,384]{3,2,1,0:T(8,128)S(1)} %get-tuple-element.259, f32[2,2,256,256]{3,2,1,0:T(8,128)S(1)} %bitcast_add_fusion.2, s32[]{:T(128)} %constant.100.clone.1..sunk.1, s32[]{:T(128)} %constant.100.clone.1..sunk.1, s32[]{:T(128)S(6)} %select_n.225, s32[]{:T(128)S(6)} %select_n.226) | dynamic-update-slice | bytes 2097156 | tf_op jit(solution)/shard_map/while/body/eval_jaxpr/dynamic_update_slice | solution.py:124
  271.1 5.8 %collective-permute-start.5 = (f32[2,2,128,384]{3,2,1,0:T(8,128)}, f32[2,2,128,384]{3,2,1,0:T(8,128)}, u32[]{:S(2)}, u32[]{:S(2)}) collective-permute-start(f32[2,2,128,384]{3,2,1,0:T(8,128)} %get-tuple-element.151), channel_id=1, source_target_pairs={{0,32},{16,48},{32,64},{48,80},{64,96},{80,112},{96,128},{112,144}... | collective-permute-start | bytes 2359304 | tf_op jit(solution)/shard_map/ppermute | solution.py:15
  280.3 29.4 %collective-permute-done.4 = f32[2,2,128,384]{3,2,1,0:T(8,128)S(1)} collective-permute-done((f32[2,2,128,384]{3,2,1,0:T(8,128)}, f32[2,2,128,384]{3,2,1,0:T(8,128)S(1)}, u32[]{:S(2)}, u32[]{:S(2)}) %collective-permute-start.4) | collective-permute-done | bytes 786464 | tf_op jit(solution)/shard_map/ppermute | solution.py:15
  315.3 11.0 %collective-permute-done.7 = f32[2,2,128,128]{3,2,1,0:T(8,128)S(1)} collective-permute-done((f32[2,2,128,128]{3,2,1,0:T(8,128)S(1)}, f32[2,2,128,128]{3,2,1,0:T(8,128)S(1)}, u32[]{:S(2)}, u32[]{:S(2)}) %collective-permute-start.7) | collective-permute-done | bytes 262176 | tf_op jit(solution)/shard_map/ppermute | solution.py:15
  327.0 228.2 %all-reduce.2.cloned.1.call-done = f32[2,4,256,256]{3,2,1,0:T(8,128)} async-done(((f32[2,4,256,256]{3,2,1,0:T(8,128)}), f32[2,4,256,256]{3,2,1,0:T(8,128)}) %all-reduce.2.cloned.1.call-update) | async-done | bytes 2097168 | tf_op jit(solution)/shard_map/psum | solution.py:119
  (79 shorter events, 123.3 us)
Async XLA Ops:
  7.2 8.7 %copy-start.4 = (s32[2,2]{1,0:T(2,128)S(1)}, s32[2,2]{1,0:T(2,128)}, u32[]{:S(2)}) copy-start(s32[2,2]{1,0:T(2,128)} %param.10) | copy-start | bytes 52
  7.2 548.1 %all-reduce.2.cloned.1.call-start = ((), (), s32[]{:S(2)}) async-start(), calls=%async_computation | async-start | bytes 4194304 | tf_op jit(solution)/shard_map/psum | solution.py:119
  7.2 10.4 %collective-permute-start = (f32[2,2,128,128]{3,2,1,0:T(8,128)}, f32[2,2,128,128]{3,2,1,0:T(8,128)S(1)}, u32[]{:S(2)}, u32[]{:S(2)}) collective-permute-start(f32[2,2,128,128]{3,2,1,0:T(8,128)} %param.8), channel_id=1, source_target_pairs={{0,15},{1,0},{2,1},{3,2},{4,3},{5,4},{6,5},{7,6},{8,7},{9,8},{10,9... | collective-permute-start | bytes 786440 | tf_op jit(solution)/shard_map/ppermute | solution.py:15
  10.5 10.3 %collective-permute-start.1 = (f32[2,2,128,128]{3,2,1,0:T(8,128)}, f32[2,2,128,128]{3,2,1,0:T(8,128)S(1)}, u32[]{:S(2)}, u32[]{:S(2)}) collective-permute-start(f32[2,2,128,128]{3,2,1,0:T(8,128)} %param.8), channel_id=1, source_target_pairs={{0,14},{1,15},{2,0},{3,1},{4,2},{5,3},{6,4},{7,5},{8,6},{9,7},{10,... | collective-permute-start | bytes 786440 | tf_op jit(solution)/shard_map/ppermute | solution.py:15
  14.4 3.2 copy-start.3
  20.8 29.8 %collective-permute-start.2 = (f32[2,2,128,384]{3,2,1,0:T(8,128)S(1)}, f32[2,2,128,384]{3,2,1,0:T(8,128)}, u32[]{:S(2)}, u32[]{:S(2)}) collective-permute-start(f32[2,2,128,384]{3,2,1,0:T(8,128)S(1)} %constant_dynamic-update-slice_fusion), channel_id=1, source_target_pairs={{0,240},{16,0},{32,16},{48,32},{64,48},{80,64},{96,80},{112,96},{1... | collective-permute-start | bytes 2359304 | tf_op jit(solution)/shard_map/ppermute | solution.py:15
  25.8 40.9 %collective-permute-start.3 = (f32[2,2,128,384]{3,2,1,0:T(8,128)S(1)}, f32[2,2,128,384]{3,2,1,0:T(8,128)}, u32[]{:S(2)}, u32[]{:S(2)}) collective-permute-start(f32[2,2,128,384]{3,2,1,0:T(8,128)S(1)} %constant_dynamic-update-slice_fusion), channel_id=1, source_target_pairs={{0,224},{16,240},{32,0},{48,16},{64,32},{80,48},{96,64},{112,80},{... | collective-permute-start | bytes 2359304 | tf_op jit(solution)/shard_map/ppermute | solution.py:15
  26.2 2.9 copy-start.1
  148.0 5.0 copy-start.2
  269.8 7.1 %copy-start = (f32[1,2,4,256,256]{4,3,2,1,0:T(8,128)S(1)}, f32[1,2,4,256,256]{4,3,2,1,0:T(8,128)}, u32[]{:S(2)}) copy-start(f32[1,2,4,256,256]{4,3,2,1,0:T(8,128)} %get-tuple-element.146) | copy-start | bytes 6291460
  271.0 38.7 %collective-permute-start.4 = (f32[2,2,128,384]{3,2,1,0:T(8,128)}, f32[2,2,128,384]{3,2,1,0:T(8,128)S(1)}, u32[]{:S(2)}, u32[]{:S(2)}) collective-permute-start(f32[2,2,128,384]{3,2,1,0:T(8,128)} %get-tuple-element.150), channel_id=1, source_target_pairs={{0,16},{16,32},{32,48},{48,64},{64,80},{80,96},{96,112},{112,128},... | collective-permute-start | bytes 2359304 | tf_op jit(solution)/shard_map/ppermute | solution.py:15
  271.1 38.7 %collective-permute-start.5 = (f32[2,2,128,384]{3,2,1,0:T(8,128)}, f32[2,2,128,384]{3,2,1,0:T(8,128)}, u32[]{:S(2)}, u32[]{:S(2)}) collective-permute-start(f32[2,2,128,384]{3,2,1,0:T(8,128)} %get-tuple-element.151), channel_id=1, source_target_pairs={{0,32},{16,48},{32,64},{48,80},{64,96},{80,112},{96,128},{112,144}... | collective-permute-start | bytes 2359304 | tf_op jit(solution)/shard_map/ppermute | solution.py:15
  311.0 4.3 collective-permute-start.6
  311.0 15.3 %collective-permute-start.7 = (f32[2,2,128,128]{3,2,1,0:T(8,128)S(1)}, f32[2,2,128,128]{3,2,1,0:T(8,128)S(1)}, u32[]{:S(2)}, u32[]{:S(2)}) collective-permute-start(f32[2,2,128,128]{3,2,1,0:T(8,128)S(1)} %get-tuple-element.159), channel_id=1, source_target_pairs={{0,2},{1,3},{2,4},{3,5},{4,6},{5,7},{6,8},{7,9},{8,10},{9,11},{10,... | collective-permute-start | bytes 786440 | tf_op jit(solution)/shard_map/ppermute | solution.py:15
Sparse Core Ops, SparseCore 0:
  280.4 274.8 all-reduce.1
where the time goes:
time: 574 us; the launch traced here: 565 us
  waiting for transfers between devices  312 us (54%)
  matrix products  144 us (25%)
  local copies, waits for them, and re-layouts  47 us (8%)
  starting transfers between devices  19.4 us (3%)
  loops' own time  14.7 us (3%)
  between operations  14.7 us (3%)
  other arithmetic  13.6 us (2%)
    psum x1, waiting for transfers between devices, per_device(): probe_grad = lax.psum(jnp.sum(grads_probe, axis=0), ('strip', 'tile'))  228 us
    ppermute x8, waiting for transfers between devices, passed_along(): return lax.ppermute(value, axis, pairs)  84.1 us
    dot_general x16, matrix products, product_right(): jnp.einsum('...ij,jk->...ik', field, matrix, precision=lax.Precision.HIGH...  70.5 us
    dot_general x16, matrix products, product_left(): jnp.einsum('ij,...jk->...ik', matrix, field, precision=lax.Precision.HIGH...  67.3 us
    dynamic_update_slice x2, local copies, waits for them, and re-layouts, single_add(): lax.dynamic_update_slice(running, current + grads_window[position], corner)  31.6 us
    ppermute x8, starting transfers between devices, passed_along(): return lax.ppermute(value, axis, pairs)  19.4 us
  transfers between devices with their start and end apart: 9, of which 7 were waited for; matrix products, arithmetic and copies ran while one was open for 2% of the time, Pallas kernels for 0%

commit v1 on v0

v1 whole, which is shorter than its diff:
```python
import jax
import jax.numpy as jnp
import ml_dtypes
import numpy as np
from jax import lax
from jax.experimental import pallas as pl
from jax.experimental.pallas import tpu as pltpu
from jax.sharding import PartitionSpec as P

FRESNEL = 0.5
BF, F32 = jnp.bfloat16, jnp.float32


def transform_tables(length):
    counter = np.arange(length)
    angles = (counter[:, None] * counter[None, :] % length) * (2 * np.pi / length)
    four = (np.cos(angles) - 1j * np.sin(angles)) / np.sqrt(length)
    centred = (counter + length // 2) % length - length // 2
    kern = np.exp(-1j * np.pi * FRESNEL * centred * centred / length)
    prop = (np.conj(four) * kern[None, :]) @ four
    parts = []
    for matrix in (four.real, four.imag, prop.real, prop.imag):
        high = matrix.astype(np.float32).astype(ml_dtypes.bfloat16)
        low = (matrix - high.astype(np.float64)).astype(np.float32)
        parts += [high, low.astype(ml_dtypes.bfloat16)]
    return np.stack(parts)


def halves(value):
    high = value.astype(BF)
    return high, (value - high.astype(F32)).astype(BF)


def product(a_high, a_low, b_high, b_low):
    total = jnp.dot(a_high, b_high, preferred_element_type=F32)
    total = total + jnp.dot(a_low, b_high, preferred_element_type=F32)
    return total + jnp.dot(a_high, b_low, preferred_element_type=F32)


FOUR, FOUR_CONJ, PROP, PROP_CONJ = 0, 1, 2, 3


def window_kernel(
    offsets, left, middle, right, probe, measured, base,
    grad_left, grad_middle, grad_right, probe_grad,
    window, moved, far, scaling, grads, tables, wide,
):
    n = probe.shape[2]
    modes = probe.shape[1]
    rows, tile = middle.shape[2], middle.shape[3]
    count = measured.shape[0]
    wide[:, :, :, :tile] = left[...]
    wide[:, :, :, tile : 2 * tile] = middle[...]
    wide[:, :, :, 2 * tile :] = right[...]
    for field in range(2):
        for part in range(2):
            re, im = base[4 * field + part], base[4 * field + 2 + part]
            for conj in range(2):
                which = 2 * field + conj
                upper, lower = (im, -im) if conj == 0 else (-im, im)
                tables[which, part, :n, :n] = re
                tables[which, part, n:, n:] = re
                tables[which, part, :n, n:] = upper
                tables[which, part, n:, :n] = lower

    def sandwich(re, im, which):
        re_high, re_low = halves(re)
        im_high, im_low = halves(im)
        inner = product(
            jnp.concatenate([re_high, im_high], axis=1),
            jnp.concatenate([re_low, im_low], axis=1),
            tables[which, 0],
            tables[which, 1],
        )
        re_high, re_low = halves(inner[:, :n])
        im_high, im_low = halves(inner[:, n:])
        outer = product(
            tables[which ^ 1, 0],
            tables[which ^ 1, 1],
            jnp.concatenate([re_high, im_high], axis=0),
            jnp.concatenate([re_low, im_low], axis=0),
        )
        return outer[:n], outer[n:]

    probe_grad[...] = jnp.zeros_like(probe_grad)

    def visit(position, carry):
        row, col = offsets[position, 0], offsets[position, 1]
        for part in range(2):
            for layer in range(2):
                plane = pltpu.roll(wide[part, layer], 3 * tile - col, 1)[:, :n]
                window[part, layer] = pltpu.roll(plane, rows - row, 0)[:n]
        scaling[...] = jnp.zeros_like(scaling)

        def forward(mode, carry):
            probe_re, probe_im = probe[0, mode], probe[1, mode]
            top_re, top_im = window[0, 0], window[1, 0]
            moved_re, moved_im = sandwich(
                probe_re * top_re - probe_im * top_im,
                probe_re * top_im + probe_im * top_re,
                PROP,
            )
            moved[0, mode] = moved_re
            moved[1, mode] = moved_im
            low_re, low_im = window[0, 1], window[1, 1]
            far_re, far_im = sandwich(
                moved_re * low_re - moved_im * low_im,
                moved_re * low_im + moved_im * low_re,
                FOUR,
            )
            far[0, mode] = far_re
            far[1, mode] = far_im
            scaling[...] += far_re * far_re + far_im * far_im
            return carry

        lax.fori_loop(0, modes, forward, 0)
        scaling[...] = 1.0 - measured[position] / jnp.sqrt(scaling[...] + 1.0)
        grads[...] = jnp.zeros_like(grads)

        def backward(mode, carry):
            factor = scaling[...]
            back_re, back_im = sandwich(factor * far[0, mode], factor * far[1, mode], FOUR_CONJ)
            moved_re, moved_im = moved[0, mode], moved[1, mode]
            grads[0, 1] += moved_re * back_re + moved_im * back_im
            grads[1, 1] += moved_re * back_im - moved_im * back_re
            low_re, low_im = window[0, 1], window[1, 1]
            source_re, source_im = sandwich(
                low_re * back_re + low_im * back_im,
                low_re * back_im - low_im * back_re,
                PROP_CONJ,
            )
            probe_re, probe_im = probe[0, mode], probe[1, mode]
            grads[0, 0] += probe_re * source_re + probe_im * source_im
            grads[1, 0] += probe_re * source_im - probe_im * source_re
            top_re, top_im = window[0, 0], window[1, 0]
            probe_grad[0, mode] += top_re * source_re + top_im * source_im
            probe_grad[1, mode] += top_re * source_im - top_im * source_re
            return carry

        lax.fori_loop(0, modes, backward, 0)
        for part in range(2):
            for layer in range(2):
                plane = jnp.concatenate(
                    [grads[part, layer], jnp.zeros((rows - n, n), F32)], axis=0
                )
                plane = pltpu.roll(plane, row, 0)
                plane = jnp.concatenate(
                    [plane, jnp.zeros((rows, 3 * tile - n), F32)], axis=1
                )
                plane = pltpu.roll(plane, col, 1)
                for at, target in enumerate((grad_left, grad_middle, grad_right)):
                    piece = plane[:, at * tile : (at + 1) * tile]

                    @pl.when(position == 0)
                    def _():
                        target[part, layer] = piece

                    @pl.when(position != 0)
                    def _():
                        target[part, layer] += piece

        return carry

    lax.fori_loop(0, count, visit, 0)


def window_gradients(offsets, left, middle, right, probe, measured):
    n, modes = probe.shape[2], probe.shape[1]
    rows, tile = middle.shape[2], middle.shape[3]
    base = jnp.asarray(transform_tables(n))
    vmem = pl.BlockSpec(memory_space=pltpu.VMEM)
    column = jax.ShapeDtypeStruct(middle.shape, F32)
    products = 2 * measured.shape[0] * modes * 4 * 2 * 4 * 3 * n**3
    return pl.pallas_call(
        window_kernel,
        out_shape=(column, column, column, jax.ShapeDtypeStruct(probe.shape, F32)),
        in_specs=[pl.BlockSpec(memory_space=pltpu.SMEM)] + [vmem] * 6,
        out_specs=(vmem,) * 4,
        scratch_shapes=[
            pltpu.VMEM((2, 2, n, n), F32),
            pltpu.VMEM(probe.shape, F32),
            pltpu.VMEM(probe.shape, F32),
            pltpu.VMEM((n, n), F32),
            pltpu.VMEM((2, 2, n, n), F32),
            pltpu.VMEM((4, 2, 2 * n, 2 * n), BF),
            pltpu.VMEM((2, 2, rows, 3 * tile), F32),
        ],
        compiler_params=pltpu.CompilerParams(vmem_limit_bytes=32 << 20),
        cost_estimate=pl.CostEstimate(flops=products, bytes_accessed=12 << 20, transcendentals=n * n),
        name="window_gradients",
    )(offsets, left, middle, right, probe, measured, base)


def around(value, axis, steps):
    count = lax.axis_size(axis)
    return lax.ppermute(value, axis, [(at, (at + steps) % count) for at in range(count)])


def exchanged(value, axis, groups=None):
    return lax.all_to_all(value, axis, 0, 0, tiled=True, axis_index_groups=groups)


def copies(value, count):
    return jnp.broadcast_to(value[None], (count,) + value.shape)


def paired_half(value):
    tiles = lax.axis_size("tile")
    core = lax.axis_index("tile") % 2
    kept = lax.dynamic_index_in_dim(value, core, 0, False)
    sent = lax.dynamic_index_in_dim(value, 1 - core, 0, False)
    return kept + lax.ppermute(sent, "tile", [(at, at ^ 1) for at in range(tiles)])


def paired_whole(half):
    tiles = lax.axis_size("tile")
    first = lax.axis_index("tile") % 2 == 0
    other = lax.ppermute(half, "tile", [(at, at ^ 1) for at in range(tiles)])
    return jnp.stack([jnp.where(first, half, other), jnp.where(first, other, half)])


def per_device(object_field, probe_modes, offsets, measured):
    tile = object_field.shape[2]
    strips, tiles = lax.axis_size("strip"), lax.axis_size("tile")
    local = jnp.stack(
        [
            (offsets[:, 0] - lax.axis_index("strip") * tile) % (tile * strips),
            (offsets[:, 1] - lax.axis_index("tile") * tile) % (tile * tiles),
        ],
        axis=1,
    )
    diagonal = [
        (s * tiles + t, (s + 1) % strips * tiles + (t + 1) % tiles)
        for s in range(strips)
        for t in range(tiles)
    ]
    above = around(object_field, "strip", 1)
    below = around(object_field, "strip", -1)
    middle = jnp.concatenate([above, object_field, below], axis=2)
    left = around(middle, "tile", 1)
    right = around(middle, "tile", -1)
    moved_offsets = lax.ppermute(local, ("strip", "tile"), diagonal)
    moved_measured = lax.ppermute(measured, ("strip", "tile"), diagonal)
    grad_left, grad_middle, grad_right, grad_probe = window_gradients(
        moved_offsets, left, middle, right, probe_modes, moved_measured
    )
    levels = [[core + 2 * z for z in range(tiles // 2)] for core in range(2)]
    from_right = around(grad_left, "tile", -1)
    from_left = around(grad_right, "tile", 1)
    part = paired_half(grad_probe.reshape(2, strips, -1, grad_probe.shape[-1]))
    shares = exchanged(part, "strip")
    shares, from_right, from_left = lax.optimization_barrier((shares, from_right, from_left))
    column = grad_middle + from_right + from_left
    from_below = around(column[:, :, :tile], "strip", -1)
    from_above = around(column[:, :, 2 * tile :], "strip", 1)
    shares = exchanged(copies(jnp.sum(shares, axis=0), tiles // 2), "tile", levels)
    shares, from_below, from_above = lax.optimization_barrier((shares, from_below, from_above))
    object_grad = column[:, :, tile : 2 * tile] + from_below + from_above
    half = exchanged(copies(jnp.sum(shares, axis=0), strips), "strip")
    return (object_grad, paired_whole(half).reshape(grad_probe.shape))


def solution(mesh):
    in_specs = (
        P(None, None, "strip", "tile"),
        P(),
        P(("strip", "tile"), None),
        P(("strip", "tile"), None, None),
    )
    out_specs = (P(None, None, "strip", "tile"), P())
    return jax.shard_map(
        per_device, mesh=mesh, in_specs=in_specs, out_specs=out_specs, check_vma=False
    )
```

time: 574 us -> 179 us (0.31); the launches traced: 565 us -> 178 us
  waiting for transfers between devices: 312 us -> 47.2 us
  matrix products: 144 us -> 0 us
  Pallas kernels: 0 us -> 52.4 us
  local copies, waits for them, and re-layouts: 47 us -> 13.8 us
  starting transfers between devices: 19.4 us -> 37.8 us
  blocking collectives: 0 us -> 18 us
  loops' own time: 14.7 us -> 0 us
  between operations: 14.7 us -> 0.74 us
    psum x1 -> x0, waiting for transfers between devices: 228 us -> none  [per_device(): probe_grad = lax.psum(jnp.sum(grads_probe, axis=0), ('strip', 'tile'))]
    dot_general x36 -> x0, matrix products: 144 us -> none  [the longest x16 70.5 us: product_right(): jnp.einsum('...ij,jk->...ik', field, matrix, precision=lax.Precision.HIGH...]
    pallas_call x0 -> x1, Pallas kernels: none -> 52.4 us  [window_gradients(): pl.pallas_call(window_kernel, out_shape=(column, column, column, jax.Shap...]
    ppermute x8 -> x12, waiting for transfers between devices: 84.1 us -> 39.6 us  [the longest x8 23.3 us: around(): lax.ppermute(value, axis, [(at, (at + steps) % count) for at in range(cou...]
    dynamic_update_slice x4 -> x0, local copies, waits for them, and re-layouts: 37.1 us -> none  [the longest x2 31.6 us: single_add(): lax.dynamic_update_slice(running, current + grads_window[position], corner)]
    all_to_all x0 -> x1, blocking collectives: none -> 18 us  [exchanged(): lax.all_to_all(value, axis, 0, 0, tiled=True, axis_index_groups=groups)]
    another operation x2 -> x0, loops' own time: 14.7 us -> none  [the longest x1 7.86 us: per_device(): windows = lax.map(single_cut, jnp.stack([rows_local, cols_local], axis=1))]
    all_to_all x0 -> x2, starting transfers between devices: none -> 11.2 us  [exchanged(): lax.all_to_all(value, axis, 0, 0, tiled=True, axis_index_groups=groups)]
  transfers between devices with their start and end apart: 9 -> 14, of which waited for: 7 -> 9; matrix products, arithmetic and copies ran while one was open for 2% -> 2% of each run, Pallas kernels for 0% -> 0%
where the time goes in v1:
time: 179 us; the launch traced here: 178 us
  Pallas kernels  52.4 us (29%)
  waiting for transfers between devices  47.2 us (26%)
  starting transfers between devices  37.8 us (21%)
  blocking collectives  18 us (10%)
  local copies, waits for them, and re-layouts  13.8 us (8%)
  other arithmetic  8.4 us (5%)
    pallas_call x1, Pallas kernels, window_gradients(): pl.pallas_call(window_kernel, out_shape=(column, column, column, jax.Shap...  52.4 us
    ppermute x8, waiting for transfers between devices, around(): lax.ppermute(value, axis, [(at, (at + steps) % count) for at in range(cou...  23.3 us
    all_to_all x1, blocking collectives, exchanged(): lax.all_to_all(value, axis, 0, 0, tiled=True, axis_index_groups=groups)  18 us
    ppermute x8, starting transfers between devices, around(): lax.ppermute(value, axis, [(at, (at + steps) % count) for at in range(cou...  13.9 us
    ppermute x1, waiting for transfers between devices, per_device(): moved_offsets = lax.ppermute(local, ('strip', 'tile'), diagonal)  12.1 us
    unnamed x26, local copies, waits for them, and re-layouts  11.7 us
    all_to_all x2, starting transfers between devices, exchanged(): lax.all_to_all(value, axis, 0, 0, tiled=True, axis_index_groups=groups)  11.2 us
    all_to_all x2, waiting for transfers between devices, exchanged(): lax.all_to_all(value, axis, 0, 0, tiled=True, axis_index_groups=groups)  7.65 us
  transfers between devices with their start and end apart: 14, of which 9 were waited for; matrix products, arithmetic and copies ran while one was open for 2% of the time, Pallas kernels for 0%

profile of v1, /device:TPU:1, one launch (start us, length us, event | category | flops | bytes accessed | tf_op | source)
XLA Modules:
  0.0 178.3 jit_solution(15393434927037814757)
XLA Ops:
  0.6 2.2 %collective-permute-start.1 = (f32[2,2,128,128]{3,2,1,0:T(8,128)}, f32[2,2,128,128]{3,2,1,0:T(8,128)S(1)}, u32[]{:S(2)}, u32[]{:S(2)}) collective-permute-start(f32[2,2,128,128]{3,2,1,0:T(8,128)} %param.5), channel_id=1, source_target_pairs={{0,16},{16,32},{32,48},{48,64},{64,80},{80,96},{96,112},{112,128},... | collective-permute-start | bytes 786440 | tf_op jit(solution)/shard_map/ppermute | solution.py:196
  2.8 3.7 %collective-permute-start.2 = (f32[2,2,128,128]{3,2,1,0:T(8,128)}, f32[2,2,128,128]{3,2,1,0:T(8,128)S(1)}, u32[]{:S(2)}, u32[]{:S(2)}) collective-permute-start(f32[2,2,128,128]{3,2,1,0:T(8,128)} %param.5), channel_id=1, source_target_pairs={{0,240},{16,0},{32,16},{48,32},{64,48},{80,64},{96,80},{112,96},{1... | collective-permute-start | bytes 786440 | tf_op jit(solution)/shard_map/ppermute | solution.py:196
  6.6 4.2 %collective-permute-done.1 = f32[2,2,128,128]{3,2,1,0:T(8,128)S(1)} collective-permute-done((f32[2,2,128,128]{3,2,1,0:T(8,128)}, f32[2,2,128,128]{3,2,1,0:T(8,128)S(1)}, u32[]{:S(2)}, u32[]{:S(2)}) %collective-permute-start.1) | collective-permute-done | bytes 262176 | tf_op jit(solution)/shard_map/ppermute | solution.py:196
  11.8 4.7 %collective-permute-start.3 = (f32[2,2,384,128]{3,2,1,0:T(8,128)S(1)}, f32[2,2,384,128]{3,2,1,0:T(8,128)S(1)}, u32[]{:S(2)}, u32[]{:S(2)}) collective-permute-start(f32[2,2,384,128]{3,2,1,0:T(8,128)S(1)} %constant_dynamic-update-slice_fusion.middle), channel_id=1, source_target_pairs={{0,1},{1,2},{2,3},{3,4},{4,5},{5,6},{6,7},{7,8},{8,9},{9,10},{10,1... | collective-permute-start | bytes 2359304 | tf_op jit(solution)/shard_map/ppermute | solution.py:196
  19.1 12.1 %collective-permute-done.offsets = s32[2,2]{1,0:T(2,128)S(1)} collective-permute-done((s32[2,2]{1,0:T(2,128)S(1)}, s32[2,2]{1,0:T(2,128)S(1)}, u32[]{:S(2)}, u32[]{:S(2)}) %collective-permute-start) | collective-permute-done | bytes 48 | tf_op jit(solution)/shard_map/ppermute | solution.py:242
  34.1 1.6 copy-done.2
  39.2 52.4 %window_gradients.1 = (f32[2,2,384,128]{3,2,1,0:T(8,128)S(1)}, f32[2,2,384,128]{3,2,1,0:T(8,128)S(1)}, f32[2,2,384,128]{3,2,1,0:T(8,128)S(1)}, f32[2,4,256,256]{3,2,1,0:T(8,128)S(1)}) custom-call(s32[2,2]{1,0:T(2,128)S(1)} %collective-permute-done.offsets, f32[2,2,384,128]{3,2,1,0:T(8,128)S(1)} %copy-done.4, f32[2,2,384,128]{3,2,1,0:T(8,128)S(1)} %copy-done.1, ...), custom_call_target="tpu_custom_call" | custom-call | flops 25769803776 | bytes 12582912 | tf_op jit(solution)/shard_map/window_gradients/pallas_call | solution.py:174
  94.5 7.1 %collective-permute-start.6 = (f32[16,64,256]{2,1,0:T(8,128)}, f32[16,64,256]{2,1,0:T(8,128)}, u32[]{:S(2)}, u32[]{:S(2)}) collective-permute-start(f32[16,64,256]{2,1,0:T(8,128)} %dynamic-slice_bitcast_fusion), channel_id=1, source_target_pairs={{0,1},{1,0},{2,3},{3,2},{4,5},{5,4},{6,7},{7,6},{8,9},{9,8},{10,11... | collective-permute-start | bytes 3145736 | tf_op jit(solution)/shard_map/ppermute | solution.py:212
  101.6 2.6 %collective-permute-done.6 = f32[16,64,256]{2,1,0:T(8,128)} collective-permute-done((f32[16,64,256]{2,1,0:T(8,128)}, f32[16,64,256]{2,1,0:T(8,128)}, u32[]{:S(2)}, u32[]{:S(2)}) %collective-permute-start.6) | collective-permute-done | bytes 1048608 | tf_op jit(solution)/shard_map/ppermute | solution.py:212
  104.2 2.3 %bitcast_add_fusion = f32[16,64,256]{2,1,0:T(8,128)} fusion(f32[16,64,256]{2,1,0:T(8,128)} %collective-permute-done.6, f32[2,16,64,256]{3,2,1,0:T(8,128)S(1)} %bitcast.8, s32[]{:T(128)S(6)} %select_n.43), kind=kLoop, calls=%fused_computation.1 | loop fusion | flops 262144 | bytes 3145732 | tf_op jit(solution)/shard_map/add | solution.py:212
  106.5 4.5 %all-to-all-start = ((f32[16,64,256]{2,1,0:T(8,128)}), f32[16,64,256]{2,1,0:T(8,128)}, u32[]{:S(2)}, u32[]{:S(2)}) async-start(f32[16,64,256]{2,1,0:T(8,128)} %bitcast_add_fusion), calls=%async_computation | async-start | bytes 2097152 | tf_op jit(solution)/shard_map/all_to_all | solution.py:200
  111.4 1.4 collective-permute-start.8
  112.8 10.1 %collective-permute-done.7 = f32[2,2,384,128]{3,2,1,0:T(8,128)} collective-permute-done((f32[2,2,384,128]{3,2,1,0:T(8,128)S(1)}, f32[2,2,384,128]{3,2,1,0:T(8,128)}, u32[]{:S(2)}, u32[]{:S(2)}) %collective-permute-start.7) | collective-permute-done | bytes 786464 | tf_op jit(solution)/shard_map/ppermute | solution.py:196
  122.9 4.7 %all-to-all-done = f32[16,64,256]{2,1,0:T(8,128)} async-done(((f32[16,64,256]{2,1,0:T(8,128)}), f32[16,64,256]{2,1,0:T(8,128)}, u32[]{:S(2)}, u32[]{:S(2)}) %all-to-all-start) | async-done | bytes 1048608 | tf_op jit(solution)/shard_map/all_to_all | solution.py:200
  129.7 6.8 %all-to-all-start.1 = ((f32[8,64,256]{2,1,0:T(8,128)}), f32[8,64,256]{2,1,0:T(8,128)S(1)}, u32[]{:S(2)}, u32[]{:S(2)}) async-start(f32[8,64,256]{2,1,0:T(8,128)} %broadcast_in_dim.4), calls=%async_computation.1 | async-start | bytes 1048576 | tf_op jit(solution)/shard_map/all_to_all | solution.py:200
  136.5 1.5 add_add_fusion
  138.0 1.4 collective-permute-start.9
  139.6 4.1 %collective-permute-done.9 = f32[2,2,128,128]{3,2,1,0:T(8,128)S(1)} collective-permute-done((f32[2,2,128,128]{3,2,1,0:T(8,128)S(1)}, f32[2,2,128,128]{3,2,1,0:T(8,128)S(1)}, u32[]{:S(2)}, u32[]{:S(2)}) %collective-permute-start.9) | collective-permute-done | bytes 262176 | tf_op jit(solution)/shard_map/ppermute | solution.py:196
  143.6 5.0 %collective-permute-done.10 = f32[2,2,128,128]{3,2,1,0:T(8,128)S(1)} collective-permute-done((f32[2,2,128,128]{3,2,1,0:T(8,128)S(1)}, f32[2,2,128,128]{3,2,1,0:T(8,128)S(1)}, u32[]{:S(2)}, u32[]{:S(2)}) %collective-permute-start.10) | collective-permute-done | bytes 262176 | tf_op jit(solution)/shard_map/ppermute | solution.py:196
  148.6 2.9 %all-to-all-done.1 = f32[8,64,256]{2,1,0:T(8,128)S(1)} async-done(((f32[8,64,256]{2,1,0:T(8,128)}), f32[8,64,256]{2,1,0:T(8,128)S(1)}, u32[]{:S(2)}, u32[]{:S(2)}) %all-to-all-start.1) | async-done | bytes 524320 | tf_op jit(solution)/shard_map/all_to_all | solution.py:200
  151.7 18.0 %all_to_all.15 = f32[16,64,256]{2,1,0:T(8,128)S(1)} all-to-all(f32[16,64,256]{2,1,0:T(8,128)S(1)} %broadcast_in_dim.5), channel_id=1, replica_groups=mesh['strip'=16,'tile'=16] {'strip'}, dimensions={0} | all-to-all | bytes 2097152 | tf_op jit(solution)/shard_map/all_to_all | solution.py:200
  169.7 4.7 %collective-permute-start.11 = (f32[16,64,256]{2,1,0:T(8,128)S(1)}, f32[16,64,256]{2,1,0:T(8,128)S(1)}, u32[]{:S(2)}, u32[]{:S(2)}) collective-permute-start(f32[16,64,256]{2,1,0:T(8,128)S(1)} %all_to_all.15), channel_id=1, source_target_pairs={{0,1},{1,0},{2,3},{3,2},{4,5},{5,4},{6,7},{7,6},{8,9},{9,8},{10,11... | collective-permute-start | bytes 3145736 | tf_op jit(solution)/shard_map/ppermute | solution.py:218
  175.2 1.5 collective-permute-done.11
  176.9 1.5 pad_maximum_fusion
  (46 shorter events, 16.6 us)
Async XLA Ops:
  0.6 10.1 %collective-permute-start.1 = (f32[2,2,128,128]{3,2,1,0:T(8,128)}, f32[2,2,128,128]{3,2,1,0:T(8,128)S(1)}, u32[]{:S(2)}, u32[]{:S(2)}) collective-permute-start(f32[2,2,128,128]{3,2,1,0:T(8,128)} %param.5), channel_id=1, source_target_pairs={{0,16},{16,32},{32,48},{48,64},{64,80},{80,96},{96,112},{112,128},... | collective-permute-start | bytes 786440 | tf_op jit(solution)/shard_map/ppermute | solution.py:196
  2.8 8.9 %collective-permute-start.2 = (f32[2,2,128,128]{3,2,1,0:T(8,128)}, f32[2,2,128,128]{3,2,1,0:T(8,128)S(1)}, u32[]{:S(2)}, u32[]{:S(2)}) collective-permute-start(f32[2,2,128,128]{3,2,1,0:T(8,128)} %param.5), channel_id=1, source_target_pairs={{0,240},{16,0},{32,16},{48,32},{64,48},{80,64},{96,80},{112,96},{1... | collective-permute-start | bytes 786440 | tf_op jit(solution)/shard_map/ppermute | solution.py:196
  11.8 19.4 %collective-permute-start.3 = (f32[2,2,384,128]{3,2,1,0:T(8,128)S(1)}, f32[2,2,384,128]{3,2,1,0:T(8,128)S(1)}, u32[]{:S(2)}, u32[]{:S(2)}) collective-permute-start(f32[2,2,384,128]{3,2,1,0:T(8,128)S(1)} %constant_dynamic-update-slice_fusion.middle), channel_id=1, source_target_pairs={{0,1},{1,2},{2,3},{3,4},{4,5},{5,6},{6,7},{7,8},{8,9},{9,10},{10,1... | collective-permute-start | bytes 2359304 | tf_op jit(solution)/shard_map/ppermute | solution.py:196
  16.5 15.5 %collective-permute-start.4 = (f32[2,2,384,128]{3,2,1,0:T(8,128)S(1)}, f32[2,2,384,128]{3,2,1,0:T(8,128)S(1)}, u32[]{:S(2)}, u32[]{:S(2)}) collective-permute-start(f32[2,2,384,128]{3,2,1,0:T(8,128)S(1)} %constant_dynamic-update-slice_fusion.middle), channel_id=1, source_target_pairs={{0,15},{1,0},{2,1},{3,2},{4,3},{5,4},{6,5},{7,6},{8,7},{9,8},{10,9... | collective-permute-start | bytes 2359304 | tf_op jit(solution)/shard_map/ppermute | solution.py:196
  16.5 0.9 copy-start
  17.4 13.8 %collective-permute-start.5 = (f32[2,256,256]{2,1,0:T(8,128)}, f32[2,256,256]{2,1,0:T(8,128)S(1)}, u32[]{:S(2)}, u32[]{:S(2)}) collective-permute-start(f32[2,256,256]{2,1,0:T(8,128)} %param.8), channel_id=1, source_target_pairs={{0,17},{1,18},{2,19},{3,20},{4,21},{5,22},{6,23},{7,24},{8,25},{9,... | collective-permute-start | bytes 1572872 | tf_op jit(solution)/shard_map/ppermute | solution.py:243
  18.3 12.9 %collective-permute-start = (s32[2,2]{1,0:T(2,128)S(1)}, s32[2,2]{1,0:T(2,128)S(1)}, u32[]{:S(2)}, u32[]{:S(2)}) collective-permute-start(s32[2,2]{1,0:T(2,128)S(1)} %pad_add_fusion), channel_id=1, source_target_pairs={{0,17},{1,18},{2,19},{3,20},{4,21},{5,22},{6,23},{7,24},{8,25},{9,... | collective-permute-start | bytes 56 | tf_op jit(solution)/shard_map/ppermute | solution.py:242
  32.1 0.9 copy-start.5
  33.0 1.1 copy-start.1
  34.1 1.6 copy-start.2
  35.7 1.1 copy-start.4
  36.9 1.1 copy-start.6
  38.0 1.2 copy-start.11
  91.6 0.9 copy-start.7
  94.5 9.7 %collective-permute-start.6 = (f32[16,64,256]{2,1,0:T(8,128)}, f32[16,64,256]{2,1,0:T(8,128)}, u32[]{:S(2)}, u32[]{:S(2)}) collective-permute-start(f32[16,64,256]{2,1,0:T(8,128)} %dynamic-slice_bitcast_fusion), channel_id=1, source_target_pairs={{0,1},{1,0},{2,3},{3,2},{4,5},{5,4},{6,7},{7,6},{8,9},{9,8},{10,11... | collective-permute-start | bytes 3145736 | tf_op jit(solution)/shard_map/ppermute | solution.py:212
  106.5 4.5 %copy-start.10 = (f32[2,2,384,128]{3,2,1,0:T(8,128)S(1)}, f32[2,2,384,128]{3,2,1,0:T(8,128)}, u32[]{:S(2)}) copy-start(f32[2,2,384,128]{3,2,1,0:T(8,128)} %copy-done.9) | copy-start | bytes 2359300
  106.5 4.9 %copy-start.8 = (f32[2,2,384,128]{3,2,1,0:T(8,128)S(1)}, f32[2,2,384,128]{3,2,1,0:T(8,128)}, u32[]{:S(2)}) copy-start(f32[2,2,384,128]{3,2,1,0:T(8,128)} %copy-done.7) | copy-start | bytes 2359300
  106.5 21.1 %all-to-all-start = ((f32[16,64,256]{2,1,0:T(8,128)}), f32[16,64,256]{2,1,0:T(8,128)}, u32[]{:S(2)}, u32[]{:S(2)}) async-start(f32[16,64,256]{2,1,0:T(8,128)} %bitcast_add_fusion), calls=%async_computation | async-start | bytes 2097152 | tf_op jit(solution)/shard_map/all_to_all | solution.py:200
  111.0 11.8 %collective-permute-start.7 = (f32[2,2,384,128]{3,2,1,0:T(8,128)S(1)}, f32[2,2,384,128]{3,2,1,0:T(8,128)}, u32[]{:S(2)}, u32[]{:S(2)}) collective-permute-start(f32[2,2,384,128]{3,2,1,0:T(8,128)S(1)} %copy-done.10), channel_id=1, source_target_pairs={{0,15},{1,0},{2,1},{3,2},{4,3},{5,4},{6,5},{7,6},{8,7},{9,8},{10,9... | collective-permute-start | bytes 2359304 | tf_op jit(solution)/shard_map/ppermute | solution.py:196
  111.4 11.4 %collective-permute-start.8 = (f32[2,2,384,128]{3,2,1,0:T(8,128)S(1)}, f32[2,2,384,128]{3,2,1,0:T(8,128)}, u32[]{:S(2)}, u32[]{:S(2)}) collective-permute-start(f32[2,2,384,128]{3,2,1,0:T(8,128)S(1)} %copy-done.8), channel_id=1, source_target_pairs={{0,1},{1,2},{2,3},{3,4},{4,5},{5,6},{6,7},{7,8},{8,9},{9,10},{10,1... | collective-permute-start | bytes 2359304 | tf_op jit(solution)/shard_map/ppermute | solution.py:196
  129.7 21.8 %all-to-all-start.1 = ((f32[8,64,256]{2,1,0:T(8,128)}), f32[8,64,256]{2,1,0:T(8,128)S(1)}, u32[]{:S(2)}, u32[]{:S(2)}) async-start(f32[8,64,256]{2,1,0:T(8,128)} %broadcast_in_dim.4), calls=%async_computation.1 | async-start | bytes 1048576 | tf_op jit(solution)/shard_map/all_to_all | solution.py:200
  138.0 5.6 %collective-permute-start.9 = (f32[2,2,128,128]{3,2,1,0:T(8,128)S(1)}, f32[2,2,128,128]{3,2,1,0:T(8,128)S(1)}, u32[]{:S(2)}, u32[]{:S(2)}) collective-permute-start(f32[2,2,128,128]{3,2,1,0:T(8,128)S(1)} %get-tuple-element.25), channel_id=1, source_target_pairs={{0,240},{16,0},{32,16},{48,32},{64,48},{80,64},{96,80},{112,96},{1... | collective-permute-start | bytes 786440 | tf_op jit(solution)/shard_map/ppermute | solution.py:196
  139.4 9.2 %collective-permute-start.10 = (f32[2,2,128,128]{3,2,1,0:T(8,128)S(1)}, f32[2,2,128,128]{3,2,1,0:T(8,128)S(1)}, u32[]{:S(2)}, u32[]{:S(2)}) collective-permute-start(f32[2,2,128,128]{3,2,1,0:T(8,128)S(1)} %get-tuple-element.24), channel_id=1, source_target_pairs={{0,16},{16,32},{32,48},{48,64},{64,80},{80,96},{96,112},{112,128},... | collective-permute-start | bytes 786440 | tf_op jit(solution)/shard_map/ppermute | solution.py:196
  169.7 7.0 %collective-permute-start.11 = (f32[16,64,256]{2,1,0:T(8,128)S(1)}, f32[16,64,256]{2,1,0:T(8,128)S(1)}, u32[]{:S(2)}, u32[]{:S(2)}) collective-permute-start(f32[16,64,256]{2,1,0:T(8,128)S(1)} %all_to_all.15), channel_id=1, source_target_pairs={{0,1},{1,0},{2,3},{3,2},{4,5},{5,4},{6,7},{7,6},{8,9},{9,8},{10,11... | collective-permute-start | bytes 3145736 | tf_op jit(solution)/shard_map/ppermute | solution.py:218
  (2 other events, 1.8 us)

commit v2 on v1

v2 whole, which is shorter than its diff:
```python
import jax
import jax.numpy as jnp
import ml_dtypes
import numpy as np
from jax import lax
from jax.experimental import pallas as pl
from jax.experimental.pallas import tpu as pltpu
from jax.sharding import PartitionSpec as P

FRESNEL = 0.5
BF, F32 = jnp.bfloat16, jnp.float32
FOUR, FOUR_CONJ, PROP, PROP_CONJ = 0, 1, 2, 3
VMEM = pl.BlockSpec(memory_space=pltpu.VMEM)
SMEM = pl.BlockSpec(memory_space=pltpu.SMEM)
ANY = pl.BlockSpec(memory_space=pl.ANY)
HBM = pl.BlockSpec(memory_space=pltpu.HBM)


def parity_tables(length):
    half = length // 2
    counter = np.arange(length)
    angles = (counter[:, None] * counter[None, :] % length) * (2 * np.pi / length)
    four = np.exp(-1j * angles) / np.sqrt(length)
    mirrored = np.concatenate([counter[:half], counter[:half - 1:-1]])
    quarter = counter - (length - 1) / 2
    shifted = np.exp(-2j * np.pi * quarter[:, None] * quarter[None, :] / length) / np.sqrt(length)
    centred = (counter + half) % length - half
    kern = np.exp(-1j * np.pi * FRESNEL * centred * centred / length)
    prop = (np.conj(four) * kern[None, :]) @ four
    blocks = []
    for matrix in (shifted, prop):
        folded = matrix[mirrored][:, mirrored]
        same, cross = folded[:half, :half], folded[:half, half:]
        even, odd = (same + cross) / 2, (same - cross) / 2
        for part in ("real", "imag"):
            for block in (even, odd):
                value = getattr(block, part)
                high = value.astype(np.float32).astype(ml_dtypes.bfloat16)
                low = (value - high.astype(np.float64)).astype(np.float32)
                blocks += [high, low.astype(ml_dtypes.bfloat16)]
    turn = np.exp(-2j * np.pi * ((length - 1) / 2) * counter / length)[mirrored]
    phase = turn[:, None] * turn[None, :]
    phase = np.stack([phase.real, phase.imag]).astype(np.float32)
    return np.stack(blocks).reshape(2, 2, 2, 2, half, half), phase


def halves(value):
    high = value.astype(BF)
    return high, (value - high.astype(F32)).astype(BF)


def product(a_high, a_low, b_high, b_low):
    total = jnp.dot(a_high, b_high, preferred_element_type=F32)
    total = total + jnp.dot(a_low, b_high, preferred_element_type=F32)
    return total + jnp.dot(a_high, b_low, preferred_element_type=F32)


def anti_diagonal(h):
    row_at = lax.broadcasted_iota(jnp.int32, (h, h), 0)
    col_at = lax.broadcasted_iota(jnp.int32, (h, h), 1)
    return (row_at + col_at == h - 1).astype(F32).astype(BF)


def folded(planes):
    n = planes[0].shape[0]
    h = n // 2
    anti = anti_diagonal(h)
    flipped = jnp.dot(
        jnp.concatenate([jnp.concatenate(halves(plane[:, h:]), axis=1) for plane in planes], axis=0),
        jnp.concatenate([anti, anti], axis=0),
        preferred_element_type=F32,
    )
    planes = [
        jnp.concatenate([plane[:, :h], flipped[at * n : (at + 1) * n]], axis=1)
        for at, plane in enumerate(planes)
    ]
    flipped = jnp.dot(
        jnp.concatenate([anti, anti], axis=1),
        jnp.concatenate([jnp.concatenate(halves(plane[h:]), axis=0) for plane in planes], axis=1),
        preferred_element_type=F32,
    )
    return [
        jnp.concatenate([plane[:h], flipped[:, at * n : (at + 1) * n]], axis=0)
        for at, plane in enumerate(planes)
    ]


def sandwich(fields, which, tables, lhs_high, lhs_low, rhs_high, rhs_low):
    n = tables.shape[-1]
    h = n // 2
    for at, field in enumerate(fields):
        for part in range(2):
            first, second = field[part][:, :h], field[part][:, h:]
            for parity, value in enumerate((first + second, first - second)):
                high, low = halves(value)
                lhs_high[parity, at * n : (at + 1) * n, part * h : (part + 1) * h] = high
                lhs_low[parity, at * n : (at + 1) * n, part * h : (part + 1) * h] = low
    for parity in range(2):
        inner = product(
            lhs_high[parity], lhs_low[parity], tables[which, parity, 0], tables[which, parity, 1]
        )
        for at in range(len(fields)):
            first = inner[at * n : at * n + h]
            second = inner[at * n + h : (at + 1) * n]
            cols = slice(at * n + parity * h, at * n + (parity + 1) * h)
            for turned, value in enumerate((first + second, first - second)):
                high, low = halves(value)
                rhs_high[turned, :h, cols] = high[:, :h]
                rhs_high[turned, h:, cols] = high[:, h:]
                rhs_low[turned, :h, cols] = low[:, :h]
                rhs_low[turned, h:, cols] = low[:, h:]
    even, odd = [
        product(
            tables[which ^ 1, turned, 0], tables[which ^ 1, turned, 1],
            rhs_high[turned], rhs_low[turned],
        )
        for turned in range(2)
    ]
    results = []
    for at in range(len(fields)):
        pair = []
        for part in range(2):
            e = even[part * h : (part + 1) * h, at * n : (at + 1) * n]
            o = odd[part * h : (part + 1) * h, at * n : (at + 1) * n]
            value = jnp.concatenate([e + o, e - o], axis=0)
            first, second = value[:, :h], value[:, h:]
            pair.append(jnp.concatenate([first + second, first - second], axis=1))
        results.append(pair)
    return results


def sandwich_scratch(n, modes):
    return [
        pltpu.VMEM((2, modes * n, n), BF),
        pltpu.VMEM((2, modes * n, n), BF),
        pltpu.VMEM((2, n, modes * n), BF),
        pltpu.VMEM((2, n, modes * n), BF),
    ]


def prepare_kernel(probe_in, measured_in, blocks, probe, measured, tables):
    h = blocks.shape[-1]
    for field in range(2):
        for parity in range(2):
            for part in range(2):
                re, im = blocks[field, 0, parity, part], blocks[field, 1, parity, part]
                for conj in range(2):
                    which = 2 * field + conj
                    upper, lower = (im, -im) if conj == 0 else (-im, im)
                    tables[which, parity, part, :h, :h] = re
                    tables[which, parity, part, h:, h:] = re
                    tables[which, parity, part, :h, h:] = upper
                    tables[which, parity, part, h:, :h] = lower

    def fold(part, carry):
        planes = folded([probe_in[part, mode] for mode in range(probe.shape[1])])
        for mode, plane in enumerate(planes):
            probe[part, mode] = plane
        return carry

    lax.fori_loop(0, 2, fold, 0)
    for at, plane in enumerate(folded([measured_in[at] for at in range(measured.shape[0])])):
        measured[at] = plane


def prepared(probe, measured, blocks):
    n = probe.shape[-1]
    return pl.pallas_call(
        prepare_kernel,
        out_shape=(
            jax.ShapeDtypeStruct(probe.shape, F32),
            jax.ShapeDtypeStruct(measured.shape, F32),
            jax.ShapeDtypeStruct((4, 2, 2, n, n), BF),
        ),
        in_specs=[VMEM] * 3,
        out_specs=(VMEM,) * 3,
        compiler_params=pltpu.CompilerParams(vmem_limit_bytes=24 << 20),
        cost_estimate=pl.CostEstimate(flops=3 << 30, bytes_accessed=6 << 20, transcendentals=0),
        name="prepare",
    )(probe, measured, blocks)


def forward_kernel(
    offsets, left, middle, right, probe, tables, phase,
    window, moved, far, intensity,
    lhs_high, lhs_low, rhs_high, rhs_low, wide, sems,
):
    n, modes = probe.shape[-1], probe.shape[1]
    rows, tile = wide.shape[2], wide.shape[3] // 3
    columns = [
        pltpu.make_async_copy(source, wide.at[:, :, :, at * tile : (at + 1) * tile], sems.at[at])
        for at, source in enumerate((left, middle, right))
    ]
    for column in columns:
        column.start()
    for column in columns:
        column.wait()
    buffers = (tables, lhs_high, lhs_low, rhs_high, rhs_low)

    def visit(position, carry):
        row, col = offsets[position, 0], offsets[position, 1]
        planes = []
        for layer in range(2):
            for part in range(2):
                plane = pltpu.roll(wide[part, layer], 3 * tile - col, 1)[:, :n]
                planes.append(pltpu.roll(plane, rows - row, 0)[:n])
        planes = folded(planes)
        window[position, 0, 0], window[position, 1, 0] = planes[0], planes[1]
        window[position, 0, 1] = planes[2] * phase[0] - planes[3] * phase[1]
        window[position, 1, 1] = planes[2] * phase[1] + planes[3] * phase[0]
        top_re, top_im = window[position, 0, 0], window[position, 1, 0]
        fields = []
        for mode in range(modes):
            probe_re, probe_im = probe[0, mode], probe[1, mode]
            fields.append(
                (probe_re * top_re - probe_im * top_im, probe_re * top_im + probe_im * top_re)
            )
        fields = sandwich(fields, PROP, *buffers)
        low_re, low_im = window[position, 0, 1], window[position, 1, 1]
        exits = []
        for mode, (re, im) in enumerate(fields):
            moved[position, 0, mode] = re
            moved[position, 1, mode] = im
            exits.append((re * low_re - im * low_im, re * low_im + im * low_re))
        fields = sandwich(exits, FOUR, *buffers)
        total = jnp.zeros((n, n), F32)
        for mode, (re, im) in enumerate(fields):
            far[position, 0, mode] = re
            far[position, 1, mode] = im
            total = total + (re * re + im * im)
        intensity[position] = total
        return carry

    lax.fori_loop(0, window.shape[0], visit, 0)


def forward(count, offsets, left, middle, right, probe, tables, phase):
    n, modes = probe.shape[-1], probe.shape[1]
    rows, tile = middle.shape[2], middle.shape[3]
    fields = jax.ShapeDtypeStruct((count,) + probe.shape, F32)
    return pl.pallas_call(
        forward_kernel,
        out_shape=(
            jax.ShapeDtypeStruct((count, 2, 2, n, n), F32),
            fields,
            fields,
            jax.ShapeDtypeStruct((count, n, n), F32),
        ),
        in_specs=[SMEM] + [ANY] * 3 + [VMEM] * 3,
        out_specs=(VMEM,) * 4,
        scratch_shapes=sandwich_scratch(n, modes)
        + [pltpu.VMEM((2, 2, rows, 3 * tile), F32), pltpu.SemaphoreType.DMA((3,))],
        compiler_params=pltpu.CompilerParams(vmem_limit_bytes=SCOPED_F << 20),
        cost_estimate=pl.CostEstimate(
            flops=count * modes * 8 * 12 * n**3, bytes_accessed=18 << 20, transcendentals=0
        ),
        name="forward",
    )(offsets, left, middle, right, probe, tables, phase)


def backward_kernel(
    scalars, window, moved, far, intensity, measured, probe, tables, phase,
    grad_left, grad_middle, grad_right, kept, sent,
    lhs_high, lhs_low, rhs_high, rhs_low, wide, probe_grad, sems,
):
    n, modes = probe.shape[-1], probe.shape[1]
    rows, tile = wide.shape[2], wide.shape[3] // 3
    count = window.shape[0]
    buffers = (tables, lhs_high, lhs_low, rhs_high, rhs_low)

    def visit(position, carry):
        scaling = 1.0 - measured[position] / jnp.sqrt(intensity[position] + 1.0)
        fields = [
            (scaling * far[position, 0, mode], scaling * far[position, 1, mode])
            for mode in range(modes)
        ]
        fields = sandwich(fields, FOUR_CONJ, *buffers)
        low_re, low_im = window[position, 0, 1], window[position, 1, 1]
        total_re = total_im = jnp.zeros((n, n), F32)
        behinds = []
        for mode, (re, im) in enumerate(fields):
            moved_re, moved_im = moved[position, 0, mode], moved[position, 1, mode]
            total_re = total_re + (moved_re * re + moved_im * im)
            total_im = total_im + (moved_re * im - moved_im * re)
            behinds.append((low_re * re + low_im * im, low_re * im - low_im * re))
        grad_low = (
            total_re * phase[0] + total_im * phase[1],
            total_im * phase[0] - total_re * phase[1],
        )
        fields = sandwich(behinds, PROP_CONJ, *buffers)
        top_re, top_im = window[position, 0, 0], window[position, 1, 0]
        total_re = total_im = jnp.zeros((n, n), F32)
        for mode, (re, im) in enumerate(fields):
            probe_re, probe_im = probe[0, mode], probe[1, mode]
            total_re = total_re + (probe_re * re + probe_im * im)
            total_im = total_im + (probe_re * im - probe_im * re)
            term_re = top_re * re + top_im * im
            term_im = top_re * im - top_im * re

            @pl.when(position == 0)
            def _():
                probe_grad[0, mode] = term_re
                probe_grad[1, mode] = term_im

            @pl.when(position != 0)
            def _():
                probe_grad[0, mode] += term_re
                probe_grad[1, mode] += term_im

        planes = folded([total_re, total_im, *grad_low])
        row, col = scalars[position, 0], scalars[position, 1]
        for layer in range(2):
            for part in range(2):
                plane = jnp.concatenate(
                    [planes[2 * layer + part], jnp.zeros((rows - n, n), F32)], axis=0
                )
                plane = pltpu.roll(plane, row, 0)
                plane = jnp.concatenate([plane, jnp.zeros((rows, 3 * tile - n), F32)], axis=1)
                plane = pltpu.roll(plane, col, 1)

                @pl.when(position == 0)
                def _():
                    wide[part, layer] = plane

                @pl.when(position != 0)
                def _():
                    wide[part, layer] += plane

        return carry

    lax.fori_loop(0, count, visit, 0)
    copies = [
        pltpu.make_async_copy(wide.at[:, :, :, at * tile : (at + 1) * tile], target, sems.at[at])
        for at, target in enumerate((grad_left, grad_middle, grad_right))
    ]
    for copy in copies:
        copy.start()

    def unfold(part, carry):
        planes = folded([probe_grad[part, mode] for mode in range(modes)])
        for mode in range(modes):
            probe_grad[part, mode] = planes[mode]
        return carry

    lax.fori_loop(0, 2, unfold, 0)
    core = scalars[count, 0]
    parts = [
        pltpu.make_async_copy(probe_grad.at[core], kept, sems.at[3]),
        pltpu.make_async_copy(probe_grad.at[1 - core], sent, sems.at[4]),
    ]
    for part in parts:
        part.start()
    for copy in copies + parts:
        copy.wait()


def backward(scalars, state, measured, probe, tables, phase, rows, tile):
    n, modes = probe.shape[-1], probe.shape[1]
    count = measured.shape[0]
    column = jax.ShapeDtypeStruct((2, 2, rows, tile), F32)
    half = jax.ShapeDtypeStruct(probe.shape[1:], F32)
    return pl.pallas_call(
        backward_kernel,
        out_shape=(column, column, column, half, half),
        in_specs=[SMEM] + [VMEM] * 8,
        out_specs=(HBM,) * 5,
        scratch_shapes=sandwich_scratch(n, modes)
        + [
            pltpu.VMEM((2, 2, rows, 3 * tile), F32),
            pltpu.VMEM(probe.shape, F32),
            pltpu.SemaphoreType.DMA((5,)),
        ],
        compiler_params=pltpu.CompilerParams(vmem_limit_bytes=SCOPED_B << 20),
        cost_estimate=pl.CostEstimate(
            flops=count * modes * 8 * 12 * n**3, bytes_accessed=18 << 20, transcendentals=count * n * n
        ),
        name="backward",
    )(scalars, *state, measured, probe, tables, phase)


SCOPED_F, SCOPED_B = 20, 20


def around(value, axis, steps):
    count = lax.axis_size(axis)
    return lax.ppermute(value, axis, [(at, (at + steps) % count) for at in range(count)])


def exchanged(value, axis, groups=None):
    return lax.all_to_all(value, axis, 0, 0, tiled=True, axis_index_groups=groups)


def copies(value, count):
    return jnp.broadcast_to(value[None], (count,) + value.shape)


def swapped(value):
    return lax.ppermute(value, "tile", [(at, at ^ 1) for at in range(lax.axis_size("tile"))])


def per_device(object_field, probe_modes, offsets, measured):
    n = probe_modes.shape[-1]
    tile = object_field.shape[2]
    strips, tiles = lax.axis_size("strip"), lax.axis_size("tile")
    blocks, phase = parity_tables(n)
    phase = jnp.asarray(phase)
    diagonal = [
        (s * tiles + t, (s + 1) % strips * tiles + (t + 1) % tiles)
        for s in range(strips)
        for t in range(tiles)
    ]
    corner = jnp.stack([lax.axis_index("strip"), lax.axis_index("tile")]).astype(jnp.int32) * tile
    wrap = jnp.array([strips * tile, tiles * tile], jnp.int32)
    core_there = 1 - lax.axis_index("tile") % 2
    scalars = jnp.concatenate(
        [(offsets - corner) % wrap, jnp.full((1, 2), core_there, jnp.int32)], axis=0
    )
    above = around(object_field, "strip", 1)
    below = around(object_field, "strip", -1)
    scalars = lax.ppermute(scalars, ("strip", "tile"), diagonal)
    probe, measured, tables = prepared(probe_modes, measured, jnp.asarray(blocks))
    middle = jnp.concatenate([above, object_field, below], axis=2)
    left = around(middle, "tile", 1)
    right = around(middle, "tile", -1)
    left, right, measured = lax.optimization_barrier((left, right, measured))
    measured = lax.ppermute(measured, ("strip", "tile"), diagonal)
    state = forward(measured.shape[0], scalars, left, middle, right, probe, tables, phase)
    grad_left, grad_middle, grad_right, kept, sent = backward(
        scalars, state, measured, probe, tables, phase, 3 * tile, tile
    )

    from_right = around(grad_left, "tile", -1)
    from_left = around(grad_right, "tile", 1)
    part = (kept + swapped(sent)).reshape(strips, -1, n)
    shares = exchanged(part, "strip")
    shares, from_right, from_left = lax.optimization_barrier((shares, from_right, from_left))
    column = grad_middle + from_right + from_left
    levels = [[core + 2 * z for z in range(tiles // 2)] for core in range(2)]
    share = jnp.sum(exchanged(copies(jnp.sum(shares, axis=0), tiles // 2), "tile", levels), axis=0)
    from_below = around(column[:, :, :tile], "strip", -1)
    from_above = around(column[:, :, 2 * tile :], "strip", 1)
    half = exchanged(copies(share, strips), "strip")
    half, from_below, from_above = lax.optimization_barrier((half, from_below, from_above))
    object_grad = column[:, :, tile : 2 * tile] + from_below + from_above
    other = swapped(half)
    first = lax.axis_index("tile") % 2 == 0
    whole = jnp.stack([jnp.where(first, half, other), jnp.where(first, other, half)])
    return (object_grad, whole.reshape(probe_modes.shape))


def solution(mesh):
    in_specs = (
        P(None, None, "strip", "tile"),
        P(),
        P(("strip", "tile"), None),
        P(("strip", "tile"), None, None),
    )
    out_specs = (P(None, None, "strip", "tile"), P())
    return jax.shard_map(
        per_device, mesh=mesh, in_specs=in_specs, out_specs=out_specs, check_vma=False
    )
```

time: 179 us -> 147 us (0.82)
  Pallas kernels: 52.4 us -> 36.8 us
  local copies, waits for them, and re-layouts: 13.8 us -> 6.75 us
  starting transfers between devices: 37.8 us -> 32.3 us
  waiting for transfers between devices: 47.2 us -> 45.3 us
    pallas_call x1 -> x3, Pallas kernels: 52.4 us -> 36.8 us  [the longest x1 19.9 us: backward(): pl.pallas_call(backward_kernel, out_shape=(column, column, column, half,...]
    ppermute x8, waiting for transfers between devices: 23.3 us -> 30.9 us  [around(): lax.ppermute(value, axis, [(at, (at + steps) % count) for at in range(cou...]
    unnamed x26 -> x14, local copies, waits for them, and re-layouts: 11.7 us -> 5.58 us
    ppermute x4, starting transfers between devices: 12.6 us -> 6.89 us  [the longest x2 6.81 us: swapped(): lax.ppermute(value, 'tile', [(at, at ^ 1) for at in range(lax.axis_size('...]
    ppermute x4, waiting for transfers between devices: 16.3 us -> 10.6 us  [the longest x1 6.63 us: per_device(): measured = lax.ppermute(measured, ('strip', 'tile'), diagonal)]
    all_to_all x2, waiting for transfers between devices: 7.65 us -> 3.79 us  [exchanged(): lax.all_to_all(value, axis, 0, 0, tiled=True, axis_index_groups=groups)]
    ppermute x8, starting transfers between devices: 13.9 us -> 17.3 us  [around(): lax.ppermute(value, axis, [(at, (at + steps) % count) for at in range(cou...]
    all_to_all x2, starting transfers between devices: 11.2 us -> 8.09 us  [exchanged(): lax.all_to_all(value, axis, 0, 0, tiled=True, axis_index_groups=groups)]
  transfers between devices with their start and end apart: 14 -> 14, of which waited for: 9 -> 9; matrix products, arithmetic and copies ran while one was open for 2% -> 3% of each run, Pallas kernels for 0% -> 11%
where the time goes in v2:
time: 147 us
  waiting for transfers between devices  45.3 us (31%)
  Pallas kernels  36.8 us (25%)
  starting transfers between devices  32.3 us (22%)
  blocking collectives  18.1 us (12%)
  other arithmetic  6.79 us (5%)
  local copies, waits for them, and re-layouts  6.75 us (5%)
    ppermute x8, waiting for transfers between devices, around(): lax.ppermute(value, axis, [(at, (at + steps) % count) for at in range(cou...  30.9 us
    pallas_call x1, Pallas kernels, backward(): pl.pallas_call(backward_kernel, out_shape=(column, column, column, half,...  19.9 us
    all_to_all x1, blocking collectives, exchanged(): lax.all_to_all(value, axis, 0, 0, tiled=True, axis_index_groups=groups)  18.1 us
    ppermute x8, starting transfers between devices, around(): lax.ppermute(value, axis, [(at, (at + steps) % count) for at in range(cou...  17.3 us
    pallas_call x1, Pallas kernels, forward(): pl.pallas_call(forward_kernel, out_shape=(jax.ShapeDtypeStruct((count, 2,...  15.1 us
    all_to_all x2, starting transfers between devices, exchanged(): lax.all_to_all(value, axis, 0, 0, tiled=True, axis_index_groups=groups)  8.09 us
    ppermute x2, starting transfers between devices, swapped(): lax.ppermute(value, 'tile', [(at, at ^ 1) for at in range(lax.axis_size('...  6.81 us
    ppermute x1, waiting for transfers between devices, per_device(): measured = lax.ppermute(measured, ('strip', 'tile'), diagonal)  6.63 us
  transfers between devices with their start and end apart: 14, of which 9 were waited for; matrix products, arithmetic and copies ran while one was open for 3% of the time, Pallas kernels for 11%

profile of v2, /device:TPU:1, one launch (start us, length us, event | category | flops | bytes accessed | tf_op | source)
XLA Modules:
  0.0 146.7 jit_solution(2711631501501034398)
XLA Ops:
  0.6 2.2 %collective-permute-start.1 = (f32[2,2,128,128]{3,2,1,0:T(8,128)}, f32[2,2,128,128]{3,2,1,0:T(8,128)S(1)}, u32[]{:S(2)}, u32[]{:S(2)}) collective-permute-start(f32[2,2,128,128]{3,2,1,0:T(8,128)} %param.7), channel_id=1, source_target_pairs={{0,16},{16,32},{32,48},{48,64},{64,80},{80,96},{96,112},{112,128},... | collective-permute-start | bytes 786440 | tf_op jit(solution)/shard_map/ppermute | solution.py:386
  2.8 3.7 %collective-permute-start.2 = (f32[2,2,128,128]{3,2,1,0:T(8,128)}, f32[2,2,128,128]{3,2,1,0:T(8,128)S(1)}, u32[]{:S(2)}, u32[]{:S(2)}) collective-permute-start(f32[2,2,128,128]{3,2,1,0:T(8,128)} %param.7), channel_id=1, source_target_pairs={{0,240},{16,0},{32,16},{48,32},{64,48},{80,64},{96,80},{112,96},{1... | collective-permute-start | bytes 786440 | tf_op jit(solution)/shard_map/ppermute | solution.py:386
  6.6 4.2 %collective-permute-done.1 = f32[2,2,128,128]{3,2,1,0:T(8,128)S(1)} collective-permute-done((f32[2,2,128,128]{3,2,1,0:T(8,128)}, f32[2,2,128,128]{3,2,1,0:T(8,128)S(1)}, u32[]{:S(2)}, u32[]{:S(2)}) %collective-permute-start.1) | collective-permute-done | bytes 262176 | tf_op jit(solution)/shard_map/ppermute | solution.py:386
  11.8 3.2 %collective-permute-start.4 = (f32[2,2,384,128]{3,2,1,0:T(8,128)S(1)}, f32[2,2,384,128]{3,2,1,0:T(8,128)S(1)}, u32[]{:S(2)}, u32[]{:S(2)}) collective-permute-start(f32[2,2,384,128]{3,2,1,0:T(8,128)S(1)} %constant_dynamic-update-slice_fusion.middle), channel_id=1, source_target_pairs={{0,15},{1,0},{2,1},{3,2},{4,3},{5,4},{6,5},{7,6},{8,7},{9,8},{10,9... | collective-permute-start | bytes 2359304 | tf_op jit(solution)/shard_map/ppermute | solution.py:386
  15.0 1.5 %collective-permute-start.3 = (f32[2,2,384,128]{3,2,1,0:T(8,128)S(1)}, f32[2,2,384,128]{3,2,1,0:T(8,128)S(1)}, u32[]{:S(2)}, u32[]{:S(2)}) collective-permute-start(f32[2,2,384,128]{3,2,1,0:T(8,128)S(1)} %constant_dynamic-update-slice_fusion.middle), channel_id=1, source_target_pairs={{0,1},{1,2},{2,3},{3,4},{4,5},{5,6},{6,7},{7,8},{8,9},{9,10},{10,1... | collective-permute-start | bytes 2359304 | tf_op jit(solution)/shard_map/ppermute | solution.py:386
  17.4 1.6 %copy-done = f32[2,4,256,256]{3,2,1,0:T(8,128)S(1)} copy-done((f32[2,4,256,256]{3,2,1,0:T(8,128)S(1)}, f32[2,4,256,256]{3,2,1,0:T(8,128)}, u32[]{:S(2)}) %copy-start) | copy-done | bytes 2097176
  21.1 1.8 %prepare.1 = (f32[2,4,256,256]{3,2,1,0:T(8,128)S(1)}, f32[2,256,256]{2,1,0:T(8,128)S(1)}, bf16[4,2,2,256,256]{4,3,2,1,0:T(8,128)(2,1)S(1)}) custom-call(f32[2,4,256,256]{3,2,1,0:T(8,128)S(1)} %copy-done, f32[2,256,256]{2,1,0:T(8,128)S(1)} %copy-done.1, bf16[2,2,2,2,128,128]{5,4,3,2,1,0:T(8,128)(2,1)S(1)} %copy-done.3), custom_call_target="tpu_custom_call" | custom-call | flops 3221225472 | bytes 6291456 | tf_op jit(solution)/shard_map/prepare/pallas_call | solution.py:168
  22.9 3.6 %collective-permute-done.4.right = f32[2,2,384,128]{3,2,1,0:T(8,128)S(1)} collective-permute-done((f32[2,2,384,128]{3,2,1,0:T(8,128)S(1)}, f32[2,2,384,128]{3,2,1,0:T(8,128)S(1)}, u32[]{:S(2)}, u32[]{:S(2)}) %collective-permute-start.4) | collective-permute-done | bytes 786464 | tf_op jit(solution)/shard_map/ppermute | solution.py:386
  26.5 15.1 %forward.1 = (f32[2,2,2,256,256]{4,3,2,1,0:T(8,128)S(1)}, f32[2,2,4,256,256]{4,3,2,1,0:T(8,128)S(1)}, f32[2,2,4,256,256]{4,3,2,1,0:T(8,128)S(1)}, f32[2,256,256]{2,1,0:T(8,128)S(1)}) custom-call(s32[3,2]{1,0:T(4,128)S(1)} %collective-permute-done.offsets.scalars, f32[2,2,384,128]{3,2,1,0:T(8,128)S(1)} %collective-permute-done.3.left, ...), custom_call_target="tpu_custom_call" | custom-call | flops 12884901888 | bytes 18874368 | tf_op jit(solution)/shard_map/forward/pallas_call | solution.py:241
  41.6 6.6 %collective-permute-done.5.measured = f32[2,256,256]{2,1,0:T(8,128)S(1)} collective-permute-done((f32[2,256,256]{2,1,0:T(8,128)S(1)}, f32[2,256,256]{2,1,0:T(8,128)S(1)}, u32[]{:S(2)}, u32[]{:S(2)}) %collective-permute-start.5) | collective-permute-done | bytes 524320 | tf_op jit(solution)/shard_map/ppermute | solution.py:426
  48.2 19.9 %backward.1 = (f32[2,2,384,128]{3,2,1,0:T(8,128)S(1)}, f32[2,2,384,128]{3,2,1,0:T(8,128)S(1)}, f32[2,2,384,128]{3,2,1,0:T(8,128)S(1)}, f32[4,256,256]{2,1,0:T(8,128)S(1)}, f32[4,256,256]{2,1,0:T(8,128)S(1)}) custom-call(s32[3,2]{1,0:T(4,128)S(1)} %collective-permute-done.offsets.scalars, f32[2,2,2,256,256]{4,3,2,1,0:T(8,128)S(1)} %get-tuple-element.28.window, ...), custom_call_target="tpu_custom_call" | custom-call | flops 12884901888 | bytes 18874368 | tf_op jit(solution)/shard_map/backward/pallas_call | solution.py:362
  68.1 2.6 %collective-permute-start.6 = (f32[4,256,256]{2,1,0:T(8,128)S(1)}, f32[4,256,256]{2,1,0:T(8,128)S(1)}, u32[]{:S(2)}, u32[]{:S(2)}) collective-permute-start(f32[4,256,256]{2,1,0:T(8,128)S(1)} %get-tuple-element.35), channel_id=1, source_target_pairs={{0,1},{1,0},{2,3},{3,2},{4,5},{5,4},{6,7},{7,6},{8,9},{9,8},{10,11... | collective-permute-start | bytes 3145736 | tf_op jit(solution)/shard_map/ppermute | solution.py:398
  70.7 2.3 %collective-permute-done.6 = f32[4,256,256]{2,1,0:T(8,128)S(1)} collective-permute-done((f32[4,256,256]{2,1,0:T(8,128)S(1)}, f32[4,256,256]{2,1,0:T(8,128)S(1)}, u32[]{:S(2)}, u32[]{:S(2)}) %collective-permute-start.6) | collective-permute-done | bytes 1048608 | tf_op jit(solution)/shard_map/ppermute | solution.py:398
  74.1 3.7 %all-to-all-start = ((f32[16,64,256]{2,1,0:T(8,128)}), f32[16,64,256]{2,1,0:T(8,128)S(1)}, u32[]{:S(2)}, u32[]{:S(2)}) async-start(f32[16,64,256]{2,1,0:T(8,128)} %bitcast.2), calls=%async_computation | async-start | bytes 2097152 | tf_op jit(solution)/shard_map/all_to_all | solution.py:390
  79.5 10.1 %collective-permute-done.7 = f32[2,2,384,128]{3,2,1,0:T(8,128)S(1)} collective-permute-done((f32[2,2,384,128]{3,2,1,0:T(8,128)S(1)}, f32[2,2,384,128]{3,2,1,0:T(8,128)S(1)}, u32[]{:S(2)}, u32[]{:S(2)}) %collective-permute-start.7) | collective-permute-done | bytes 786464 | tf_op jit(solution)/shard_map/ppermute | solution.py:386
  90.5 3.8 %all-to-all-done = f32[16,64,256]{2,1,0:T(8,128)S(1)} async-done(((f32[16,64,256]{2,1,0:T(8,128)}), f32[16,64,256]{2,1,0:T(8,128)S(1)}, u32[]{:S(2)}, u32[]{:S(2)}) %all-to-all-start) | async-done | bytes 1048608 | tf_op jit(solution)/shard_map/all_to_all | solution.py:390
  94.4 18.1 %all_to_all.15 = f32[8,64,256]{2,1,0:T(8,128)S(1)} all-to-all(f32[8,64,256]{2,1,0:T(8,128)S(1)} %broadcast_in_dim.6), channel_id=1, replica_groups={{0,2,4,6,8,10,12,14},{1,3,5,7,9,11,13,15},{16,18,20,22,24,26,28,30},{17..., dimensions={0} | all-to-all | bytes 1048576 | tf_op jit(solution)/shard_map/all_to_all | solution.py:390
  113.6 4.4 %all-to-all-start.2 = ((f32[16,64,256]{2,1,0:T(8,128)}), f32[16,64,256]{2,1,0:T(8,128)S(1)}, u32[]{:S(2)}, u32[]{:S(2)}) async-start(f32[16,64,256]{2,1,0:T(8,128)} %broadcast_in_dim.7), calls=%async_computation.2 | async-start | bytes 2097152 | tf_op jit(solution)/shard_map/all_to_all | solution.py:390
  119.3 1.4 collective-permute-start.10
  120.8 3.4 %collective-permute-start.9 = (f32[2,2,128,128]{3,2,1,0:T(8,128)S(1)}, f32[2,2,128,128]{3,2,1,0:T(8,128)S(1)}, u32[]{:S(2)}, u32[]{:S(2)}) collective-permute-start(f32[2,2,128,128]{3,2,1,0:T(8,128)S(1)} %get-tuple-element.47), channel_id=1, source_target_pairs={{0,240},{16,0},{32,16},{48,32},{64,48},{80,64},{96,80},{112,96},{1... | collective-permute-start | bytes 786440 | tf_op jit(solution)/shard_map/ppermute | solution.py:386
  124.2 12.8 %collective-permute-done.10 = f32[2,2,128,128]{3,2,1,0:T(8,128)S(1)} collective-permute-done((f32[2,2,128,128]{3,2,1,0:T(8,128)S(1)}, f32[2,2,128,128]{3,2,1,0:T(8,128)S(1)}, u32[]{:S(2)}, u32[]{:S(2)}) %collective-permute-start.10) | collective-permute-done | bytes 262176 | tf_op jit(solution)/shard_map/ppermute | solution.py:386
  137.2 4.3 %collective-permute-start.11 = (f32[16,64,256]{2,1,0:T(8,128)S(1)}, f32[16,64,256]{2,1,0:T(8,128)}, u32[]{:S(2)}, u32[]{:S(2)}) collective-permute-start(f32[16,64,256]{2,1,0:T(8,128)S(1)} %all-to-all-done.2), channel_id=1, source_target_pairs={{0,1},{1,0},{2,3},{3,2},{4,5},{5,4},{6,7},{7,6},{8,9},{9,8},{10,11... | collective-permute-start | bytes 3145736 | tf_op jit(solution)/shard_map/ppermute | solution.py:398
  142.2 1.7 %collective-permute-done.11 = f32[16,64,256]{2,1,0:T(8,128)} collective-permute-done((f32[16,64,256]{2,1,0:T(8,128)S(1)}, f32[16,64,256]{2,1,0:T(8,128)}, u32[]{:S(2)}, u32[]{:S(2)}) %collective-permute-start.11) | collective-permute-done | bytes 1048608 | tf_op jit(solution)/shard_map/ppermute | solution.py:398
  145.2 1.5 %pad_maximum_fusion = f32[2,4,256,256]{3,2,1,0:T(8,128)} fusion(f32[1,4,256,256]{3,2,1,0:T(8,128)S(1)} %bitcast.6, f32[1,4,256,256]{3,2,1,0:T(8,128)S(1)} %bitcast.5), kind=kLoop, calls=%fused_computation | loop fusion | flops 524288 | bytes 4194304 | tf_op jit(solution)/shard_map/stack | solution.py:447
  (36 shorter events, 12.5 us)
Async XLA Ops:
  0.6 10.1 %collective-permute-start.1 = (f32[2,2,128,128]{3,2,1,0:T(8,128)}, f32[2,2,128,128]{3,2,1,0:T(8,128)S(1)}, u32[]{:S(2)}, u32[]{:S(2)}) collective-permute-start(f32[2,2,128,128]{3,2,1,0:T(8,128)} %param.7), channel_id=1, source_target_pairs={{0,16},{16,32},{32,48},{48,64},{64,80},{80,96},{96,112},{112,128},... | collective-permute-start | bytes 786440 | tf_op jit(solution)/shard_map/ppermute | solution.py:386
  2.8 8.9 %collective-permute-start.2 = (f32[2,2,128,128]{3,2,1,0:T(8,128)}, f32[2,2,128,128]{3,2,1,0:T(8,128)S(1)}, u32[]{:S(2)}, u32[]{:S(2)}) collective-permute-start(f32[2,2,128,128]{3,2,1,0:T(8,128)} %param.7), channel_id=1, source_target_pairs={{0,240},{16,0},{32,16},{48,32},{64,48},{80,64},{96,80},{112,96},{1... | collective-permute-start | bytes 786440 | tf_op jit(solution)/shard_map/ppermute | solution.py:386
  11.8 14.7 %collective-permute-start.4 = (f32[2,2,384,128]{3,2,1,0:T(8,128)S(1)}, f32[2,2,384,128]{3,2,1,0:T(8,128)S(1)}, u32[]{:S(2)}, u32[]{:S(2)}) collective-permute-start(f32[2,2,384,128]{3,2,1,0:T(8,128)S(1)} %constant_dynamic-update-slice_fusion.middle), channel_id=1, source_target_pairs={{0,15},{1,0},{2,1},{3,2},{4,3},{5,4},{6,5},{7,6},{8,7},{9,8},{10,9... | collective-permute-start | bytes 2359304 | tf_op jit(solution)/shard_map/ppermute | solution.py:386
  15.0 11.5 %collective-permute-start.3 = (f32[2,2,384,128]{3,2,1,0:T(8,128)S(1)}, f32[2,2,384,128]{3,2,1,0:T(8,128)S(1)}, u32[]{:S(2)}, u32[]{:S(2)}) collective-permute-start(f32[2,2,384,128]{3,2,1,0:T(8,128)S(1)} %constant_dynamic-update-slice_fusion.middle), channel_id=1, source_target_pairs={{0,1},{1,2},{2,3},{3,4},{4,5},{5,6},{6,7},{7,8},{8,9},{9,10},{10,1... | collective-permute-start | bytes 2359304 | tf_op jit(solution)/shard_map/ppermute | solution.py:386
  17.3 9.2 %collective-permute-start = (s32[3,2]{1,0:T(4,128)S(1)}, s32[3,2]{1,0:T(4,128)S(1)}, u32[]{:S(2)}, u32[]{:S(2)}) collective-permute-start(s32[3,2]{1,0:T(4,128)S(1)} %concatenate.11), channel_id=1, source_target_pairs={{0,17},{1,18},{2,19},{3,20},{4,21},{5,22},{6,23},{7,24},{8,25},{9,... | collective-permute-start | bytes 80 | tf_op jit(solution)/shard_map/ppermute | solution.py:420
  17.4 1.6 %copy-start = (f32[2,4,256,256]{3,2,1,0:T(8,128)S(1)}, f32[2,4,256,256]{3,2,1,0:T(8,128)}, u32[]{:S(2)}) copy-start(f32[2,4,256,256]{3,2,1,0:T(8,128)} %probe_in.1) | copy-start | bytes 6291460
  19.0 1.0 copy-start.1
  20.0 1.0 copy-start.3
  21.1 5.4 %copy-start.2 = (f32[2,256,256]{2,1,0:T(8,128)S(1)}, f32[2,256,256]{2,1,0:T(8,128)}, u32[]{:S(2)}) copy-start(f32[2,256,256]{2,1,0:T(8,128)} %constant.40.clone.phase) | copy-start | bytes 1572868
  26.5 21.7 %collective-permute-start.5 = (f32[2,256,256]{2,1,0:T(8,128)S(1)}, f32[2,256,256]{2,1,0:T(8,128)S(1)}, u32[]{:S(2)}, u32[]{:S(2)}) collective-permute-start(f32[2,256,256]{2,1,0:T(8,128)S(1)} %get-tuple-element.32), channel_id=1, source_target_pairs={{0,17},{1,18},{2,19},{3,20},{4,21},{5,22},{6,23},{7,24},{8,25},{9,... | collective-permute-start | bytes 1572872 | tf_op jit(solution)/shard_map/ppermute | solution.py:426
  68.1 4.8 %collective-permute-start.6 = (f32[4,256,256]{2,1,0:T(8,128)S(1)}, f32[4,256,256]{2,1,0:T(8,128)S(1)}, u32[]{:S(2)}, u32[]{:S(2)}) collective-permute-start(f32[4,256,256]{2,1,0:T(8,128)S(1)} %get-tuple-element.35), channel_id=1, source_target_pairs={{0,1},{1,0},{2,3},{3,2},{4,5},{5,4},{6,7},{7,6},{8,9},{9,8},{10,11... | collective-permute-start | bytes 3145736 | tf_op jit(solution)/shard_map/ppermute | solution.py:398
  74.1 20.2 %all-to-all-start = ((f32[16,64,256]{2,1,0:T(8,128)}), f32[16,64,256]{2,1,0:T(8,128)S(1)}, u32[]{:S(2)}, u32[]{:S(2)}) async-start(f32[16,64,256]{2,1,0:T(8,128)} %bitcast.2), calls=%async_computation | async-start | bytes 2097152 | tf_op jit(solution)/shard_map/all_to_all | solution.py:390
  77.8 11.8 %collective-permute-start.7 = (f32[2,2,384,128]{3,2,1,0:T(8,128)S(1)}, f32[2,2,384,128]{3,2,1,0:T(8,128)S(1)}, u32[]{:S(2)}, u32[]{:S(2)}) collective-permute-start(f32[2,2,384,128]{3,2,1,0:T(8,128)S(1)} %get-tuple-element.36), channel_id=1, source_target_pairs={{0,15},{1,0},{2,1},{3,2},{4,3},{5,4},{6,5},{7,6},{8,7},{9,8},{10,9... | collective-permute-start | bytes 2359304 | tf_op jit(solution)/shard_map/ppermute | solution.py:386
  78.1 12.4 %collective-permute-start.8 = (f32[2,2,384,128]{3,2,1,0:T(8,128)S(1)}, f32[2,2,384,128]{3,2,1,0:T(8,128)}, u32[]{:S(2)}, u32[]{:S(2)}) collective-permute-start(f32[2,2,384,128]{3,2,1,0:T(8,128)S(1)} %get-tuple-element.37), channel_id=1, source_target_pairs={{0,1},{1,2},{2,3},{3,4},{4,5},{5,6},{6,7},{7,8},{8,9},{9,10},{10,1... | collective-permute-start | bytes 2359304 | tf_op jit(solution)/shard_map/ppermute | solution.py:386
  89.6 0.9 copy-start.4
  112.5 5.6 %copy-start.5 = (f32[2,2,384,128]{3,2,1,0:T(8,128)S(1)}, f32[2,2,384,128]{3,2,1,0:T(8,128)}, u32[]{:S(2)}) copy-start(f32[2,2,384,128]{3,2,1,0:T(8,128)} %copy-done.4) | copy-start | bytes 2359300
  113.6 23.6 %all-to-all-start.2 = ((f32[16,64,256]{2,1,0:T(8,128)}), f32[16,64,256]{2,1,0:T(8,128)S(1)}, u32[]{:S(2)}, u32[]{:S(2)}) async-start(f32[16,64,256]{2,1,0:T(8,128)} %broadcast_in_dim.7), calls=%async_computation.2 | async-start | bytes 2097152 | tf_op jit(solution)/shard_map/all_to_all | solution.py:390
  119.3 17.7 %collective-permute-start.10 = (f32[2,2,128,128]{3,2,1,0:T(8,128)S(1)}, f32[2,2,128,128]{3,2,1,0:T(8,128)S(1)}, u32[]{:S(2)}, u32[]{:S(2)}) collective-permute-start(f32[2,2,128,128]{3,2,1,0:T(8,128)S(1)} %get-tuple-element.46), channel_id=1, source_target_pairs={{0,16},{16,32},{32,48},{48,64},{64,80},{80,96},{96,112},{112,128},... | collective-permute-start | bytes 786440 | tf_op jit(solution)/shard_map/ppermute | solution.py:386
  120.8 16.4 %collective-permute-start.9 = (f32[2,2,128,128]{3,2,1,0:T(8,128)S(1)}, f32[2,2,128,128]{3,2,1,0:T(8,128)S(1)}, u32[]{:S(2)}, u32[]{:S(2)}) collective-permute-start(f32[2,2,128,128]{3,2,1,0:T(8,128)S(1)} %get-tuple-element.47), channel_id=1, source_target_pairs={{0,240},{16,0},{32,16},{48,32},{64,48},{80,64},{96,80},{112,96},{1... | collective-permute-start | bytes 786440 | tf_op jit(solution)/shard_map/ppermute | solution.py:386
  137.2 6.7 %collective-permute-start.11 = (f32[16,64,256]{2,1,0:T(8,128)S(1)}, f32[16,64,256]{2,1,0:T(8,128)}, u32[]{:S(2)}, u32[]{:S(2)}) collective-permute-start(f32[16,64,256]{2,1,0:T(8,128)S(1)} %all-to-all-done.2), channel_id=1, source_target_pairs={{0,1},{1,0},{2,3},{3,2},{4,5},{5,4},{6,7},{7,6},{8,9},{9,8},{10,11... | collective-permute-start | bytes 3145736 | tf_op jit(solution)/shard_map/ppermute | solution.py:398

commit v3 on v2

--- a/solution.py
+++ b/solution.py
@@ -138,7 +138,7 @@
     ]
 
 
-def prepare_kernel(probe_in, measured_in, blocks, probe, measured, tables):
+def prepare_kernel(probe_in, blocks, probe, tables):
     h = blocks.shape[-1]
     for field in range(2):
         for parity in range(2):
@@ -159,42 +159,45 @@
         return carry
 
     lax.fori_loop(0, 2, fold, 0)
-    for at, plane in enumerate(folded([measured_in[at] for at in range(measured.shape[0])])):
-        measured[at] = plane
-
-
-def prepared(probe, measured, blocks):
+
+
+def prepared(probe, blocks):
     n = probe.shape[-1]
     return pl.pallas_call(
         prepare_kernel,
         out_shape=(
             jax.ShapeDtypeStruct(probe.shape, F32),
-            jax.ShapeDtypeStruct(measured.shape, F32),
             jax.ShapeDtypeStruct((4, 2, 2, n, n), BF),
         ),
-        in_specs=[VMEM] * 3,
-        out_specs=(VMEM,) * 3,
+        in_specs=[VMEM] * 2,
+        out_specs=(VMEM,) * 2,
         compiler_params=pltpu.CompilerParams(vmem_limit_bytes=24 << 20),
         cost_estimate=pl.CostEstimate(flops=3 << 30, bytes_accessed=6 << 20, transcendentals=0),
         name="prepare",
-    )(probe, measured, blocks)
+    )(probe, blocks)
 
 
 def forward_kernel(
-    offsets, left, middle, right, probe, tables, phase,
+    offsets, left, left_edges, middle, middle_edges, right, right_edges, probe, tables, phase,
     window, moved, far, intensity,
     lhs_high, lhs_low, rhs_high, rhs_low, wide, sems,
 ):
     n, modes = probe.shape[-1], probe.shape[1]
     rows, tile = wide.shape[2], wide.shape[3] // 3
-    columns = [
-        pltpu.make_async_copy(source, wide.at[:, :, :, at * tile : (at + 1) * tile], sems.at[at])
-        for at, source in enumerate((left, middle, right))
-    ]
-    for column in columns:
-        column.start()
-    for column in columns:
-        column.wait()
+    pieces = []
+    for across, (own, edges) in enumerate(
+        ((left, left_edges), (middle, middle_edges), (right, right_edges))
+    ):
+        sources = (edges.at[:, :, :tile], own, edges.at[:, :, tile:])
+        for down, source in enumerate(sources):
+            place = wide.at[
+                :, :, down * tile : (down + 1) * tile, across * tile : (across + 1) * tile
+            ]
+            pieces.append(pltpu.make_async_copy(source, place, sems.at[len(pieces)]))
+    for piece in pieces:
+        piece.start()
+    for piece in pieces:
+        piece.wait()
     buffers = (tables, lhs_high, lhs_low, rhs_high, rhs_low)
 
     def visit(position, carry):
@@ -234,9 +237,9 @@
     lax.fori_loop(0, window.shape[0], visit, 0)
 
 
-def forward(count, offsets, left, middle, right, probe, tables, phase):
+def forward(count, offsets, tiles, probe, tables, phase):
     n, modes = probe.shape[-1], probe.shape[1]
-    rows, tile = middle.shape[2], middle.shape[3]
+    tile = tiles[0].shape[-1]
     fields = jax.ShapeDtypeStruct((count,) + probe.shape, F32)
     return pl.pallas_call(
         forward_kernel,
@@ -246,30 +249,31 @@
             fields,
             jax.ShapeDtypeStruct((count, n, n), F32),
         ),
-        in_specs=[SMEM] + [ANY] * 3 + [VMEM] * 3,
+        in_specs=[SMEM] + [ANY] * 6 + [VMEM] * 3,
         out_specs=(VMEM,) * 4,
         scratch_shapes=sandwich_scratch(n, modes)
-        + [pltpu.VMEM((2, 2, rows, 3 * tile), F32), pltpu.SemaphoreType.DMA((3,))],
+        + [pltpu.VMEM((2, 2, 3 * tile, 3 * tile), F32), pltpu.SemaphoreType.DMA((9,))],
         compiler_params=pltpu.CompilerParams(vmem_limit_bytes=SCOPED_F << 20),
         cost_estimate=pl.CostEstimate(
             flops=count * modes * 8 * 12 * n**3, bytes_accessed=18 << 20, transcendentals=0
         ),
         name="forward",
-    )(offsets, left, middle, right, probe, tables, phase)
+    )(offsets, *tiles, probe, tables, phase)
 
 
 def backward_kernel(
-    scalars, window, moved, far, intensity, measured, probe, tables, phase,
-    grad_left, grad_middle, grad_right, kept, sent,
-    lhs_high, lhs_low, rhs_high, rhs_low, wide, probe_grad, sems,
+    core, window, moved, far, intensity, measured, probe, tables, phase,
+    totals, kept, sent,
+    lhs_high, lhs_low, rhs_high, rhs_low, probe_grad, amplitude, sems,
 ):
     n, modes = probe.shape[-1], probe.shape[1]
-    rows, tile = wide.shape[2], wide.shape[3] // 3
-    count = window.shape[0]
     buffers = (tables, lhs_high, lhs_low, rhs_high, rhs_low)
+    count = measured.shape[0]
+    for at, plane in enumerate(folded([measured[at] for at in range(count)])):
+        amplitude[at] = plane
 
     def visit(position, carry):
-        scaling = 1.0 - measured[position] / jnp.sqrt(intensity[position] + 1.0)
+        scaling = 1.0 - amplitude[position] / jnp.sqrt(intensity[position] + 1.0)
         fields = [
             (scaling * far[position, 0, mode], scaling * far[position, 1, mode])
             for mode in range(modes)
@@ -283,10 +287,8 @@
             total_re = total_re + (moved_re * re + moved_im * im)
             total_im = total_im + (moved_re * im - moved_im * re)
             behinds.append((low_re * re + low_im * im, low_re * im - low_im * re))
-        grad_low = (
-            total_re * phase[0] + total_im * phase[1],
-            total_im * phase[0] - total_re * phase[1],
-        )
+        totals[position, 0, 1] = total_re * phase[0] + total_im * phase[1]
+        totals[position, 1, 1] = total_im * phase[0] - total_re * phase[1]
         fields = sandwich(behinds, PROP_CONJ, *buffers)
         top_re, top_im = window[position, 0, 0], window[position, 1, 0]
         total_re = total_im = jnp.zeros((n, n), F32)
@@ -307,34 +309,11 @@
                 probe_grad[0, mode] += term_re
                 probe_grad[1, mode] += term_im
 
-        planes = folded([total_re, total_im, *grad_low])
-        row, col = scalars[position, 0], scalars[position, 1]
-        for layer in range(2):
-            for part in range(2):
-                plane = jnp.concatenate(
-                    [planes[2 * layer + part], jnp.zeros((rows - n, n), F32)], axis=0
-                )
-                plane = pltpu.roll(plane, row, 0)
-                plane = jnp.concatenate([plane, jnp.zeros((rows, 3 * tile - n), F32)], axis=1)
-                plane = pltpu.roll(plane, col, 1)
-
-                @pl.when(position == 0)
-                def _():
-                    wide[part, layer] = plane
-
-                @pl.when(position != 0)
-                def _():
-                    wide[part, layer] += plane
-
+        totals[position, 0, 0] = total_re
+        totals[position, 1, 0] = total_im
         return carry
 
-    lax.fori_loop(0, count, visit, 0)
-    copies = [
-        pltpu.make_async_copy(wide.at[:, :, :, at * tile : (at + 1) * tile], target, sems.at[at])
-        for at, target in enumerate((grad_left, grad_middle, grad_right))
-    ]
-    for copy in copies:
-        copy.start()
+    lax.fori_loop(0, window.shape[0], visit, 0)
 
     def unfold(part, carry):
         planes = folded([probe_grad[part, mode] for mode in range(modes)])
@@ -343,39 +322,86 @@
         return carry
 
     lax.fori_loop(0, 2, unfold, 0)
-    core = scalars[count, 0]
-    parts = [
-        pltpu.make_async_copy(probe_grad.at[core], kept, sems.at[3]),
-        pltpu.make_async_copy(probe_grad.at[1 - core], sent, sems.at[4]),
-    ]
-    for part in parts:
-        part.start()
-    for copy in copies + parts:
+    copies = [
+        pltpu.make_async_copy(probe_grad.at[part], target, sems.at[at])
+        for at, (part, target) in enumerate(((core[0], kept), (1 - core[0], sent)))
+    ]
+    for copy in copies:
+        copy.start()
+    for copy in copies:
         copy.wait()
 
 
-def backward(scalars, state, measured, probe, tables, phase, rows, tile):
+def backward(core, state, measured, probe, tables, phase):
     n, modes = probe.shape[-1], probe.shape[1]
     count = measured.shape[0]
-    column = jax.ShapeDtypeStruct((2, 2, rows, tile), F32)
     half = jax.ShapeDtypeStruct(probe.shape[1:], F32)
     return pl.pallas_call(
         backward_kernel,
-        out_shape=(column, column, column, half, half),
+        out_shape=(jax.ShapeDtypeStruct((count, 2, 2, n, n), F32), half, half),
         in_specs=[SMEM] + [VMEM] * 8,
-        out_specs=(HBM,) * 5,
+        out_specs=(VMEM, HBM, HBM),
         scratch_shapes=sandwich_scratch(n, modes)
         + [
-            pltpu.VMEM((2, 2, rows, 3 * tile), F32),
             pltpu.VMEM(probe.shape, F32),
-            pltpu.SemaphoreType.DMA((5,)),
+            pltpu.VMEM(measured.shape, F32),
+            pltpu.SemaphoreType.DMA((2,)),
         ],
         compiler_params=pltpu.CompilerParams(vmem_limit_bytes=SCOPED_B << 20),
         cost_estimate=pl.CostEstimate(
             flops=count * modes * 8 * 12 * n**3, bytes_accessed=18 << 20, transcendentals=count * n * n
         ),
         name="backward",
-    )(scalars, *state, measured, probe, tables, phase)
+    )(core, *state, measured, probe, tables, phase)
+
+
+def place_kernel(scalars, totals, grad_left, grad_middle, grad_right, wide, sems):
+    n = totals.shape[-1]
+    rows, tile = wide.shape[2], wide.shape[3] // 3
+
+    def visit(position, carry):
+        row, col = scalars[position, 0], scalars[position, 1]
+        at = [(part, layer) for layer in range(2) for part in range(2)]
+        planes = folded([totals[position, part, layer] for part, layer in at])
+        for (part, layer), plane in zip(at, planes):
+            plane = jnp.concatenate([plane, jnp.zeros((rows - n, n), F32)], axis=0)
+            plane = pltpu.roll(plane, row, 0)
+            plane = jnp.concatenate([plane, jnp.zeros((rows, 3 * tile - n), F32)], axis=1)
+            plane = pltpu.roll(plane, col, 1)
+
+            @pl.when(position == 0)
+            def _():
+                wide[part, layer] = plane
+
+            @pl.when(position != 0)
+            def _():
+                wide[part, layer] += plane
+
+        return carry
+
+    lax.fori_loop(0, totals.shape[0], visit, 0)
+    copies = [
+        pltpu.make_async_copy(wide.at[:, :, :, at * tile : (at + 1) * tile], target, sems.at[at])
+        for at, target in enumerate((grad_left, grad_middle, grad_right))
+    ]
+    for copy in copies:
+        copy.start()
+    for copy in copies:
+        copy.wait()
+
+
+def placed(scalars, totals, rows, tile):
+    column = jax.ShapeDtypeStruct((2, 2, rows, tile), F32)
+    return pl.pallas_call(
+        place_kernel,
+        out_shape=(column,) * 3,
+        in_specs=[SMEM, VMEM],
+        out_specs=(HBM,) * 3,
+        scratch_shapes=[pltpu.VMEM((2, 2, rows, 3 * tile), F32), pltpu.SemaphoreType.DMA((3,))],
+        compiler_params=pltpu.CompilerParams(vmem_limit_bytes=16 << 20),
+        cost_estimate=pl.CostEstimate(flops=2 << 30, bytes_accessed=8 << 20, transcendentals=0),
+        name="place",
+    )(scalars, totals)
 
 
 SCOPED_F, SCOPED_B = 20, 20
@@ -402,6 +428,7 @@
     n = probe_modes.shape[-1]
     tile = object_field.shape[2]
     strips, tiles = lax.axis_size("strip"), lax.axis_size("tile")
+    both = ("strip", "tile")
     blocks, phase = parity_tables(n)
     phase = jnp.asarray(phase)
     diagonal = [
@@ -411,40 +438,65 @@
     ]
     corner = jnp.stack([lax.axis_index("strip"), lax.axis_index("tile")]).astype(jnp.int32) * tile
     wrap = jnp.array([strips * tile, tiles * tile], jnp.int32)
-    core_there = 1 - lax.axis_index("tile") % 2
-    scalars = jnp.concatenate(
-        [(offsets - corner) % wrap, jnp.full((1, 2), core_there, jnp.int32)], axis=0
-    )
+    scalars = lax.ppermute((offsets - corner) % wrap, both, diagonal)
     above = around(object_field, "strip", 1)
     below = around(object_field, "strip", -1)
-    scalars = lax.ppermute(scalars, ("strip", "tile"), diagonal)
-    probe, measured, tables = prepared(probe_modes, measured, jnp.asarray(blocks))
-    middle = jnp.concatenate([above, object_field, below], axis=2)
-    left = around(middle, "tile", 1)
-    right = around(middle, "tile", -1)
-    left, right, measured = lax.optimization_barrier((left, right, measured))
-    measured = lax.ppermute(measured, ("strip", "tile"), diagonal)
-    state = forward(measured.shape[0], scalars, left, middle, right, probe, tables, phase)
-    grad_left, grad_middle, grad_right, kept, sent = backward(
-        scalars, state, measured, probe, tables, phase, 3 * tile, tile
-    )
-
+    left = around(object_field, "tile", 1)
+    right = around(object_field, "tile", -1)
+    above, below, left, right, scalars, measured = lax.optimization_barrier(
+        (above, below, left, right, scalars, measured)
+    )
+    probe, tables = prepared(probe_modes, jnp.asarray(blocks))
+    edges = jnp.concatenate([above, below], axis=2)
+    left_edges = around(edges, "tile", 1)
+    right_edges = around(edges, "tile", -1)
+    measured = lax.ppermute(measured, both, diagonal)
+    pieces = (left, left_edges, object_field, edges, right, right_edges)
+    state = forward(measured.shape[0], scalars, pieces, probe, tables, phase)
+    core = (lax.axis_index("tile") % 2).astype(jnp.int32)
+    totals, kept, sent = backward(core.reshape(1), state, measured, probe, tables, phase)
+
+    cores, pairs = 2, 2
+    levels = tiles // cores
+    groups = [
+        [s * tiles + (pairs * group + at) * cores + c for s in range(strips) for at in range(pairs)]
+        for c in range(cores)
+        for group in range(levels // pairs)
+    ]
+    received = swapped(sent)
+    grad_left, grad_middle, grad_right = placed(scalars, totals, 3 * tile, tile)
+    received, grad_left, grad_middle, grad_right = lax.optimization_barrier(
+        (received, grad_left, grad_middle, grad_right)
+    )
     from_right = around(grad_left, "tile", -1)
     from_left = around(grad_right, "tile", 1)
-    part = (kept + swapped(sent)).reshape(strips, -1, n)
-    shares = exchanged(part, "strip")
-    shares, from_right, from_left = lax.optimization_barrier((shares, from_right, from_left))
+    shares = exchanged((kept + received).reshape(strips, -1, n), "strip")
     column = grad_middle + from_right + from_left
-    levels = [[core + 2 * z for z in range(tiles // 2)] for core in range(2)]
-    share = jnp.sum(exchanged(copies(jnp.sum(shares, axis=0), tiles // 2), "tile", levels), axis=0)
-    from_below = around(column[:, :, :tile], "strip", -1)
-    from_above = around(column[:, :, 2 * tile :], "strip", 1)
-    half = exchanged(copies(share, strips), "strip")
-    half, from_below, from_above = lax.optimization_barrier((half, from_below, from_above))
+    upper, lower = column[:, :, :tile], column[:, :, 2 * tile :]
+    from_below = around(upper, "strip", -1)
+    from_above = around(lower, "strip", 1)
+    shares, from_below, from_above = lax.optimization_barrier((shares, from_below, from_above))
+
+    def across(value, distance):
+        step = [
+            (z * cores + c, (z ^ distance) * cores + c) for z in range(levels) for c in range(cores)
+        ]
+        return lax.ppermute(value, "tile", step)
+
+    shares = jnp.sum(shares, axis=0).reshape(pairs, -1, n)
+    mine = lax.axis_index("tile") // cores % pairs
+    share = lax.dynamic_index_in_dim(shares, mine, 0, False) + across(
+        lax.dynamic_index_in_dim(shares, 1 - mine, 0, False), 1
+    )
+    distance = pairs
+    while distance < levels:
+        share = share + across(share, distance)
+        distance *= 2
     object_grad = column[:, :, tile : 2 * tile] + from_below + from_above
+    half = exchanged(copies(share, strips * pairs), both, groups)
     other = swapped(half)
-    first = lax.axis_index("tile") % 2 == 0
-    whole = jnp.stack([jnp.where(first, half, other), jnp.where(first, other, half)])
+    mine = (jnp.arange(cores) == lax.axis_index("tile") % cores).reshape(cores, 1, 1, 1)
+    whole = jnp.where(mine, half[None], other[None])
     return (object_grad, whole.reshape(probe_modes.shape))
 
 

time: 147 us -> 139 us (0.946)
  local copies, waits for them, and re-layouts: 6.75 us -> 2.84 us
  waiting for transfers between devices: 45.3 us -> 42.7 us
    ppermute x8 -> x10, waiting for transfers between devices: 30.9 us -> 12.9 us  [around(): lax.ppermute(value, axis, [(at, (at + steps) % count) for at in range(cou...]
    ppermute x2 -> x5, waiting for transfers between devices: 6.63 us -> 21.4 us  [the longest x3 11.5 us: across(): return lax.ppermute(value, 'tile', step)]
    all_to_all x2 -> x1, starting transfers between devices: 8.09 us -> 3.66 us  [exchanged(): lax.all_to_all(value, axis, 0, 0, tiled=True, axis_index_groups=groups)]
    all_to_all x2 -> x1, waiting for transfers between devices: 3.79 us -> 6.87 us  [exchanged(): lax.all_to_all(value, axis, 0, 0, tiled=True, axis_index_groups=groups)]
    unnamed x14 -> x11, local copies, waits for them, and re-layouts: 5.58 us -> 2.66 us
    ppermute x2, waiting for transfers between devices: 3.96 us -> 1.54 us  [swapped(): lax.ppermute(value, 'tile', [(at, at ^ 1) for at in range(lax.axis_size('...]
    ppermute x2, starting transfers between devices: 6.81 us -> 8.74 us  [swapped(): lax.ppermute(value, 'tile', [(at, at ^ 1) for at in range(lax.axis_size('...]
    ppermute x2 -> x5, starting transfers between devices: 0.08 us -> 1.81 us  [the longest x3 1.72 us: across(): return lax.ppermute(value, 'tile', step)]
  transfers between devices with their start and end apart: 14 -> 18, of which waited for: 9 -> 10; matrix products, arithmetic and copies ran while one was open for 3% -> 3% of each run, Pallas kernels for 11% -> 14%
where the time goes in v3:
time: 139 us; the launch traced here: 138 us
  waiting for transfers between devices  42.7 us (31%)
  Pallas kernels  35.9 us (26%)
  starting transfers between devices  31 us (22%)
  blocking collectives  19.5 us (14%)
  other arithmetic  5.78 us (4%)
  local copies, waits for them, and re-layouts  2.84 us (2%)
    all_to_all x1, blocking collectives, exchanged(): lax.all_to_all(value, axis, 0, 0, tiled=True, axis_index_groups=groups)  19.5 us
    ppermute x10, starting transfers between devices, around(): lax.ppermute(value, axis, [(at, (at + steps) % count) for at in range(cou...  16.8 us
    pallas_call x1, Pallas kernels, backward(): pl.pallas_call(backward_kernel, out_shape=(jax.ShapeDtypeStruct((count, 2...  15.8 us
    pallas_call x1, Pallas kernels, forward(): pl.pallas_call(forward_kernel, out_shape=(jax.ShapeDtypeStruct((count, 2,...  15 us
    ppermute x10, waiting for transfers between devices, around(): lax.ppermute(value, axis, [(at, (at + steps) % count) for at in range(cou...  12.9 us
    ppermute x3, waiting for transfers between devices, across(): return lax.ppermute(value, 'tile', step)  11.5 us
    ppermute x1, waiting for transfers between devices, per_device(): scalars = lax.ppermute((offsets - corner) % wrap, both, diagonal)  9.85 us
    ppermute x2, starting transfers between devices, swapped(): lax.ppermute(value, 'tile', [(at, at ^ 1) for at in range(lax.axis_size('...  8.74 us
  transfers between devices with their start and end apart: 18, of which 10 were waited for; matrix products, arithmetic and copies ran while one was open for 3% of the time, Pallas kernels for 14%

profile of v3, /device:TPU:1, one launch (start us, length us, event | category | flops | bytes accessed | tf_op | source)
XLA Modules:
  0.0 138.4 jit_solution(15246277895835099046)
XLA Ops:
  0.6 3.0 %collective-permute-start.2 = (f32[2,2,128,128]{3,2,1,0:T(8,128)}, f32[2,2,128,128]{3,2,1,0:T(8,128)S(1)}, u32[]{:S(2)}, u32[]{:S(2)}) collective-permute-start(f32[2,2,128,128]{3,2,1,0:T(8,128)} %middle.1), channel_id=1, source_target_pairs={{0,1},{1,2},{2,3},{3,4},{4,5},{5,6},{6,7},{7,8},{8,9},{9,10},{10,1... | collective-permute-start | bytes 786440 | tf_op jit(solution)/shard_map/ppermute | solution.py:412
  3.7 4.9 %collective-permute-start.1 = (f32[2,2,128,128]{3,2,1,0:T(8,128)}, f32[2,2,128,128]{3,2,1,0:T(8,128)S(1)}, u32[]{:S(2)}, u32[]{:S(2)}) collective-permute-start(f32[2,2,128,128]{3,2,1,0:T(8,128)} %middle.1), channel_id=1, source_target_pairs={{0,240},{16,0},{32,16},{48,32},{64,48},{80,64},{96,80},{112,96},{1... | collective-permute-start | bytes 786440 | tf_op jit(solution)/shard_map/ppermute | solution.py:412
  9.4 9.8 %collective-permute-done.4.offsets.scalars = s32[2,2]{1,0:T(2,128)S(1)} collective-permute-done((s32[2,2]{1,0:T(2,128)S(1)}, s32[2,2]{1,0:T(2,128)S(1)}, u32[]{:S(2)}, u32[]{:S(2)}) %collective-permute-start.4) | collective-permute-done | bytes 48 | tf_op jit(solution)/shard_map/ppermute | solution.py:441
  19.5 2.2 %collective-permute-start.6 = (f32[2,2,256,128]{3,2,1,0:T(8,128)S(1)}, f32[2,2,256,128]{3,2,1,0:T(8,128)S(1)}, u32[]{:S(2)}, u32[]{:S(2)}) collective-permute-start(f32[2,2,256,128]{3,2,1,0:T(8,128)S(1)} %constant_dynamic-update-slice_fusion.middle_edges), channel_id=1, source_target_pairs={{0,15},{1,0},{2,1},{3,2},{4,3},{5,4},{6,5},{7,6},{8,7},{9,8},{10,9... | collective-permute-start | bytes 1572872 | tf_op jit(solution)/shard_map/ppermute | solution.py:412
  21.8 1.6 %copy-done = f32[2,4,256,256]{3,2,1,0:T(8,128)S(1)} copy-done((f32[2,4,256,256]{3,2,1,0:T(8,128)S(1)}, f32[2,4,256,256]{3,2,1,0:T(8,128)}, u32[]{:S(2)}) %copy-start) | copy-done | bytes 2097176
  25.9 2.6 %collective-permute-done.6.right_edges = f32[2,2,256,128]{3,2,1,0:T(8,128)S(1)} collective-permute-done((f32[2,2,256,128]{3,2,1,0:T(8,128)S(1)}, f32[2,2,256,128]{3,2,1,0:T(8,128)S(1)}, u32[]{:S(2)}, u32[]{:S(2)}) %collective-permute-start.6) | collective-permute-done | bytes 524320 | tf_op jit(solution)/shard_map/ppermute | solution.py:412
  28.5 15.0 %forward.1 = (f32[2,2,2,256,256]{4,3,2,1,0:T(8,128)S(1)}, f32[2,2,4,256,256]{4,3,2,1,0:T(8,128)S(1)}, f32[2,2,4,256,256]{4,3,2,1,0:T(8,128)S(1)}, f32[2,256,256]{2,1,0:T(8,128)S(1)}) custom-call(s32[2,2]{1,0:T(2,128)S(1)} %collective-permute-done.4.offsets.scalars, f32[2,2,128,128]{3,2,1,0:T(8,128)S(1)} %collective-permute-done.2.left, ...), custom_call_target="tpu_custom_call" | custom-call | flops 12884901888 | bytes 18874368 | tf_op jit(solution)/shard_map/forward/pallas_call | solution.py:244
  43.5 15.8 %backward.1 = (f32[2,2,2,256,256]{4,3,2,1,0:T(8,128)S(1)}, f32[4,256,256]{2,1,0:T(8,128)S(1)}, f32[4,256,256]{2,1,0:T(8,128)S(1)}) custom-call(s32[1]{0:T(128)} %bitcast.core, f32[2,2,2,256,256]{4,3,2,1,0:T(8,128)S(1)} %get-tuple-element.34.window, f32[2,2,4,256,256]{4,3,2,1,0:T(8,128)S(1)} %get-tuple-element.35.moved, ...), custom_call_target="tpu_custom_call" | custom-call | flops 12884901888 | bytes 18874368 | tf_op jit(solution)/shard_map/backward/pallas_call | solution.py:339
  59.3 5.9 %collective-permute-start.8 = (f32[4,256,256]{2,1,0:T(8,128)S(1)}, f32[4,256,256]{2,1,0:T(8,128)S(1)}, u32[]{:S(2)}, u32[]{:S(2)}) collective-permute-start(f32[4,256,256]{2,1,0:T(8,128)S(1)} %get-tuple-element.39), channel_id=1, source_target_pairs={{0,1},{1,0},{2,3},{3,2},{4,5},{5,4},{6,7},{7,6},{8,9},{9,8},{10,11... | collective-permute-start | bytes 3145736 | tf_op jit(solution)/shard_map/ppermute | solution.py:424
  65.2 3.6 %place.1 = (f32[2,2,384,128]{3,2,1,0:T(8,128)S(1)}, f32[2,2,384,128]{3,2,1,0:T(8,128)S(1)}, f32[2,2,384,128]{3,2,1,0:T(8,128)S(1)}) custom-call(s32[2,2]{1,0:T(2,128)S(1)} %collective-permute-done.4.offsets.scalars, f32[2,2,2,256,256]{4,3,2,1,0:T(8,128)S(1)} %get-tuple-element.40.totals), custom_call_target="tpu_custom_call" | custom-call | flops 2147483648 | bytes 8388608 | tf_op jit(solution)/shard_map/place/pallas_call | solution.py:395
  68.9 1.7 %collective-permute-start.10 = (f32[2,2,384,128]{3,2,1,0:T(8,128)S(1)}, f32[2,2,384,128]{3,2,1,0:T(8,128)}, u32[]{:S(2)}, u32[]{:S(2)}) collective-permute-start(f32[2,2,384,128]{3,2,1,0:T(8,128)S(1)} %get-tuple-element.46), channel_id=1, source_target_pairs={{0,1},{1,2},{2,3},{3,4},{4,5},{5,6},{6,7},{7,8},{8,9},{9,10},{10,1... | collective-permute-start | bytes 2359304 | tf_op jit(solution)/shard_map/ppermute | solution.py:412
  71.7 3.7 %all-to-all-start = ((f32[16,64,256]{2,1,0:T(8,128)}), f32[16,64,256]{2,1,0:T(8,128)S(1)}, u32[]{:S(2)}, u32[]{:S(2)}) async-start(f32[16,64,256]{2,1,0:T(8,128)} %bitcast.3), calls=%async_computation | async-start | bytes 2097152 | tf_op jit(solution)/shard_map/all_to_all | solution.py:416
  75.4 5.3 %collective-permute-done.9 = f32[2,2,384,128]{3,2,1,0:T(8,128)} collective-permute-done((f32[2,2,384,128]{3,2,1,0:T(8,128)S(1)}, f32[2,2,384,128]{3,2,1,0:T(8,128)}, u32[]{:S(2)}, u32[]{:S(2)}) %collective-permute-start.9) | collective-permute-done | bytes 786464 | tf_op jit(solution)/shard_map/ppermute | solution.py:412
  82.3 4.8 %collective-permute-start.11 = (f32[2,2,128,128]{3,2,1,0:T(8,128)S(1)}, f32[2,2,128,128]{3,2,1,0:T(8,128)S(1)}, u32[]{:S(2)}, u32[]{:S(2)}) collective-permute-start(f32[2,2,128,128]{3,2,1,0:T(8,128)S(1)} %get-tuple-element.53), channel_id=1, source_target_pairs={{0,240},{16,0},{32,16},{48,32},{64,48},{80,64},{96,80},{112,96},{1... | collective-permute-start | bytes 786440 | tf_op jit(solution)/shard_map/ppermute | solution.py:412
  87.1 6.9 %all-to-all-done = f32[16,64,256]{2,1,0:T(8,128)S(1)} async-done(((f32[16,64,256]{2,1,0:T(8,128)}), f32[16,64,256]{2,1,0:T(8,128)S(1)}, u32[]{:S(2)}, u32[]{:S(2)}) %all-to-all-start) | async-done | bytes 1048608 | tf_op jit(solution)/shard_map/all_to_all | solution.py:416
  93.9 4.7 %collective-permute-done.12 = f32[2,2,128,128]{3,2,1,0:T(8,128)S(1)} collective-permute-done((f32[2,2,128,128]{3,2,1,0:T(8,128)S(1)}, f32[2,2,128,128]{3,2,1,0:T(8,128)S(1)}, u32[]{:S(2)}, u32[]{:S(2)}) %collective-permute-start.12) | collective-permute-done | bytes 262176 | tf_op jit(solution)/shard_map/ppermute | solution.py:412
  98.9 2.7 %collective-permute-done.13 = f32[32,256]{1,0:T(8,128)S(1)} collective-permute-done((f32[32,256]{1,0:T(8,128)S(1)}, f32[32,256]{1,0:T(8,128)S(1)}, u32[]{:S(2)}, u32[]{:S(2)}) %collective-permute-start.13) | collective-permute-done | bytes 32800 | tf_op jit(solution)/shard_map/ppermute | solution.py:484
  101.6 3.7 %collective-permute-done.14 = f32[32,256]{1,0:T(8,128)S(1)} collective-permute-done((f32[32,256]{1,0:T(8,128)S(1)}, f32[32,256]{1,0:T(8,128)S(1)}, u32[]{:S(2)}, u32[]{:S(2)}) %collective-permute-start.14) | collective-permute-done | bytes 32800 | tf_op jit(solution)/shard_map/ppermute | solution.py:484
  105.4 1.6 %collective-permute-start.15 = (f32[32,256]{1,0:T(8,128)S(1)}, f32[32,256]{1,0:T(8,128)S(1)}, u32[]{:S(2)}, u32[]{:S(2)}) collective-permute-start(f32[32,256]{1,0:T(8,128)S(1)} %add.62), channel_id=1, source_target_pairs={{0,8},{1,9},{2,10},{3,11},{4,12},{5,13},{6,14},{7,15},{8,0},{9,1},... | collective-permute-start | bytes 98312 | tf_op jit(solution)/shard_map/ppermute | solution.py:484
  107.0 5.0 %collective-permute-done.15 = f32[32,256]{1,0:T(8,128)S(1)} collective-permute-done((f32[32,256]{1,0:T(8,128)S(1)}, f32[32,256]{1,0:T(8,128)S(1)}, u32[]{:S(2)}, u32[]{:S(2)}) %collective-permute-start.15) | collective-permute-done | bytes 32800 | tf_op jit(solution)/shard_map/ppermute | solution.py:484
  112.2 19.5 %all_to_all.10 = f32[32,32,256]{2,1,0:T(8,128)S(1)} all-to-all(f32[32,32,256]{2,1,0:T(8,128)S(1)} %broadcast_in_dim.40), channel_id=1, replica_groups={{0,2,16,18,32,34,48,50,64,66,80,82,96,98,112,114,128,130,144,146,160,16..., dimensions={0} | all-to-all | bytes 2097152 | tf_op jit(solution)/shard_map/all_to_all | solution.py:416
  131.6 2.9 %collective-permute-start.16 = (f32[32,32,256]{2,1,0:T(8,128)S(1)}, f32[32,32,256]{2,1,0:T(8,128)S(1)}, u32[]{:S(2)}, u32[]{:S(2)}) collective-permute-start(f32[32,32,256]{2,1,0:T(8,128)S(1)} %all_to_all.10), channel_id=1, source_target_pairs={{0,1},{1,0},{2,3},{3,2},{4,5},{5,4},{6,7},{7,6},{8,9},{9,8},{10,11... | collective-permute-start | bytes 3145736 | tf_op jit(solution)/shard_map/ppermute | solution.py:424
  135.2 1.5 %collective-permute-done.16 = f32[32,32,256]{2,1,0:T(8,128)S(1)} collective-permute-done((f32[32,32,256]{2,1,0:T(8,128)S(1)}, f32[32,32,256]{2,1,0:T(8,128)S(1)}, u32[]{:S(2)}, u32[]{:S(2)}) %collective-permute-start.16) | collective-permute-done | bytes 1048608 | tf_op jit(solution)/shard_map/ppermute | solution.py:424
  136.8 1.6 %broadcast_select_fusion = f32[2,4,256,256]{3,2,1,0:T(8,128)} fusion(f32[4,256,256]{2,1,0:T(8,128)S(1)} %bitcast.12, f32[4,256,256]{2,1,0:T(8,128)S(1)} %bitcast.11, pred[2]{0:T(512)(128)(4,1)S(1)} %iota_compare_fusion), kind=kLoop, calls=%fused_computation | loop fusion | flops 524288 | bytes 4194306 | tf_op jit(solution)/shard_map/jit(_where)/select_n | solution.py:499
  (43 shorter events, 7.4 us)
Async XLA Ops:
  0.6 18.6 %collective-permute-start.2 = (f32[2,2,128,128]{3,2,1,0:T(8,128)}, f32[2,2,128,128]{3,2,1,0:T(8,128)S(1)}, u32[]{:S(2)}, u32[]{:S(2)}) collective-permute-start(f32[2,2,128,128]{3,2,1,0:T(8,128)} %middle.1), channel_id=1, source_target_pairs={{0,1},{1,2},{2,3},{3,4},{4,5},{5,6},{6,7},{7,8},{8,9},{9,10},{10,1... | collective-permute-start | bytes 786440 | tf_op jit(solution)/shard_map/ppermute | solution.py:412
  3.7 15.6 %collective-permute-start.1 = (f32[2,2,128,128]{3,2,1,0:T(8,128)}, f32[2,2,128,128]{3,2,1,0:T(8,128)S(1)}, u32[]{:S(2)}, u32[]{:S(2)}) collective-permute-start(f32[2,2,128,128]{3,2,1,0:T(8,128)} %middle.1), channel_id=1, source_target_pairs={{0,240},{16,0},{32,16},{48,32},{64,48},{80,64},{96,80},{112,96},{1... | collective-permute-start | bytes 786440 | tf_op jit(solution)/shard_map/ppermute | solution.py:412
  8.6 10.9 %collective-permute-start = (f32[2,2,128,128]{3,2,1,0:T(8,128)}, f32[2,2,128,128]{3,2,1,0:T(8,128)S(1)}, u32[]{:S(2)}, u32[]{:S(2)}) collective-permute-start(f32[2,2,128,128]{3,2,1,0:T(8,128)} %middle.1), channel_id=1, source_target_pairs={{0,16},{16,32},{32,48},{48,64},{64,80},{80,96},{96,112},{112,128},... | collective-permute-start | bytes 786440 | tf_op jit(solution)/shard_map/ppermute | solution.py:412
  8.6 10.9 %collective-permute-start.3 = (f32[2,2,128,128]{3,2,1,0:T(8,128)}, f32[2,2,128,128]{3,2,1,0:T(8,128)S(1)}, u32[]{:S(2)}, u32[]{:S(2)}) collective-permute-start(f32[2,2,128,128]{3,2,1,0:T(8,128)} %middle.1), channel_id=1, source_target_pairs={{0,15},{1,0},{2,1},{3,2},{4,3},{5,4},{6,5},{7,6},{8,7},{9,8},{10,9... | collective-permute-start | bytes 786440 | tf_op jit(solution)/shard_map/ppermute | solution.py:412
  9.4 9.9 %collective-permute-start.4 = (s32[2,2]{1,0:T(2,128)S(1)}, s32[2,2]{1,0:T(2,128)S(1)}, u32[]{:S(2)}, u32[]{:S(2)}) collective-permute-start(s32[2,2]{1,0:T(2,128)S(1)} %and_select_fusion), channel_id=1, source_target_pairs={{0,17},{1,18},{2,19},{3,20},{4,21},{5,22},{6,23},{7,24},{8,25},{9,... | collective-permute-start | bytes 56 | tf_op jit(solution)/shard_map/ppermute | solution.py:441
  19.5 8.9 %collective-permute-start.6 = (f32[2,2,256,128]{3,2,1,0:T(8,128)S(1)}, f32[2,2,256,128]{3,2,1,0:T(8,128)S(1)}, u32[]{:S(2)}, u32[]{:S(2)}) collective-permute-start(f32[2,2,256,128]{3,2,1,0:T(8,128)S(1)} %constant_dynamic-update-slice_fusion.middle_edges), channel_id=1, source_target_pairs={{0,15},{1,0},{2,1},{3,2},{4,3},{5,4},{6,5},{7,6},{8,7},{9,8},{10,9... | collective-permute-start | bytes 1572872 | tf_op jit(solution)/shard_map/ppermute | solution.py:412
  21.7 6.7 %collective-permute-start.5 = (f32[2,2,256,128]{3,2,1,0:T(8,128)S(1)}, f32[2,2,256,128]{3,2,1,0:T(8,128)S(1)}, u32[]{:S(2)}, u32[]{:S(2)}) collective-permute-start(f32[2,2,256,128]{3,2,1,0:T(8,128)S(1)} %constant_dynamic-update-slice_fusion.middle_edges), channel_id=1, source_target_pairs={{0,1},{1,2},{2,3},{3,4},{4,5},{5,6},{6,7},{7,8},{8,9},{9,10},{10,1... | collective-permute-start | bytes 1572872 | tf_op jit(solution)/shard_map/ppermute | solution.py:412
  21.8 1.6 %copy-start = (f32[2,4,256,256]{3,2,1,0:T(8,128)S(1)}, f32[2,4,256,256]{3,2,1,0:T(8,128)}, u32[]{:S(2)}) copy-start(f32[2,4,256,256]{3,2,1,0:T(8,128)} %probe_in.1) | copy-start | bytes 6291460
  23.3 1.0 copy-start.3
  24.4 1.4 %copy-start.4 = (f32[2,256,256]{2,1,0:T(8,128)S(1)}, f32[2,256,256]{2,1,0:T(8,128)}, u32[]{:S(2)}) copy-start(f32[2,256,256]{2,1,0:T(8,128)} %param.10) | copy-start | bytes 1572868
  24.4 4.1 %copy-start.1 = (f32[2,2,128,128]{3,2,1,0:T(8,128)S(1)}, f32[2,2,128,128]{3,2,1,0:T(8,128)}, u32[]{:S(2)}) copy-start(f32[2,2,128,128]{3,2,1,0:T(8,128)} %middle.1) | copy-start | bytes 786436
  24.4 4.1 %copy-start.2 = (f32[2,256,256]{2,1,0:T(8,128)S(1)}, f32[2,256,256]{2,1,0:T(8,128)}, u32[]{:S(2)}) copy-start(f32[2,256,256]{2,1,0:T(8,128)} %constant.62.clone.phase) | copy-start | bytes 1572868
  25.8 17.7 %collective-permute-start.7 = (f32[2,256,256]{2,1,0:T(8,128)S(1)}, f32[2,256,256]{2,1,0:T(8,128)S(1)}, u32[]{:S(2)}, u32[]{:S(2)}) collective-permute-start(f32[2,256,256]{2,1,0:T(8,128)S(1)} %copy-done.4), channel_id=1, source_target_pairs={{0,17},{1,18},{2,19},{3,20},{4,21},{5,22},{6,23},{7,24},{8,25},{9,... | collective-permute-start | bytes 1572872 | tf_op jit(solution)/shard_map/ppermute | solution.py:453
  59.3 9.5 %collective-permute-start.8 = (f32[4,256,256]{2,1,0:T(8,128)S(1)}, f32[4,256,256]{2,1,0:T(8,128)S(1)}, u32[]{:S(2)}, u32[]{:S(2)}) collective-permute-start(f32[4,256,256]{2,1,0:T(8,128)S(1)} %get-tuple-element.39), channel_id=1, source_target_pairs={{0,1},{1,0},{2,3},{3,2},{4,5},{5,4},{6,7},{7,6},{8,9},{9,8},{10,11... | collective-permute-start | bytes 3145736 | tf_op jit(solution)/shard_map/ppermute | solution.py:424
  68.8 11.8 %collective-permute-start.9 = (f32[2,2,384,128]{3,2,1,0:T(8,128)S(1)}, f32[2,2,384,128]{3,2,1,0:T(8,128)}, u32[]{:S(2)}, u32[]{:S(2)}) collective-permute-start(f32[2,2,384,128]{3,2,1,0:T(8,128)S(1)} %get-tuple-element.45), channel_id=1, source_target_pairs={{0,15},{1,0},{2,1},{3,2},{4,3},{5,4},{6,5},{7,6},{8,7},{9,8},{10,9... | collective-permute-start | bytes 2359304 | tf_op jit(solution)/shard_map/ppermute | solution.py:412
  68.9 11.8 %collective-permute-start.10 = (f32[2,2,384,128]{3,2,1,0:T(8,128)S(1)}, f32[2,2,384,128]{3,2,1,0:T(8,128)}, u32[]{:S(2)}, u32[]{:S(2)}) collective-permute-start(f32[2,2,384,128]{3,2,1,0:T(8,128)S(1)} %get-tuple-element.46), channel_id=1, source_target_pairs={{0,1},{1,2},{2,3},{3,4},{4,5},{5,6},{6,7},{7,8},{8,9},{9,10},{10,1... | collective-permute-start | bytes 2359304 | tf_op jit(solution)/shard_map/ppermute | solution.py:412
  71.7 22.2 %all-to-all-start = ((f32[16,64,256]{2,1,0:T(8,128)}), f32[16,64,256]{2,1,0:T(8,128)S(1)}, u32[]{:S(2)}, u32[]{:S(2)}) async-start(f32[16,64,256]{2,1,0:T(8,128)} %bitcast.3), calls=%async_computation | async-start | bytes 2097152 | tf_op jit(solution)/shard_map/all_to_all | solution.py:416
  82.2 16.5 %collective-permute-start.12 = (f32[2,2,128,128]{3,2,1,0:T(8,128)S(1)}, f32[2,2,128,128]{3,2,1,0:T(8,128)S(1)}, u32[]{:S(2)}, u32[]{:S(2)}) collective-permute-start(f32[2,2,128,128]{3,2,1,0:T(8,128)S(1)} %get-tuple-element.52), channel_id=1, source_target_pairs={{0,16},{16,32},{32,48},{48,64},{64,80},{80,96},{96,112},{112,128},... | collective-permute-start | bytes 786440 | tf_op jit(solution)/shard_map/ppermute | solution.py:412
  82.3 16.4 %collective-permute-start.11 = (f32[2,2,128,128]{3,2,1,0:T(8,128)S(1)}, f32[2,2,128,128]{3,2,1,0:T(8,128)S(1)}, u32[]{:S(2)}, u32[]{:S(2)}) collective-permute-start(f32[2,2,128,128]{3,2,1,0:T(8,128)S(1)} %get-tuple-element.53), channel_id=1, source_target_pairs={{0,240},{16,0},{32,16},{48,32},{64,48},{80,64},{96,80},{112,96},{1... | collective-permute-start | bytes 786440 | tf_op jit(solution)/shard_map/ppermute | solution.py:412
  98.8 2.9 %collective-permute-start.13 = (f32[32,256]{1,0:T(8,128)S(1)}, f32[32,256]{1,0:T(8,128)S(1)}, u32[]{:S(2)}, u32[]{:S(2)}) collective-permute-start(f32[32,256]{1,0:T(8,128)S(1)} %dynamic-slice_bitcast_fusion), channel_id=1, source_target_pairs={{0,2},{1,3},{2,0},{3,1},{4,6},{5,7},{6,4},{7,5},{8,10},{9,11},{10,... | collective-permute-start | bytes 98312 | tf_op jit(solution)/shard_map/ppermute | solution.py:484
  101.6 3.7 %collective-permute-start.14 = (f32[32,256]{1,0:T(8,128)S(1)}, f32[32,256]{1,0:T(8,128)S(1)}, u32[]{:S(2)}, u32[]{:S(2)}) collective-permute-start(f32[32,256]{1,0:T(8,128)S(1)} %bitcast_add_fusion), channel_id=1, source_target_pairs={{0,4},{1,5},{2,6},{3,7},{4,0},{5,1},{6,2},{7,3},{8,12},{9,13},{10,... | collective-permute-start | bytes 98312 | tf_op jit(solution)/shard_map/ppermute | solution.py:484
  105.4 6.7 %collective-permute-start.15 = (f32[32,256]{1,0:T(8,128)S(1)}, f32[32,256]{1,0:T(8,128)S(1)}, u32[]{:S(2)}, u32[]{:S(2)}) collective-permute-start(f32[32,256]{1,0:T(8,128)S(1)} %add.62), channel_id=1, source_target_pairs={{0,8},{1,9},{2,10},{3,11},{4,12},{5,13},{6,14},{7,15},{8,0},{9,1},... | collective-permute-start | bytes 98312 | tf_op jit(solution)/shard_map/ppermute | solution.py:484
  131.6 5.2 %collective-permute-start.16 = (f32[32,32,256]{2,1,0:T(8,128)S(1)}, f32[32,32,256]{2,1,0:T(8,128)S(1)}, u32[]{:S(2)}, u32[]{:S(2)}) collective-permute-start(f32[32,32,256]{2,1,0:T(8,128)S(1)} %all_to_all.10), channel_id=1, source_target_pairs={{0,1},{1,0},{2,3},{3,2},{4,5},{5,4},{6,7},{7,6},{8,9},{9,8},{10,11... | collective-permute-start | bytes 3145736 | tf_op jit(solution)/shard_map/ppermute | solution.py:424

commit v4 on v3

--- a/solution.py
+++ b/solution.py
@@ -10,6 +10,7 @@
 FRESNEL = 0.5
 BF, F32 = jnp.bfloat16, jnp.float32
 FOUR, FOUR_CONJ, PROP, PROP_CONJ = 0, 1, 2, 3
+CHUNK = 1
 VMEM = pl.BlockSpec(memory_space=pltpu.VMEM)
 SMEM = pl.BlockSpec(memory_space=pltpu.SMEM)
 ANY = pl.BlockSpec(memory_space=pl.ANY)
@@ -88,44 +89,79 @@
 def sandwich(fields, which, tables, lhs_high, lhs_low, rhs_high, rhs_low):
     n = tables.shape[-1]
     h = n // 2
-    for at, field in enumerate(fields):
-        for part in range(2):
-            first, second = field[part][:, :h], field[part][:, h:]
-            for parity, value in enumerate((first + second, first - second)):
-                high, low = halves(value)
-                lhs_high[parity, at * n : (at + 1) * n, part * h : (part + 1) * h] = high
-                lhs_low[parity, at * n : (at + 1) * n, part * h : (part + 1) * h] = low
-    for parity in range(2):
-        inner = product(
-            lhs_high[parity], lhs_low[parity], tables[which, parity, 0], tables[which, parity, 1]
-        )
-        for at in range(len(fields)):
-            first = inner[at * n : at * n + h]
-            second = inner[at * n + h : (at + 1) * n]
-            cols = slice(at * n + parity * h, at * n + (parity + 1) * h)
-            for turned, value in enumerate((first + second, first - second)):
-                high, low = halves(value)
-                rhs_high[turned, :h, cols] = high[:, :h]
-                rhs_high[turned, h:, cols] = high[:, h:]
-                rhs_low[turned, :h, cols] = low[:, :h]
-                rhs_low[turned, h:, cols] = low[:, h:]
-    even, odd = [
-        product(
-            tables[which ^ 1, turned, 0], tables[which ^ 1, turned, 1],
-            rhs_high[turned], rhs_low[turned],
-        )
-        for turned in range(2)
-    ]
+    chunks = [range(at, at + CHUNK) for at in range(0, len(fields), CHUNK)]
+
+    def split(chunk):
+        for at in chunk:
+            for part in range(2):
+                first, second = fields[at][part][:, :h], fields[at][part][:, h:]
+                for parity, value in enumerate((first + second, first - second)):
+                    high, low = halves(value)
+                    lhs_high[parity, at * n : (at + 1) * n, part * h : (part + 1) * h] = high
+                    lhs_low[parity, at * n : (at + 1) * n, part * h : (part + 1) * h] = low
+
+    def inner(chunk):
+        span = slice(chunk[0] * n, (chunk[-1] + 1) * n)
+        return [
+            product(
+                lhs_high[parity, span], lhs_low[parity, span],
+                tables[which, parity, 0], tables[which, parity, 1],
+            )
+            for parity in range(2)
+        ]
+
+    def turn(chunk, values):
+        for parity, value in enumerate(values):
+            for at in chunk:
+                base = (at - chunk[0]) * n
+                first, second = value[base : base + h], value[base + h : base + n]
+                cols = slice(at * n + parity * h, at * n + (parity + 1) * h)
+                for turned, mixed in enumerate((first + second, first - second)):
+                    high, low = halves(mixed)
+                    rhs_high[turned, :h, cols] = high[:, :h]
+                    rhs_high[turned, h:, cols] = high[:, h:]
+                    rhs_low[turned, :h, cols] = low[:, :h]
+                    rhs_low[turned, h:, cols] = low[:, h:]
+
+    def outer(chunk):
+        span = slice(chunk[0] * n, (chunk[-1] + 1) * n)
+        return [
+            product(
+                tables[which ^ 1, turned, 0], tables[which ^ 1, turned, 1],
+                rhs_high[turned, :, span], rhs_low[turned, :, span],
+            )
+            for turned in range(2)
+        ]
+
+    def joined(chunk, values):
+        results = []
+        for at in chunk:
+            base = (at - chunk[0]) * n
+            pair = []
+            for part in range(2):
+                e = values[0][part * h : (part + 1) * h, base : base + n]
+                o = values[1][part * h : (part + 1) * h, base : base + n]
+                value = jnp.concatenate([e + o, e - o], axis=0)
+                first, second = value[:, :h], value[:, h:]
+                pair.append(jnp.concatenate([first + second, first - second], axis=1))
+            results.append(pair)
+        return results
+
     results = []
-    for at in range(len(fields)):
-        pair = []
-        for part in range(2):
-            e = even[part * h : (part + 1) * h, at * n : (at + 1) * n]
-            o = odd[part * h : (part + 1) * h, at * n : (at + 1) * n]
-            value = jnp.concatenate([e + o, e - o], axis=0)
-            first, second = value[:, :h], value[:, h:]
-            pair.append(jnp.concatenate([first + second, first - second], axis=1))
-        results.append(pair)
+    middle, last = {}, {}
+    steps = len(chunks)
+    split(chunks[0])
+    for at in range(steps):
+        middle[at] = inner(chunks[at])
+        if at + 1 < steps:
+            split(chunks[at + 1])
+        if at > 0:
+            last[at - 1] = outer(chunks[at - 1])
+        turn(chunks[at], middle[at])
+        if at > 0:
+            results += joined(chunks[at - 1], last[at - 1])
+    last[steps - 1] = outer(chunks[steps - 1])
+    results += joined(chunks[steps - 1], last[steps - 1])
     return results
 
 
@@ -178,9 +214,9 @@
 
 
 def forward_kernel(
-    offsets, left, left_edges, middle, middle_edges, right, right_edges, probe, tables, phase,
-    window, moved, far, intensity,
-    lhs_high, lhs_low, rhs_high, rhs_low, wide, sems,
+    left, left_edges, middle, middle_edges, right, right_edges, probe, tables, phase,
+    window, moved, far, intensity, offsets,
+    lhs_high, lhs_low, rhs_high, rhs_low, wide, numbers, sems,
 ):
     n, modes = probe.shape[-1], probe.shape[1]
     rows, tile = wide.shape[2], wide.shape[3] // 3
@@ -188,16 +224,22 @@
     for across, (own, edges) in enumerate(
         ((left, left_edges), (middle, middle_edges), (right, right_edges))
     ):
-        sources = (edges.at[:, :, :tile], own, edges.at[:, :, tile:])
+        sources = (edges.at[:, :, :tile], own, edges.at[:, :, tile + 8 :])
         for down, source in enumerate(sources):
             place = wide.at[
                 :, :, down * tile : (down + 1) * tile, across * tile : (across + 1) * tile
             ]
             pieces.append(pltpu.make_async_copy(source, place, sems.at[len(pieces)]))
+    pieces.append(
+        pltpu.make_async_copy(left_edges.at[:, :, tile : tile + 8], numbers, sems.at[len(pieces)])
+    )
     for piece in pieces:
         piece.start()
     for piece in pieces:
         piece.wait()
+    for position in range(window.shape[0]):
+        for axis in range(2):
+            offsets[position, axis] = numbers[position, axis, 0, 0].astype(jnp.int32)
     buffers = (tables, lhs_high, lhs_low, rhs_high, rhs_low)
 
     def visit(position, carry):
@@ -237,7 +279,7 @@
     lax.fori_loop(0, window.shape[0], visit, 0)
 
 
-def forward(count, offsets, tiles, probe, tables, phase):
+def forward(count, tiles, probe, tables, phase):
     n, modes = probe.shape[-1], probe.shape[1]
     tile = tiles[0].shape[-1]
     fields = jax.ShapeDtypeStruct((count,) + probe.shape, F32)
@@ -248,17 +290,22 @@
             fields,
             fields,
             jax.ShapeDtypeStruct((count, n, n), F32),
+            jax.ShapeDtypeStruct((count, 2), jnp.int32),
         ),
-        in_specs=[SMEM] + [ANY] * 6 + [VMEM] * 3,
-        out_specs=(VMEM,) * 4,
+        in_specs=[ANY] * 6 + [VMEM] * 3,
+        out_specs=(VMEM,) * 4 + (SMEM,),
         scratch_shapes=sandwich_scratch(n, modes)
-        + [pltpu.VMEM((2, 2, 3 * tile, 3 * tile), F32), pltpu.SemaphoreType.DMA((9,))],
+        + [
+            pltpu.VMEM((2, 2, 3 * tile, 3 * tile), F32),
+            pltpu.SMEM((2, 2, 8, tile), F32),
+            pltpu.SemaphoreType.DMA((10,)),
+        ],
         compiler_params=pltpu.CompilerParams(vmem_limit_bytes=SCOPED_F << 20),
         cost_estimate=pl.CostEstimate(
             flops=count * modes * 8 * 12 * n**3, bytes_accessed=18 << 20, transcendentals=0
         ),
         name="forward",
-    )(offsets, *tiles, probe, tables, phase)
+    )(*tiles, probe, tables, phase)
 
 
 def backward_kernel(
@@ -438,13 +485,16 @@
     ]
     corner = jnp.stack([lax.axis_index("strip"), lax.axis_index("tile")]).astype(jnp.int32) * tile
     wrap = jnp.array([strips * tile, tiles * tile], jnp.int32)
-    scalars = lax.ppermute((offsets - corner) % wrap, both, diagonal)
-    above = around(object_field, "strip", 1)
+    local = ((offsets - corner) % wrap).astype(F32)[:, :, None, None]
+    sent_down = jnp.concatenate(
+        [object_field, jnp.broadcast_to(local, local.shape[:2] + (8, tile))], axis=2
+    )
+    above = around(sent_down, "strip", 1)
     below = around(object_field, "strip", -1)
     left = around(object_field, "tile", 1)
     right = around(object_field, "tile", -1)
-    above, below, left, right, scalars, measured = lax.optimization_barrier(
-        (above, below, left, right, scalars, measured)
+    above, below, left, right, measured = lax.optimization_barrier(
+        (above, below, left, right, measured)
     )
     probe, tables = prepared(probe_modes, jnp.asarray(blocks))
     edges = jnp.concatenate([above, below], axis=2)
@@ -452,7 +502,7 @@
     right_edges = around(edges, "tile", -1)
     measured = lax.ppermute(measured, both, diagonal)
     pieces = (left, left_edges, object_field, edges, right, right_edges)
-    state = forward(measured.shape[0], scalars, pieces, probe, tables, phase)
+    *state, scalars = forward(measured.shape[0], pieces, probe, tables, phase)
     core = (lax.axis_index("tile") % 2).astype(jnp.int32)
     totals, kept, sent = backward(core.reshape(1), state, measured, probe, tables, phase)
 
@@ -463,19 +513,17 @@
         for c in range(cores)
         for group in range(levels // pairs)
     ]
-    received = swapped(sent)
+    part = (kept + swapped(sent)).reshape(strips, -1, n)
+    part, totals = lax.optimization_barrier((part, totals))
+    shares = exchanged(part, "strip")
     grad_left, grad_middle, grad_right = placed(scalars, totals, 3 * tile, tile)
-    received, grad_left, grad_middle, grad_right = lax.optimization_barrier(
-        (received, grad_left, grad_middle, grad_right)
-    )
     from_right = around(grad_left, "tile", -1)
     from_left = around(grad_right, "tile", 1)
-    shares = exchanged((kept + received).reshape(strips, -1, n), "strip")
+    shares, from_right, from_left = lax.optimization_barrier((shares, from_right, from_left))
     column = grad_middle + from_right + from_left
     upper, lower = column[:, :, :tile], column[:, :, 2 * tile :]
     from_below = around(upper, "strip", -1)
     from_above = around(lower, "strip", 1)
-    shares, from_below, from_above = lax.optimization_barrier((shares, from_below, from_above))
 
     def across(value, distance):
         step = [
@@ -492,6 +540,7 @@
     while distance < levels:
         share = share + across(share, distance)
         distance *= 2
+    share, from_below, from_above = lax.optimization_barrier((share, from_below, from_above))
     object_grad = column[:, :, tile : 2 * tile] + from_below + from_above
     half = exchanged(copies(share, strips * pairs), both, groups)
     other = swapped(half)

time: 139 us -> 132 us (0.950)
  waiting for transfers between devices: 42.7 us -> 28.5 us
  starting transfers between devices: 31 us -> 40.7 us
  blocking collectives: 19.5 us -> 16.6 us
  Pallas kernels: 35.9 us -> 34.2 us
  local copies, waits for them, and re-layouts: 2.84 us -> 4.5 us
    ppermute x1 -> x0, waiting for transfers between devices: 9.85 us -> none  [per_device(): scalars = lax.ppermute((offsets - corner) % wrap, both, diagonal)]
    ppermute x3, waiting for transfers between devices: 11.5 us -> 4.44 us  [across(): return lax.ppermute(value, 'tile', step)]
    all_to_all x1, waiting for transfers between devices: 6.87 us -> 0.01 us  [exchanged(): lax.all_to_all(value, axis, 0, 0, tiled=True, axis_index_groups=groups)]
    ppermute x10, waiting for transfers between devices: 12.9 us -> 18.6 us  [around(): lax.ppermute(value, axis, [(at, (at + steps) % count) for at in range(cou...]
    ppermute x3, starting transfers between devices: 1.72 us -> 6.59 us  [across(): return lax.ppermute(value, 'tile', step)]
    ppermute x2, starting transfers between devices: 8.74 us -> 11.9 us  [swapped(): lax.ppermute(value, 'tile', [(at, at ^ 1) for at in range(lax.axis_size('...]
    all_to_all x1, blocking collectives: 19.5 us -> 16.6 us  [exchanged(): lax.all_to_all(value, axis, 0, 0, tiled=True, axis_index_groups=groups)]
    ppermute x2, waiting for transfers between devices: 1.54 us -> 3.81 us  [swapped(): lax.ppermute(value, 'tile', [(at, at ^ 1) for at in range(lax.axis_size('...]
  transfers between devices with their start and end apart: 18 -> 17, of which waited for: 10 -> 9; matrix products, arithmetic and copies ran while one was open for 3% -> 2% of each run, Pallas kernels for 14% -> 15%
where the time goes in v4:
time: 132 us
  starting transfers between devices  40.7 us (31%)
  Pallas kernels  34.2 us (26%)
  waiting for transfers between devices  28.5 us (22%)
  blocking collectives  16.6 us (13%)
  other arithmetic  6.81 us (5%)
  local copies, waits for them, and re-layouts  4.5 us (3%)
    ppermute x10, waiting for transfers between devices, around(): lax.ppermute(value, axis, [(at, (at + steps) % count) for at in range(cou...  18.6 us
    ppermute x10, starting transfers between devices, around(): lax.ppermute(value, axis, [(at, (at + steps) % count) for at in range(cou...  17.3 us
    all_to_all x1, blocking collectives, exchanged(): lax.all_to_all(value, axis, 0, 0, tiled=True, axis_index_groups=groups)  16.6 us
    pallas_call x1, Pallas kernels, backward(): pl.pallas_call(backward_kernel, out_shape=(jax.ShapeDtypeStruct((count, 2...  14.9 us
    pallas_call x1, Pallas kernels, forward(): pl.pallas_call(forward_kernel, out_shape=(jax.ShapeDtypeStruct((count, 2,...  14.2 us
    ppermute x2, starting transfers between devices, swapped(): lax.ppermute(value, 'tile', [(at, at ^ 1) for at in range(lax.axis_size('...  11.9 us
    ppermute x3, starting transfers between devices, across(): return lax.ppermute(value, 'tile', step)  6.59 us
    all_to_all x1, starting transfers between devices, exchanged(): lax.all_to_all(value, axis, 0, 0, tiled=True, axis_index_groups=groups)  4.84 us
  transfers between devices with their start and end apart: 17, of which 9 were waited for; matrix products, arithmetic and copies ran while one was open for 2% of the time, Pallas kernels for 15%

profile of v4, /device:TPU:1, one launch (start us, length us, event | category | flops | bytes accessed | tf_op | source)
XLA Modules:
  0.0 132.0 jit_solution(13972521497770548930)
XLA Ops:
  2.4 2.2 %collective-permute-start = (f32[2,2,136,128]{3,2,1,0:T(8,128)S(1)}, f32[2,2,136,128]{3,2,1,0:T(8,128)S(1)}, u32[]{:S(2)}, u32[]{:S(2)}) collective-permute-start(f32[2,2,136,128]{3,2,1,0:T(8,128)S(1)} %pad_maximum_fusion), channel_id=1, source_target_pairs={{0,16},{16,32},{32,48},{48,64},{64,80},{80,96},{96,112},{112,128},... | collective-permute-start | bytes 835592 | tf_op jit(solution)/shard_map/ppermute | solution.py:459
  4.7 2.5 %collective-permute-start.2 = (f32[2,2,128,128]{3,2,1,0:T(8,128)}, f32[2,2,128,128]{3,2,1,0:T(8,128)S(1)}, u32[]{:S(2)}, u32[]{:S(2)}) collective-permute-start(f32[2,2,128,128]{3,2,1,0:T(8,128)} %middle.1), channel_id=1, source_target_pairs={{0,1},{1,2},{2,3},{3,4},{4,5},{5,6},{6,7},{7,8},{8,9},{9,10},{10,1... | collective-permute-start | bytes 786440 | tf_op jit(solution)/shard_map/ppermute | solution.py:459
  7.1 3.5 %collective-permute-start.1 = (f32[2,2,128,128]{3,2,1,0:T(8,128)}, f32[2,2,128,128]{3,2,1,0:T(8,128)S(1)}, u32[]{:S(2)}, u32[]{:S(2)}) collective-permute-start(f32[2,2,128,128]{3,2,1,0:T(8,128)} %middle.1), channel_id=1, source_target_pairs={{0,240},{16,0},{32,16},{48,32},{64,48},{80,64},{96,80},{112,96},{1... | collective-permute-start | bytes 786440 | tf_op jit(solution)/shard_map/ppermute | solution.py:459
  11.1 5.3 %collective-permute-done.1 = f32[2,2,128,128]{3,2,1,0:T(8,128)S(1)} collective-permute-done((f32[2,2,128,128]{3,2,1,0:T(8,128)}, f32[2,2,128,128]{3,2,1,0:T(8,128)S(1)}, u32[]{:S(2)}, u32[]{:S(2)}) %collective-permute-start.1) | collective-permute-done | bytes 262176 | tf_op jit(solution)/shard_map/ppermute | solution.py:459
  16.7 2.0 %collective-permute-start.5 = (f32[2,2,264,128]{3,2,1,0:T(8,128)S(1)}, f32[2,2,264,128]{3,2,1,0:T(8,128)S(1)}, u32[]{:S(2)}, u32[]{:S(2)}) collective-permute-start(f32[2,2,264,128]{3,2,1,0:T(8,128)S(1)} %constant_dynamic-update-slice_fusion.middle_edges), channel_id=1, source_target_pairs={{0,15},{1,0},{2,1},{3,2},{4,3},{5,4},{6,5},{7,6},{8,7},{9,8},{10,9... | collective-permute-start | bytes 1622024 | tf_op jit(solution)/shard_map/ppermute | solution.py:459
  18.7 1.6 %copy-done.1 = f32[2,4,256,256]{3,2,1,0:T(8,128)S(1)} copy-done((f32[2,4,256,256]{3,2,1,0:T(8,128)S(1)}, f32[2,4,256,256]{3,2,1,0:T(8,128)}, u32[]{:S(2)}) %copy-start.1) | copy-done | bytes 2097176
  22.8 3.0 %collective-permute-done.5.right_edges = f32[2,2,264,128]{3,2,1,0:T(8,128)S(1)} collective-permute-done((f32[2,2,264,128]{3,2,1,0:T(8,128)S(1)}, f32[2,2,264,128]{3,2,1,0:T(8,128)S(1)}, u32[]{:S(2)}, u32[]{:S(2)}) %collective-permute-start.5) | collective-permute-done | bytes 540704 | tf_op jit(solution)/shard_map/ppermute | solution.py:459
  25.8 14.2 %forward.1 = (f32[2,2,2,256,256]{4,3,2,1,0:T(8,128)S(1)}, f32[2,2,4,256,256]{4,3,2,1,0:T(8,128)S(1)}, f32[2,2,4,256,256]{4,3,2,1,0:T(8,128)S(1)}, f32[2,256,256]{2,1,0:T(8,128)S(1)}, s32[2,2]{1,0:T(2,128)S(1)}) custom-call(f32[2,2,128,128]{3,2,1,0:T(8,128)S(1)} %collective-permute-done.2.left, f32[2,2,264,128]{3,2,1,0:T(8,128)S(1)} %collective-permute-done.4.left_edges, ...), custom_call_target="tpu_custom_call" | custom-call | flops 12884901888 | bytes 18874368 | tf_op jit(solution)/shard_map/forward/pallas_call | solution.py:286
  40.0 1.6 %collective-permute-done.6.measured = f32[2,256,256]{2,1,0:T(8,128)S(1)} collective-permute-done((f32[2,256,256]{2,1,0:T(8,128)S(1)}, f32[2,256,256]{2,1,0:T(8,128)S(1)}, u32[]{:S(2)}, u32[]{:S(2)}) %collective-permute-start.6) | collective-permute-done | bytes 524320 | tf_op jit(solution)/shard_map/ppermute | solution.py:503
  41.6 14.9 %backward.1 = (f32[2,2,2,256,256]{4,3,2,1,0:T(8,128)S(1)}, f32[4,256,256]{2,1,0:T(8,128)S(1)}, f32[4,256,256]{2,1,0:T(8,128)S(1)}) custom-call(s32[1]{0:T(128)} %bitcast.2.core, f32[2,2,2,256,256]{4,3,2,1,0:T(8,128)S(1)} %get-tuple-element.35.window, f32[2,2,4,256,256]{4,3,2,1,0:T(8,128)S(1)} %get-tuple-element.36.moved, ...), custom_call_target="tpu_custom_call" | custom-call | flops 12884901888 | bytes 18874368 | tf_op jit(solution)/shard_map/backward/pallas_call | solution.py:386
  56.6 4.3 %collective-permute-start.7 = (f32[4,256,256]{2,1,0:T(8,128)S(1)}, f32[4,256,256]{2,1,0:T(8,128)S(1)}, u32[]{:S(2)}, u32[]{:S(2)}) collective-permute-start(f32[4,256,256]{2,1,0:T(8,128)S(1)} %get-tuple-element.41), channel_id=1, source_target_pairs={{0,1},{1,0},{2,3},{3,2},{4,5},{5,4},{6,7},{7,6},{8,9},{9,8},{10,11... | collective-permute-start | bytes 3145736 | tf_op jit(solution)/shard_map/ppermute | solution.py:471
  60.9 2.3 %collective-permute-done.7 = f32[4,256,256]{2,1,0:T(8,128)S(1)} collective-permute-done((f32[4,256,256]{2,1,0:T(8,128)S(1)}, f32[4,256,256]{2,1,0:T(8,128)S(1)}, u32[]{:S(2)}, u32[]{:S(2)}) %collective-permute-start.7) | collective-permute-done | bytes 1048608 | tf_op jit(solution)/shard_map/ppermute | solution.py:471
  64.3 4.8 %all-to-all-start = ((f32[16,64,256]{2,1,0:T(8,128)}), f32[16,64,256]{2,1,0:T(8,128)S(1)}, u32[]{:S(2)}, u32[]{:S(2)}) async-start(f32[16,64,256]{2,1,0:T(8,128)} %bitcast.3), calls=%async_computation | async-start | bytes 2097152 | tf_op jit(solution)/shard_map/all_to_all | solution.py:463
  69.2 1.6 %copy-done.5 = f32[2,2,2,256,256]{4,3,2,1,0:T(8,128)S(1)} copy-done((f32[2,2,2,256,256]{4,3,2,1,0:T(8,128)S(1)}, f32[2,2,2,256,256]{4,3,2,1,0:T(8,128)}, u32[]{:S(2)}) %copy-start.5) | copy-done | bytes 2097176
  70.8 3.6 %place.1 = (f32[2,2,384,128]{3,2,1,0:T(8,128)S(1)}, f32[2,2,384,128]{3,2,1,0:T(8,128)S(1)}, f32[2,2,384,128]{3,2,1,0:T(8,128)S(1)}) custom-call(s32[2,2]{1,0:T(2,128)S(1)} %get-tuple-element.34.scalars, f32[2,2,2,256,256]{4,3,2,1,0:T(8,128)S(1)} %copy-done.5), custom_call_target="tpu_custom_call" | custom-call | flops 2147483648 | bytes 8388608 | tf_op jit(solution)/shard_map/place/pallas_call | solution.py:442
  76.2 10.1 %collective-permute-done.8 = f32[2,2,384,128]{3,2,1,0:T(8,128)} collective-permute-done((f32[2,2,384,128]{3,2,1,0:T(8,128)S(1)}, f32[2,2,384,128]{3,2,1,0:T(8,128)}, u32[]{:S(2)}, u32[]{:S(2)}) %collective-permute-start.8) | collective-permute-done | bytes 786464 | tf_op jit(solution)/shard_map/ppermute | solution.py:459
  89.4 3.4 %collective-permute-start.13 = (f32[2,2,128,128]{3,2,1,0:T(8,128)S(1)}, f32[2,2,128,128]{3,2,1,0:T(8,128)S(1)}, u32[]{:S(2)}, u32[]{:S(2)}) collective-permute-start(f32[2,2,128,128]{3,2,1,0:T(8,128)S(1)} %get-tuple-element.55), channel_id=1, source_target_pairs={{0,240},{16,0},{32,16},{48,32},{64,48},{80,64},{96,80},{112,96},{1... | collective-permute-start | bytes 786440 | tf_op jit(solution)/shard_map/ppermute | solution.py:459
  92.9 3.0 %collective-permute-start.11 = (f32[32,256]{1,0:T(8,128)S(1)}, f32[32,256]{1,0:T(8,128)S(1)}, u32[]{:S(2)}, u32[]{:S(2)}) collective-permute-start(f32[32,256]{1,0:T(8,128)S(1)} %bitcast_add_fusion), channel_id=1, source_target_pairs={{0,4},{1,5},{2,6},{3,7},{4,0},{5,1},{6,2},{7,3},{8,12},{9,13},{10,... | collective-permute-start | bytes 98312 | tf_op jit(solution)/shard_map/ppermute | solution.py:532
  97.1 3.5 %collective-permute-start.12 = (f32[32,256]{1,0:T(8,128)S(1)}, f32[32,256]{1,0:T(8,128)S(1)}, u32[]{:S(2)}, u32[]{:S(2)}) collective-permute-start(f32[32,256]{1,0:T(8,128)S(1)} %add.60), channel_id=1, source_target_pairs={{0,8},{1,9},{2,10},{3,11},{4,12},{5,13},{6,14},{7,15},{8,0},{9,1},... | collective-permute-start | bytes 98312 | tf_op jit(solution)/shard_map/ppermute | solution.py:532
  100.7 3.1 %collective-permute-done.12 = f32[32,256]{1,0:T(8,128)S(1)} collective-permute-done((f32[32,256]{1,0:T(8,128)S(1)}, f32[32,256]{1,0:T(8,128)S(1)}, u32[]{:S(2)}, u32[]{:S(2)}) %collective-permute-start.12) | collective-permute-done | bytes 32800 | tf_op jit(solution)/shard_map/ppermute | solution.py:532
  103.9 16.6 %all_to_all.10 = f32[32,32,256]{2,1,0:T(8,128)S(1)} all-to-all(f32[32,32,256]{2,1,0:T(8,128)S(1)} %broadcast_in_dim.47), channel_id=1, replica_groups={{0,2,16,18,32,34,48,50,64,66,80,82,96,98,112,114,128,130,144,146,160,16..., dimensions={0} | all-to-all | bytes 2097152 | tf_op jit(solution)/shard_map/all_to_all | solution.py:463
  120.5 7.6 %collective-permute-start.15 = (f32[32,32,256]{2,1,0:T(8,128)S(1)}, f32[32,32,256]{2,1,0:T(8,128)S(1)}, u32[]{:S(2)}, u32[]{:S(2)}) collective-permute-start(f32[32,32,256]{2,1,0:T(8,128)S(1)} %all_to_all.10), channel_id=1, source_target_pairs={{0,1},{1,0},{2,3},{3,2},{4,5},{5,4},{6,7},{7,6},{8,9},{9,8},{10,11... | collective-permute-start | bytes 3145736 | tf_op jit(solution)/shard_map/ppermute | solution.py:471
  128.8 1.5 %collective-permute-done.15 = f32[32,32,256]{2,1,0:T(8,128)S(1)} collective-permute-done((f32[32,32,256]{2,1,0:T(8,128)S(1)}, f32[32,32,256]{2,1,0:T(8,128)S(1)}, u32[]{:S(2)}, u32[]{:S(2)}) %collective-permute-start.15) | collective-permute-done | bytes 1048608 | tf_op jit(solution)/shard_map/ppermute | solution.py:471
  130.4 1.6 %broadcast_select_fusion = f32[2,4,256,256]{3,2,1,0:T(8,128)} fusion(f32[4,256,256]{2,1,0:T(8,128)S(1)} %bitcast.12, f32[4,256,256]{2,1,0:T(8,128)S(1)} %bitcast.11, pred[2]{0:T(512)(128)(4,1)S(1)} %iota_compare_fusion), kind=kLoop, calls=%fused_computation | loop fusion | flops 524288 | bytes 4194306 | tf_op jit(solution)/shard_map/jit(_where)/select_n | solution.py:548
  (47 shorter events, 13.3 us)
Async XLA Ops:
  2.4 14.2 %collective-permute-start = (f32[2,2,136,128]{3,2,1,0:T(8,128)S(1)}, f32[2,2,136,128]{3,2,1,0:T(8,128)S(1)}, u32[]{:S(2)}, u32[]{:S(2)}) collective-permute-start(f32[2,2,136,128]{3,2,1,0:T(8,128)S(1)} %pad_maximum_fusion), channel_id=1, source_target_pairs={{0,16},{16,32},{32,48},{48,64},{64,80},{80,96},{96,112},{112,128},... | collective-permute-start | bytes 835592 | tf_op jit(solution)/shard_map/ppermute | solution.py:459
  4.7 6.5 %collective-permute-start.2 = (f32[2,2,128,128]{3,2,1,0:T(8,128)}, f32[2,2,128,128]{3,2,1,0:T(8,128)S(1)}, u32[]{:S(2)}, u32[]{:S(2)}) collective-permute-start(f32[2,2,128,128]{3,2,1,0:T(8,128)} %middle.1), channel_id=1, source_target_pairs={{0,1},{1,2},{2,3},{3,4},{4,5},{5,6},{6,7},{7,8},{8,9},{9,10},{10,1... | collective-permute-start | bytes 786440 | tf_op jit(solution)/shard_map/ppermute | solution.py:459
  7.1 9.3 %collective-permute-start.1 = (f32[2,2,128,128]{3,2,1,0:T(8,128)}, f32[2,2,128,128]{3,2,1,0:T(8,128)S(1)}, u32[]{:S(2)}, u32[]{:S(2)}) collective-permute-start(f32[2,2,128,128]{3,2,1,0:T(8,128)} %middle.1), channel_id=1, source_target_pairs={{0,240},{16,0},{32,16},{48,32},{64,48},{80,64},{96,80},{112,96},{1... | collective-permute-start | bytes 786440 | tf_op jit(solution)/shard_map/ppermute | solution.py:459
  10.6 6.0 %collective-permute-start.3 = (f32[2,2,128,128]{3,2,1,0:T(8,128)}, f32[2,2,128,128]{3,2,1,0:T(8,128)S(1)}, u32[]{:S(2)}, u32[]{:S(2)}) collective-permute-start(f32[2,2,128,128]{3,2,1,0:T(8,128)} %middle.1), channel_id=1, source_target_pairs={{0,15},{1,0},{2,1},{3,2},{4,3},{5,4},{6,5},{7,6},{8,7},{9,8},{10,9... | collective-permute-start | bytes 786440 | tf_op jit(solution)/shard_map/ppermute | solution.py:459
  16.7 9.1 %collective-permute-start.5 = (f32[2,2,264,128]{3,2,1,0:T(8,128)S(1)}, f32[2,2,264,128]{3,2,1,0:T(8,128)S(1)}, u32[]{:S(2)}, u32[]{:S(2)}) collective-permute-start(f32[2,2,264,128]{3,2,1,0:T(8,128)S(1)} %constant_dynamic-update-slice_fusion.middle_edges), channel_id=1, source_target_pairs={{0,15},{1,0},{2,1},{3,2},{4,3},{5,4},{6,5},{7,6},{8,7},{9,8},{10,9... | collective-permute-start | bytes 1622024 | tf_op jit(solution)/shard_map/ppermute | solution.py:459
  18.6 7.1 %collective-permute-start.4 = (f32[2,2,264,128]{3,2,1,0:T(8,128)S(1)}, f32[2,2,264,128]{3,2,1,0:T(8,128)S(1)}, u32[]{:S(2)}, u32[]{:S(2)}) collective-permute-start(f32[2,2,264,128]{3,2,1,0:T(8,128)S(1)} %constant_dynamic-update-slice_fusion.middle_edges), channel_id=1, source_target_pairs={{0,1},{1,2},{2,3},{3,4},{4,5},{5,6},{6,7},{7,8},{8,9},{9,10},{10,1... | collective-permute-start | bytes 1622024 | tf_op jit(solution)/shard_map/ppermute | solution.py:459
  18.6 1.6 %copy-start.1 = (f32[2,4,256,256]{3,2,1,0:T(8,128)S(1)}, f32[2,4,256,256]{3,2,1,0:T(8,128)}, u32[]{:S(2)}) copy-start(f32[2,4,256,256]{3,2,1,0:T(8,128)} %probe_in.1) | copy-start | bytes 6291460
  20.2 1.0 copy-start.3
  21.3 1.4 %copy-start.6 = (f32[2,256,256]{2,1,0:T(8,128)S(1)}, f32[2,256,256]{2,1,0:T(8,128)}, u32[]{:S(2)}) copy-start(f32[2,256,256]{2,1,0:T(8,128)} %param.10) | copy-start | bytes 1572868
  21.3 4.5 %copy-start = (f32[2,2,128,128]{3,2,1,0:T(8,128)S(1)}, f32[2,2,128,128]{3,2,1,0:T(8,128)}, u32[]{:S(2)}) copy-start(f32[2,2,128,128]{3,2,1,0:T(8,128)} %middle.1) | copy-start | bytes 786436
  21.3 4.5 %copy-start.2 = (f32[2,256,256]{2,1,0:T(8,128)S(1)}, f32[2,256,256]{2,1,0:T(8,128)}, u32[]{:S(2)}) copy-start(f32[2,256,256]{2,1,0:T(8,128)} %constant.62.clone.phase) | copy-start | bytes 1572868
  22.7 18.9 %collective-permute-start.6 = (f32[2,256,256]{2,1,0:T(8,128)S(1)}, f32[2,256,256]{2,1,0:T(8,128)S(1)}, u32[]{:S(2)}, u32[]{:S(2)}) collective-permute-start(f32[2,256,256]{2,1,0:T(8,128)S(1)} %copy-done.6), channel_id=1, source_target_pairs={{0,17},{1,18},{2,19},{3,20},{4,21},{5,22},{6,23},{7,24},{8,25},{9,... | collective-permute-start | bytes 1572872 | tf_op jit(solution)/shard_map/ppermute | solution.py:503
  56.6 7.8 %copy-start.4 = (f32[2,2,2,256,256]{4,3,2,1,0:T(8,128)}, f32[2,2,2,256,256]{4,3,2,1,0:T(8,128)S(1)}, u32[]{:S(2)}) copy-start(f32[2,2,2,256,256]{4,3,2,1,0:T(8,128)S(1)} %get-tuple-element.43.totals) | copy-start | bytes 6291460
  56.6 6.6 %collective-permute-start.7 = (f32[4,256,256]{2,1,0:T(8,128)S(1)}, f32[4,256,256]{2,1,0:T(8,128)S(1)}, u32[]{:S(2)}, u32[]{:S(2)}) collective-permute-start(f32[4,256,256]{2,1,0:T(8,128)S(1)} %get-tuple-element.41), channel_id=1, source_target_pairs={{0,1},{1,0},{2,3},{3,2},{4,5},{5,4},{6,7},{7,6},{8,9},{9,8},{10,11... | collective-permute-start | bytes 3145736 | tf_op jit(solution)/shard_map/ppermute | solution.py:471
  64.3 21.9 %all-to-all-start = ((f32[16,64,256]{2,1,0:T(8,128)}), f32[16,64,256]{2,1,0:T(8,128)S(1)}, u32[]{:S(2)}, u32[]{:S(2)}) async-start(f32[16,64,256]{2,1,0:T(8,128)} %bitcast.3), calls=%async_computation | async-start | bytes 2097152 | tf_op jit(solution)/shard_map/all_to_all | solution.py:463
  69.2 1.6 %copy-start.5 = (f32[2,2,2,256,256]{4,3,2,1,0:T(8,128)S(1)}, f32[2,2,2,256,256]{4,3,2,1,0:T(8,128)}, u32[]{:S(2)}) copy-start(f32[2,2,2,256,256]{4,3,2,1,0:T(8,128)} %copy-done.4) | copy-start | bytes 6291460
  74.4 11.8 %collective-permute-start.8 = (f32[2,2,384,128]{3,2,1,0:T(8,128)S(1)}, f32[2,2,384,128]{3,2,1,0:T(8,128)}, u32[]{:S(2)}, u32[]{:S(2)}) collective-permute-start(f32[2,2,384,128]{3,2,1,0:T(8,128)S(1)} %get-tuple-element.46), channel_id=1, source_target_pairs={{0,15},{1,0},{2,1},{3,2},{4,3},{5,4},{6,5},{7,6},{8,7},{9,8},{10,9... | collective-permute-start | bytes 2359304 | tf_op jit(solution)/shard_map/ppermute | solution.py:459
  75.1 11.2 %collective-permute-start.9 = (f32[2,2,384,128]{3,2,1,0:T(8,128)S(1)}, f32[2,2,384,128]{3,2,1,0:T(8,128)}, u32[]{:S(2)}, u32[]{:S(2)}) collective-permute-start(f32[2,2,384,128]{3,2,1,0:T(8,128)S(1)} %get-tuple-element.47), channel_id=1, source_target_pairs={{0,1},{1,2},{2,3},{3,4},{4,5},{5,6},{6,7},{7,8},{8,9},{9,10},{10,1... | collective-permute-start | bytes 2359304 | tf_op jit(solution)/shard_map/ppermute | solution.py:459
  86.4 6.5 %collective-permute-start.10 = (f32[32,256]{1,0:T(8,128)S(1)}, f32[32,256]{1,0:T(8,128)S(1)}, u32[]{:S(2)}, u32[]{:S(2)}) collective-permute-start(f32[32,256]{1,0:T(8,128)S(1)} %dynamic-slice_bitcast_fusion), channel_id=1, source_target_pairs={{0,2},{1,3},{2,0},{3,1},{4,6},{5,7},{6,4},{7,5},{8,10},{9,11},{10,... | collective-permute-start | bytes 98312 | tf_op jit(solution)/shard_map/ppermute | solution.py:532
  88.0 15.8 %collective-permute-start.14 = (f32[2,2,128,128]{3,2,1,0:T(8,128)S(1)}, f32[2,2,128,128]{3,2,1,0:T(8,128)S(1)}, u32[]{:S(2)}, u32[]{:S(2)}) collective-permute-start(f32[2,2,128,128]{3,2,1,0:T(8,128)S(1)} %get-tuple-element.54), channel_id=1, source_target_pairs={{0,16},{16,32},{32,48},{48,64},{64,80},{80,96},{96,112},{112,128},... | collective-permute-start | bytes 786440 | tf_op jit(solution)/shard_map/ppermute | solution.py:459
  89.4 14.4 %collective-permute-start.13 = (f32[2,2,128,128]{3,2,1,0:T(8,128)S(1)}, f32[2,2,128,128]{3,2,1,0:T(8,128)S(1)}, u32[]{:S(2)}, u32[]{:S(2)}) collective-permute-start(f32[2,2,128,128]{3,2,1,0:T(8,128)S(1)} %get-tuple-element.55), channel_id=1, source_target_pairs={{0,240},{16,0},{32,16},{48,32},{64,48},{80,64},{96,80},{112,96},{1... | collective-permute-start | bytes 786440 | tf_op jit(solution)/shard_map/ppermute | solution.py:459
  92.9 4.3 %collective-permute-start.11 = (f32[32,256]{1,0:T(8,128)S(1)}, f32[32,256]{1,0:T(8,128)S(1)}, u32[]{:S(2)}, u32[]{:S(2)}) collective-permute-start(f32[32,256]{1,0:T(8,128)S(1)} %bitcast_add_fusion), channel_id=1, source_target_pairs={{0,4},{1,5},{2,6},{3,7},{4,0},{5,1},{6,2},{7,3},{8,12},{9,13},{10,... | collective-permute-start | bytes 98312 | tf_op jit(solution)/shard_map/ppermute | solution.py:532
  97.1 6.7 %collective-permute-start.12 = (f32[32,256]{1,0:T(8,128)S(1)}, f32[32,256]{1,0:T(8,128)S(1)}, u32[]{:S(2)}, u32[]{:S(2)}) collective-permute-start(f32[32,256]{1,0:T(8,128)S(1)} %add.60), channel_id=1, source_target_pairs={{0,8},{1,9},{2,10},{3,11},{4,12},{5,13},{6,14},{7,15},{8,0},{9,1},... | collective-permute-start | bytes 98312 | tf_op jit(solution)/shard_map/ppermute | solution.py:532
  120.5 9.9 %collective-permute-start.15 = (f32[32,32,256]{2,1,0:T(8,128)S(1)}, f32[32,32,256]{2,1,0:T(8,128)S(1)}, u32[]{:S(2)}, u32[]{:S(2)}) collective-permute-start(f32[32,32,256]{2,1,0:T(8,128)S(1)} %all_to_all.10), channel_id=1, source_target_pairs={{0,1},{1,0},{2,3},{3,2},{4,5},{5,4},{6,7},{7,6},{8,9},{9,8},{10,11... | collective-permute-start | bytes 3145736 | tf_op jit(solution)/shard_map/ppermute | solution.py:471

commit v5 on v4

--- a/solution.py
+++ b/solution.py
@@ -172,6 +172,31 @@
         pltpu.VMEM((2, n, modes * n), BF),
         pltpu.VMEM((2, n, modes * n), BF),
     ]
+
+
+def label_kernel(offsets, corner, tile_in, out, sem):
+    tile = tile_in.shape[-1]
+    copy = pltpu.make_async_copy(tile_in, out.at[:, :, :tile], sem)
+    copy.start()
+    for position in range(offsets.shape[0]):
+        for axis in range(2):
+            number = (offsets[position, axis] - corner[axis]).astype(F32)
+            out[position, axis, tile:] = jnp.full((8, tile), number, F32)
+    copy.wait()
+
+
+def labelled(offsets, corner, field):
+    tile = field.shape[-1]
+    return pl.pallas_call(
+        label_kernel,
+        out_shape=jax.ShapeDtypeStruct(field.shape[:2] + (tile + 8, tile), F32),
+        in_specs=[SMEM, SMEM, ANY],
+        out_specs=VMEM,
+        scratch_shapes=[pltpu.SemaphoreType.DMA],
+        compiler_params=pltpu.CompilerParams(vmem_limit_bytes=4 << 20),
+        cost_estimate=pl.CostEstimate(flops=0, bytes_accessed=1 << 19, transcendentals=0),
+        name="label",
+    )(offsets, corner, field)
 
 
 def prepare_kernel(probe_in, blocks, probe, tables):
@@ -484,11 +509,7 @@
         for t in range(tiles)
     ]
     corner = jnp.stack([lax.axis_index("strip"), lax.axis_index("tile")]).astype(jnp.int32) * tile
-    wrap = jnp.array([strips * tile, tiles * tile], jnp.int32)
-    local = ((offsets - corner) % wrap).astype(F32)[:, :, None, None]
-    sent_down = jnp.concatenate(
-        [object_field, jnp.broadcast_to(local, local.shape[:2] + (8, tile))], axis=2
-    )
+    sent_down = labelled(offsets, corner, object_field)
     above = around(sent_down, "strip", 1)
     below = around(object_field, "strip", -1)
     left = around(object_field, "tile", 1)
@@ -513,17 +534,19 @@
         for c in range(cores)
         for group in range(levels // pairs)
     ]
-    part = (kept + swapped(sent)).reshape(strips, -1, n)
-    part, totals = lax.optimization_barrier((part, totals))
-    shares = exchanged(part, "strip")
+    received = swapped(sent)
     grad_left, grad_middle, grad_right = placed(scalars, totals, 3 * tile, tile)
+    received, grad_left, grad_middle, grad_right = lax.optimization_barrier(
+        (received, grad_left, grad_middle, grad_right)
+    )
     from_right = around(grad_left, "tile", -1)
     from_left = around(grad_right, "tile", 1)
-    shares, from_right, from_left = lax.optimization_barrier((shares, from_right, from_left))
+    shares = exchanged((kept + received).reshape(strips, -1, n), "strip")
     column = grad_middle + from_right + from_left
     upper, lower = column[:, :, :tile], column[:, :, 2 * tile :]
     from_below = around(upper, "strip", -1)
     from_above = around(lower, "strip", 1)
+    shares, column, upper, lower = lax.optimization_barrier((shares, column, upper, lower))
 
     def across(value, distance):
         step = [
@@ -537,10 +560,10 @@
         lax.dynamic_index_in_dim(shares, 1 - mine, 0, False), 1
     )
     distance = pairs
+    share, from_below, from_above = lax.optimization_barrier((share, from_below, from_above))
     while distance < levels:
         share = share + across(share, distance)
         distance *= 2
-    share, from_below, from_above = lax.optimization_barrier((share, from_below, from_above))
     object_grad = column[:, :, tile : 2 * tile] + from_below + from_above
     half = exchanged(copies(share, strips * pairs), both, groups)
     other = swapped(half)

time: 132 us -> 132 us (level)
  starting transfers between devices: 40.7 us -> 34 us
  waiting for transfers between devices: 28.5 us -> 32.6 us
  blocking collectives: 16.6 us -> 19.5 us
  other arithmetic: 6.81 us -> 5.09 us
    all_to_all x1, waiting for transfers between devices: 0.01 us -> 5.21 us  [exchanged(): lax.all_to_all(value, axis, 0, 0, tiled=True, axis_index_groups=groups)]
    ppermute x2, starting transfers between devices: 11.9 us -> 7.26 us  [swapped(): lax.ppermute(value, 'tile', [(at, at ^ 1) for at in range(lax.axis_size('...]
    ppermute x3, waiting for transfers between devices: 4.44 us -> 8.71 us  [across(): return lax.ppermute(value, 'tile', step)]
    ppermute x10, waiting for transfers between devices: 18.6 us -> 15.5 us  [around(): lax.ppermute(value, axis, [(at, (at + steps) % count) for at in range(cou...]
    all_to_all x1, blocking collectives: 16.6 us -> 19.5 us  [exchanged(): lax.all_to_all(value, axis, 0, 0, tiled=True, axis_index_groups=groups)]
    ppermute x2, waiting for transfers between devices: 3.81 us -> 1.54 us  [swapped(): lax.ppermute(value, 'tile', [(at, at ^ 1) for at in range(lax.axis_size('...]
    ppermute x3, starting transfers between devices: 6.59 us -> 4.76 us  [across(): return lax.ppermute(value, 'tile', step)]
  transfers between devices with their start and end apart: 17 -> 17, of which waited for: 9 -> 11; matrix products, arithmetic and copies ran while one was open for 2% -> 3% of each run, Pallas kernels for 15% -> 15%
where the time goes in v5:
time: 132 us; the launch traced here: 131 us
  Pallas kernels  34.7 us (26%)
  starting transfers between devices  34 us (26%)
  waiting for transfers between devices  32.6 us (25%)
  blocking collectives  19.5 us (15%)
  other arithmetic  5.09 us (4%)
  local copies, waits for them, and re-layouts  4.47 us (3%)
    all_to_all x1, blocking collectives, exchanged(): lax.all_to_all(value, axis, 0, 0, tiled=True, axis_index_groups=groups)  19.5 us
    ppermute x10, starting transfers between devices, around(): lax.ppermute(value, axis, [(at, (at + steps) % count) for at in range(cou...  17.1 us
    ppermute x10, waiting for transfers between devices, around(): lax.ppermute(value, axis, [(at, (at + steps) % count) for at in range(cou...  15.5 us
    pallas_call x1, Pallas kernels, backward(): pl.pallas_call(backward_kernel, out_shape=(jax.ShapeDtypeStruct((count, 2...  14.9 us
    pallas_call x1, Pallas kernels, forward(): pl.pallas_call(forward_kernel, out_shape=(jax.ShapeDtypeStruct((count, 2,...  14.2 us
    ppermute x3, waiting for transfers between devices, across(): return lax.ppermute(value, 'tile', step)  8.71 us
    ppermute x2, starting transfers between devices, swapped(): lax.ppermute(value, 'tile', [(at, at ^ 1) for at in range(lax.axis_size('...  7.26 us
    all_to_all x1, waiting for transfers between devices, exchanged(): lax.all_to_all(value, axis, 0, 0, tiled=True, axis_index_groups=groups)  5.21 us
  transfers between devices with their start and end apart: 17, of which 11 were waited for; matrix products, arithmetic and copies ran while one was open for 3% of the time, Pallas kernels for 15%

profile of v5, /device:TPU:1, one launch (start us, length us, event | category | flops | bytes accessed | tf_op | source)
XLA Modules:
  0.0 131.2 jit_solution(12600628369649314590)
XLA Ops:
  2.9 2.2 %collective-permute-start = (f32[2,2,136,128]{3,2,1,0:T(8,128)S(1)}, f32[2,2,136,128]{3,2,1,0:T(8,128)S(1)}, u32[]{:S(2)}, u32[]{:S(2)}) collective-permute-start(f32[2,2,136,128]{3,2,1,0:T(8,128)S(1)} %label.1), channel_id=1, source_target_pairs={{0,16},{16,32},{32,48},{48,64},{64,80},{80,96},{96,112},{112,128},... | collective-permute-start | bytes 835592 | tf_op jit(solution)/shard_map/ppermute | solution.py:484
  5.1 2.5 %collective-permute-start.2 = (f32[2,2,128,128]{3,2,1,0:T(8,128)S(1)}, f32[2,2,128,128]{3,2,1,0:T(8,128)S(1)}, u32[]{:S(2)}, u32[]{:S(2)}) collective-permute-start(f32[2,2,128,128]{3,2,1,0:T(8,128)S(1)} %copy-done), channel_id=1, source_target_pairs={{0,1},{1,2},{2,3},{3,4},{4,5},{5,6},{6,7},{7,8},{8,9},{9,10},{10,1... | collective-permute-start | bytes 786440 | tf_op jit(solution)/shard_map/ppermute | solution.py:484
  7.6 3.5 %collective-permute-start.1 = (f32[2,2,128,128]{3,2,1,0:T(8,128)S(1)}, f32[2,2,128,128]{3,2,1,0:T(8,128)S(1)}, u32[]{:S(2)}, u32[]{:S(2)}) collective-permute-start(f32[2,2,128,128]{3,2,1,0:T(8,128)S(1)} %copy-done), channel_id=1, source_target_pairs={{0,240},{16,0},{32,16},{48,32},{64,48},{80,64},{96,80},{112,96},{1... | collective-permute-start | bytes 786440 | tf_op jit(solution)/shard_map/ppermute | solution.py:484
  11.6 5.0 %collective-permute-done.1 = f32[2,2,128,128]{3,2,1,0:T(8,128)S(1)} collective-permute-done((f32[2,2,128,128]{3,2,1,0:T(8,128)S(1)}, f32[2,2,128,128]{3,2,1,0:T(8,128)S(1)}, u32[]{:S(2)}, u32[]{:S(2)}) %collective-permute-start.1) | collective-permute-done | bytes 262176 | tf_op jit(solution)/shard_map/ppermute | solution.py:484
  17.0 1.9 %collective-permute-start.5 = (f32[2,2,264,128]{3,2,1,0:T(8,128)S(1)}, f32[2,2,264,128]{3,2,1,0:T(8,128)S(1)}, u32[]{:S(2)}, u32[]{:S(2)}) collective-permute-start(f32[2,2,264,128]{3,2,1,0:T(8,128)S(1)} %constant_dynamic-update-slice_fusion.middle_edges), channel_id=1, source_target_pairs={{0,15},{1,0},{2,1},{3,2},{4,3},{5,4},{6,5},{7,6},{8,7},{9,8},{10,9... | collective-permute-start | bytes 1622024 | tf_op jit(solution)/shard_map/ppermute | solution.py:484
  23.0 3.1 %collective-permute-done.5.right_edges = f32[2,2,264,128]{3,2,1,0:T(8,128)S(1)} collective-permute-done((f32[2,2,264,128]{3,2,1,0:T(8,128)S(1)}, f32[2,2,264,128]{3,2,1,0:T(8,128)S(1)}, u32[]{:S(2)}, u32[]{:S(2)}) %collective-permute-start.5) | collective-permute-done | bytes 540704 | tf_op jit(solution)/shard_map/ppermute | solution.py:484
  26.1 14.2 %forward.1 = (f32[2,2,2,256,256]{4,3,2,1,0:T(8,128)S(1)}, f32[2,2,4,256,256]{4,3,2,1,0:T(8,128)S(1)}, f32[2,2,4,256,256]{4,3,2,1,0:T(8,128)S(1)}, f32[2,256,256]{2,1,0:T(8,128)S(1)}, s32[2,2]{1,0:T(2,128)S(1)}) custom-call(f32[2,2,128,128]{3,2,1,0:T(8,128)S(1)} %collective-permute-done.2.left, f32[2,2,264,128]{3,2,1,0:T(8,128)S(1)} %collective-permute-done.4.left_edges, ...), custom_call_target="tpu_custom_call" | custom-call | flops 12884901888 | bytes 18874368 | tf_op jit(solution)/shard_map/forward/pallas_call | solution.py:311
  40.3 1.6 %collective-permute-done.6.measured = f32[2,256,256]{2,1,0:T(8,128)S(1)} collective-permute-done((f32[2,256,256]{2,1,0:T(8,128)S(1)}, f32[2,256,256]{2,1,0:T(8,128)S(1)}, u32[]{:S(2)}, u32[]{:S(2)}) %collective-permute-start.6) | collective-permute-done | bytes 524320 | tf_op jit(solution)/shard_map/ppermute | solution.py:524
  41.9 14.9 %backward.1 = (f32[2,2,2,256,256]{4,3,2,1,0:T(8,128)S(1)}, f32[4,256,256]{2,1,0:T(8,128)S(1)}, f32[4,256,256]{2,1,0:T(8,128)S(1)}) custom-call(s32[1]{0:T(128)} %bitcast.core, f32[2,2,2,256,256]{4,3,2,1,0:T(8,128)S(1)} %get-tuple-element.35.window, f32[2,2,4,256,256]{4,3,2,1,0:T(8,128)S(1)} %get-tuple-element.36.moved, ...), custom_call_target="tpu_custom_call" | custom-call | flops 12884901888 | bytes 18874368 | tf_op jit(solution)/shard_map/backward/pallas_call | solution.py:411
  56.8 4.4 %collective-permute-start.7 = (f32[4,256,256]{2,1,0:T(8,128)S(1)}, f32[4,256,256]{2,1,0:T(8,128)S(1)}, u32[]{:S(2)}, u32[]{:S(2)}) collective-permute-start(f32[4,256,256]{2,1,0:T(8,128)S(1)} %get-tuple-element.41), channel_id=1, source_target_pairs={{0,1},{1,0},{2,3},{3,2},{4,5},{5,4},{6,7},{7,6},{8,9},{9,8},{10,11... | collective-permute-start | bytes 3145736 | tf_op jit(solution)/shard_map/ppermute | solution.py:496
  61.3 3.6 %place.1 = (f32[2,2,384,128]{3,2,1,0:T(8,128)S(1)}, f32[2,2,384,128]{3,2,1,0:T(8,128)S(1)}, f32[2,2,384,128]{3,2,1,0:T(8,128)S(1)}) custom-call(s32[2,2]{1,0:T(2,128)S(1)} %get-tuple-element.42.scalars, f32[2,2,2,256,256]{4,3,2,1,0:T(8,128)S(1)} %get-tuple-element.43.totals), custom_call_target="tpu_custom_call" | custom-call | flops 2147483648 | bytes 8388608 | tf_op jit(solution)/shard_map/place/pallas_call | solution.py:467
  65.0 1.7 %collective-permute-start.9 = (f32[2,2,384,128]{3,2,1,0:T(8,128)S(1)}, f32[2,2,384,128]{3,2,1,0:T(8,128)}, u32[]{:S(2)}, u32[]{:S(2)}) collective-permute-start(f32[2,2,384,128]{3,2,1,0:T(8,128)S(1)} %get-tuple-element.50), channel_id=1, source_target_pairs={{0,1},{1,2},{2,3},{3,4},{4,5},{5,6},{6,7},{7,8},{8,9},{9,10},{10,1... | collective-permute-start | bytes 2359304 | tf_op jit(solution)/shard_map/ppermute | solution.py:484
  67.8 4.7 %all-to-all-start = ((f32[16,64,256]{2,1,0:T(8,128)}), f32[16,64,256]{2,1,0:T(8,128)S(1)}, u32[]{:S(2)}, u32[]{:S(2)}) async-start(f32[16,64,256]{2,1,0:T(8,128)} %bitcast.3), calls=%async_computation | async-start | bytes 2097152 | tf_op jit(solution)/shard_map/all_to_all | solution.py:488
  72.6 4.2 %collective-permute-done.8 = f32[2,2,384,128]{3,2,1,0:T(8,128)} collective-permute-done((f32[2,2,384,128]{3,2,1,0:T(8,128)S(1)}, f32[2,2,384,128]{3,2,1,0:T(8,128)}, u32[]{:S(2)}, u32[]{:S(2)}) %collective-permute-start.8) | collective-permute-done | bytes 786464 | tf_op jit(solution)/shard_map/ppermute | solution.py:484
  78.4 4.8 %collective-permute-start.11 = (f32[2,2,128,128]{3,2,1,0:T(8,128)S(1)}, f32[2,2,128,128]{3,2,1,0:T(8,128)S(1)}, u32[]{:S(2)}, u32[]{:S(2)}) collective-permute-start(f32[2,2,128,128]{3,2,1,0:T(8,128)S(1)} %get-tuple-element.57), channel_id=1, source_target_pairs={{0,240},{16,0},{32,16},{48,32},{64,48},{80,64},{96,80},{112,96},{1... | collective-permute-start | bytes 786440 | tf_op jit(solution)/shard_map/ppermute | solution.py:484
  83.1 5.2 %all-to-all-done = f32[16,64,256]{2,1,0:T(8,128)S(1)} async-done(((f32[16,64,256]{2,1,0:T(8,128)}), f32[16,64,256]{2,1,0:T(8,128)S(1)}, u32[]{:S(2)}, u32[]{:S(2)}) %all-to-all-start) | async-done | bytes 1048608 | tf_op jit(solution)/shard_map/all_to_all | solution.py:488
  88.5 3.0 %collective-permute-done.10 = f32[32,256]{1,0:T(8,128)S(1)} collective-permute-done((f32[32,256]{1,0:T(8,128)S(1)}, f32[32,256]{1,0:T(8,128)S(1)}, u32[]{:S(2)}, u32[]{:S(2)}) %collective-permute-start.10) | collective-permute-done | bytes 32800 | tf_op jit(solution)/shard_map/ppermute | solution.py:555
  91.6 3.0 %collective-permute-done.12 = f32[2,2,128,128]{3,2,1,0:T(8,128)S(1)} collective-permute-done((f32[2,2,128,128]{3,2,1,0:T(8,128)S(1)}, f32[2,2,128,128]{3,2,1,0:T(8,128)S(1)}, u32[]{:S(2)}, u32[]{:S(2)}) %collective-permute-start.12) | collective-permute-done | bytes 262176 | tf_op jit(solution)/shard_map/ppermute | solution.py:484
  94.6 3.7 %collective-permute-done.13 = f32[32,256]{1,0:T(8,128)S(1)} collective-permute-done((f32[32,256]{1,0:T(8,128)S(1)}, f32[32,256]{1,0:T(8,128)S(1)}, u32[]{:S(2)}, u32[]{:S(2)}) %collective-permute-start.13) | collective-permute-done | bytes 32800 | tf_op jit(solution)/shard_map/ppermute | solution.py:555
  98.2 4.7 %collective-permute-start.14 = (f32[32,256]{1,0:T(8,128)S(1)}, f32[32,256]{1,0:T(8,128)S(1)}, u32[]{:S(2)}, u32[]{:S(2)}) collective-permute-start(f32[32,256]{1,0:T(8,128)S(1)} %add.51), channel_id=1, source_target_pairs={{0,8},{1,9},{2,10},{3,11},{4,12},{5,13},{6,14},{7,15},{8,0},{9,1},... | collective-permute-start | bytes 98312 | tf_op jit(solution)/shard_map/ppermute | solution.py:555
  102.9 2.0 %collective-permute-done.14 = f32[32,256]{1,0:T(8,128)S(1)} collective-permute-done((f32[32,256]{1,0:T(8,128)S(1)}, f32[32,256]{1,0:T(8,128)S(1)}, u32[]{:S(2)}, u32[]{:S(2)}) %collective-permute-start.14) | collective-permute-done | bytes 32800 | tf_op jit(solution)/shard_map/ppermute | solution.py:555
  105.0 19.5 %all_to_all.10 = f32[32,32,256]{2,1,0:T(8,128)S(1)} all-to-all(f32[32,32,256]{2,1,0:T(8,128)S(1)} %broadcast_in_dim.37), channel_id=1, replica_groups={{0,2,16,18,32,34,48,50,64,66,80,82,96,98,112,114,128,130,144,146,160,16..., dimensions={0} | all-to-all | bytes 2097152 | tf_op jit(solution)/shard_map/all_to_all | solution.py:488
  124.5 2.8 %collective-permute-start.15 = (f32[32,32,256]{2,1,0:T(8,128)S(1)}, f32[32,32,256]{2,1,0:T(8,128)S(1)}, u32[]{:S(2)}, u32[]{:S(2)}) collective-permute-start(f32[32,32,256]{2,1,0:T(8,128)S(1)} %all_to_all.10), channel_id=1, source_target_pairs={{0,1},{1,0},{2,3},{3,2},{4,5},{5,4},{6,7},{7,6},{8,9},{9,8},{10,11... | collective-permute-start | bytes 3145736 | tf_op jit(solution)/shard_map/ppermute | solution.py:496
  129.6 1.6 %broadcast_select_fusion = f32[2,4,256,256]{3,2,1,0:T(8,128)} fusion(f32[4,256,256]{2,1,0:T(8,128)S(1)} %bitcast.12, f32[4,256,256]{2,1,0:T(8,128)S(1)} %bitcast.11, pred[2]{0:T(512)(128)(4,1)S(1)} %iota_compare_fusion), kind=kLoop, calls=%fused_computation | loop fusion | flops 524288 | bytes 4194306 | tf_op jit(solution)/shard_map/jit(_where)/select_n | solution.py:571
  (45 shorter events, 12.6 us)
Async XLA Ops:
  0.7 1.0 copy-start
  1.7 0.7 copy-start.2
  2.9 14.0 %collective-permute-start = (f32[2,2,136,128]{3,2,1,0:T(8,128)S(1)}, f32[2,2,136,128]{3,2,1,0:T(8,128)S(1)}, u32[]{:S(2)}, u32[]{:S(2)}) collective-permute-start(f32[2,2,136,128]{3,2,1,0:T(8,128)S(1)} %label.1), channel_id=1, source_target_pairs={{0,16},{16,32},{32,48},{48,64},{64,80},{80,96},{96,112},{112,128},... | collective-permute-start | bytes 835592 | tf_op jit(solution)/shard_map/ppermute | solution.py:484
  5.1 6.5 %collective-permute-start.2 = (f32[2,2,128,128]{3,2,1,0:T(8,128)S(1)}, f32[2,2,128,128]{3,2,1,0:T(8,128)S(1)}, u32[]{:S(2)}, u32[]{:S(2)}) collective-permute-start(f32[2,2,128,128]{3,2,1,0:T(8,128)S(1)} %copy-done), channel_id=1, source_target_pairs={{0,1},{1,2},{2,3},{3,4},{4,5},{5,6},{6,7},{7,8},{8,9},{9,10},{10,1... | collective-permute-start | bytes 786440 | tf_op jit(solution)/shard_map/ppermute | solution.py:484
  7.6 9.0 %collective-permute-start.1 = (f32[2,2,128,128]{3,2,1,0:T(8,128)S(1)}, f32[2,2,128,128]{3,2,1,0:T(8,128)S(1)}, u32[]{:S(2)}, u32[]{:S(2)}) collective-permute-start(f32[2,2,128,128]{3,2,1,0:T(8,128)S(1)} %copy-done), channel_id=1, source_target_pairs={{0,240},{16,0},{32,16},{48,32},{64,48},{80,64},{96,80},{112,96},{1... | collective-permute-start | bytes 786440 | tf_op jit(solution)/shard_map/ppermute | solution.py:484
  11.1 5.8 %collective-permute-start.3 = (f32[2,2,128,128]{3,2,1,0:T(8,128)S(1)}, f32[2,2,128,128]{3,2,1,0:T(8,128)S(1)}, u32[]{:S(2)}, u32[]{:S(2)}) collective-permute-start(f32[2,2,128,128]{3,2,1,0:T(8,128)S(1)} %copy-done), channel_id=1, source_target_pairs={{0,15},{1,0},{2,1},{3,2},{4,3},{5,4},{6,5},{7,6},{8,7},{9,8},{10,9... | collective-permute-start | bytes 786440 | tf_op jit(solution)/shard_map/ppermute | solution.py:484
  17.0 9.1 %collective-permute-start.5 = (f32[2,2,264,128]{3,2,1,0:T(8,128)S(1)}, f32[2,2,264,128]{3,2,1,0:T(8,128)S(1)}, u32[]{:S(2)}, u32[]{:S(2)}) collective-permute-start(f32[2,2,264,128]{3,2,1,0:T(8,128)S(1)} %constant_dynamic-update-slice_fusion.middle_edges), channel_id=1, source_target_pairs={{0,15},{1,0},{2,1},{3,2},{4,3},{5,4},{6,5},{7,6},{8,7},{9,8},{10,9... | collective-permute-start | bytes 1622024 | tf_op jit(solution)/shard_map/ppermute | solution.py:484
  18.8 7.2 %collective-permute-start.4 = (f32[2,2,264,128]{3,2,1,0:T(8,128)S(1)}, f32[2,2,264,128]{3,2,1,0:T(8,128)S(1)}, u32[]{:S(2)}, u32[]{:S(2)}) collective-permute-start(f32[2,2,264,128]{3,2,1,0:T(8,128)S(1)} %constant_dynamic-update-slice_fusion.middle_edges), channel_id=1, source_target_pairs={{0,1},{1,2},{2,3},{3,4},{4,5},{5,6},{6,7},{7,8},{8,9},{9,10},{10,1... | collective-permute-start | bytes 1622024 | tf_op jit(solution)/shard_map/ppermute | solution.py:484
  18.8 1.6 %copy-start.3 = (f32[2,4,256,256]{3,2,1,0:T(8,128)S(1)}, f32[2,4,256,256]{3,2,1,0:T(8,128)}, u32[]{:S(2)}) copy-start(f32[2,4,256,256]{3,2,1,0:T(8,128)} %probe_in.1) | copy-start | bytes 6291460
  20.4 1.0 copy-start.5
  21.5 1.4 %copy-start.6 = (f32[2,256,256]{2,1,0:T(8,128)S(1)}, f32[2,256,256]{2,1,0:T(8,128)}, u32[]{:S(2)}) copy-start(f32[2,256,256]{2,1,0:T(8,128)} %param.9) | copy-start | bytes 1572868
  21.5 4.6 %copy-start.1 = (f32[2,2,128,128]{3,2,1,0:T(8,128)S(1)}, f32[2,2,128,128]{3,2,1,0:T(8,128)}, u32[]{:S(2)}) copy-start(f32[2,2,128,128]{3,2,1,0:T(8,128)} %middle.1) | copy-start | bytes 786436
  21.5 4.6 %copy-start.4 = (f32[2,256,256]{2,1,0:T(8,128)S(1)}, f32[2,256,256]{2,1,0:T(8,128)}, u32[]{:S(2)}) copy-start(f32[2,256,256]{2,1,0:T(8,128)} %constant.54.clone.phase) | copy-start | bytes 1572868
  22.9 19.0 %collective-permute-start.6 = (f32[2,256,256]{2,1,0:T(8,128)S(1)}, f32[2,256,256]{2,1,0:T(8,128)S(1)}, u32[]{:S(2)}, u32[]{:S(2)}) collective-permute-start(f32[2,256,256]{2,1,0:T(8,128)S(1)} %copy-done.6), channel_id=1, source_target_pairs={{0,17},{1,18},{2,19},{3,20},{4,21},{5,22},{6,23},{7,24},{8,25},{9,... | collective-permute-start | bytes 1572872 | tf_op jit(solution)/shard_map/ppermute | solution.py:524
  56.8 8.1 %collective-permute-start.7 = (f32[4,256,256]{2,1,0:T(8,128)S(1)}, f32[4,256,256]{2,1,0:T(8,128)S(1)}, u32[]{:S(2)}, u32[]{:S(2)}) collective-permute-start(f32[4,256,256]{2,1,0:T(8,128)S(1)} %get-tuple-element.41), channel_id=1, source_target_pairs={{0,1},{1,0},{2,3},{3,2},{4,5},{5,4},{6,7},{7,6},{8,9},{9,8},{10,11... | collective-permute-start | bytes 3145736 | tf_op jit(solution)/shard_map/ppermute | solution.py:496
  64.9 11.8 %collective-permute-start.8 = (f32[2,2,384,128]{3,2,1,0:T(8,128)S(1)}, f32[2,2,384,128]{3,2,1,0:T(8,128)}, u32[]{:S(2)}, u32[]{:S(2)}) collective-permute-start(f32[2,2,384,128]{3,2,1,0:T(8,128)S(1)} %get-tuple-element.49), channel_id=1, source_target_pairs={{0,15},{1,0},{2,1},{3,2},{4,3},{5,4},{6,5},{7,6},{8,7},{9,8},{10,9... | collective-permute-start | bytes 2359304 | tf_op jit(solution)/shard_map/ppermute | solution.py:484
  65.0 11.8 %collective-permute-start.9 = (f32[2,2,384,128]{3,2,1,0:T(8,128)S(1)}, f32[2,2,384,128]{3,2,1,0:T(8,128)}, u32[]{:S(2)}, u32[]{:S(2)}) collective-permute-start(f32[2,2,384,128]{3,2,1,0:T(8,128)S(1)} %get-tuple-element.50), channel_id=1, source_target_pairs={{0,1},{1,2},{2,3},{3,4},{4,5},{5,6},{6,7},{7,8},{8,9},{9,10},{10,1... | collective-permute-start | bytes 2359304 | tf_op jit(solution)/shard_map/ppermute | solution.py:484
  67.8 20.6 %all-to-all-start = ((f32[16,64,256]{2,1,0:T(8,128)}), f32[16,64,256]{2,1,0:T(8,128)S(1)}, u32[]{:S(2)}, u32[]{:S(2)}) async-start(f32[16,64,256]{2,1,0:T(8,128)} %bitcast.3), calls=%async_computation | async-start | bytes 2097152 | tf_op jit(solution)/shard_map/all_to_all | solution.py:488
  78.3 16.3 %collective-permute-start.12 = (f32[2,2,128,128]{3,2,1,0:T(8,128)S(1)}, f32[2,2,128,128]{3,2,1,0:T(8,128)S(1)}, u32[]{:S(2)}, u32[]{:S(2)}) collective-permute-start(f32[2,2,128,128]{3,2,1,0:T(8,128)S(1)} %get-tuple-element.56), channel_id=1, source_target_pairs={{0,16},{16,32},{32,48},{48,64},{64,80},{80,96},{96,112},{112,128},... | collective-permute-start | bytes 786440 | tf_op jit(solution)/shard_map/ppermute | solution.py:484
  78.4 16.2 %collective-permute-start.11 = (f32[2,2,128,128]{3,2,1,0:T(8,128)S(1)}, f32[2,2,128,128]{3,2,1,0:T(8,128)S(1)}, u32[]{:S(2)}, u32[]{:S(2)}) collective-permute-start(f32[2,2,128,128]{3,2,1,0:T(8,128)S(1)} %get-tuple-element.57), channel_id=1, source_target_pairs={{0,240},{16,0},{32,16},{48,32},{64,48},{80,64},{96,80},{112,96},{1... | collective-permute-start | bytes 786440 | tf_op jit(solution)/shard_map/ppermute | solution.py:484
  88.4 3.1 %collective-permute-start.10 = (f32[32,256]{1,0:T(8,128)S(1)}, f32[32,256]{1,0:T(8,128)S(1)}, u32[]{:S(2)}, u32[]{:S(2)}) collective-permute-start(f32[32,256]{1,0:T(8,128)S(1)} %dynamic-slice_bitcast_fusion), channel_id=1, source_target_pairs={{0,2},{1,3},{2,0},{3,1},{4,6},{5,7},{6,4},{7,5},{8,10},{9,11},{10,... | collective-permute-start | bytes 98312 | tf_op jit(solution)/shard_map/ppermute | solution.py:555
  94.6 3.7 %collective-permute-start.13 = (f32[32,256]{1,0:T(8,128)S(1)}, f32[32,256]{1,0:T(8,128)S(1)}, u32[]{:S(2)}, u32[]{:S(2)}) collective-permute-start(f32[32,256]{1,0:T(8,128)S(1)} %bitcast_add_fusion), channel_id=1, source_target_pairs={{0,4},{1,5},{2,6},{3,7},{4,0},{5,1},{6,2},{7,3},{8,12},{9,13},{10,... | collective-permute-start | bytes 98312 | tf_op jit(solution)/shard_map/ppermute | solution.py:555
  98.2 6.7 %collective-permute-start.14 = (f32[32,256]{1,0:T(8,128)S(1)}, f32[32,256]{1,0:T(8,128)S(1)}, u32[]{:S(2)}, u32[]{:S(2)}) collective-permute-start(f32[32,256]{1,0:T(8,128)S(1)} %add.51), channel_id=1, source_target_pairs={{0,8},{1,9},{2,10},{3,11},{4,12},{5,13},{6,14},{7,15},{8,0},{9,1},... | collective-permute-start | bytes 98312 | tf_op jit(solution)/shard_map/ppermute | solution.py:555
  124.5 5.1 %collective-permute-start.15 = (f32[32,32,256]{2,1,0:T(8,128)S(1)}, f32[32,32,256]{2,1,0:T(8,128)S(1)}, u32[]{:S(2)}, u32[]{:S(2)}) collective-permute-start(f32[32,32,256]{2,1,0:T(8,128)S(1)} %all_to_all.10), channel_id=1, source_target_pairs={{0,1},{1,0},{2,3},{3,2},{4,5},{5,4},{6,7},{7,6},{8,9},{9,8},{10,11... | collective-permute-start | bytes 3145736 | tf_op jit(solution)/shard_map/ppermute | solution.py:496

commit v6 on v3

--- a/solution.py
+++ b/solution.py
@@ -10,6 +10,7 @@
 FRESNEL = 0.5
 BF, F32 = jnp.bfloat16, jnp.float32
 FOUR, FOUR_CONJ, PROP, PROP_CONJ = 0, 1, 2, 3
+STAGGER = 1
 VMEM = pl.BlockSpec(memory_space=pltpu.VMEM)
 SMEM = pl.BlockSpec(memory_space=pltpu.SMEM)
 ANY = pl.BlockSpec(memory_space=pl.ANY)
@@ -85,47 +86,66 @@
     ]
 
 
-def sandwich(fields, which, tables, lhs_high, lhs_low, rhs_high, rhs_low):
+def sandwich(field, which, at, tables, lhs_high, lhs_low, rhs_high, rhs_low):
     n = tables.shape[-1]
     h = n // 2
-    for at, field in enumerate(fields):
-        for part in range(2):
-            first, second = field[part][:, :h], field[part][:, h:]
-            for parity, value in enumerate((first + second, first - second)):
-                high, low = halves(value)
-                lhs_high[parity, at * n : (at + 1) * n, part * h : (part + 1) * h] = high
-                lhs_low[parity, at * n : (at + 1) * n, part * h : (part + 1) * h] = low
-    for parity in range(2):
-        inner = product(
-            lhs_high[parity], lhs_low[parity], tables[which, parity, 0], tables[which, parity, 1]
+    rows = slice(at * n, (at + 1) * n)
+    for part in range(2):
+        first, second = field[part][:, :h], field[part][:, h:]
+        for parity, value in enumerate((first + second, first - second)):
+            high, low = halves(value)
+            lhs_high[parity, rows, part * h : (part + 1) * h] = high
+            lhs_low[parity, rows, part * h : (part + 1) * h] = low
+    yield
+    inner = [
+        product(
+            lhs_high[parity, rows], lhs_low[parity, rows],
+            tables[which, parity, 0], tables[which, parity, 1],
         )
-        for at in range(len(fields)):
-            first = inner[at * n : at * n + h]
-            second = inner[at * n + h : (at + 1) * n]
-            cols = slice(at * n + parity * h, at * n + (parity + 1) * h)
-            for turned, value in enumerate((first + second, first - second)):
-                high, low = halves(value)
-                rhs_high[turned, :h, cols] = high[:, :h]
-                rhs_high[turned, h:, cols] = high[:, h:]
-                rhs_low[turned, :h, cols] = low[:, :h]
-                rhs_low[turned, h:, cols] = low[:, h:]
-    even, odd = [
+        for parity in range(2)
+    ]
+    yield
+    for parity, value in enumerate(inner):
+        first, second = value[:h], value[h:]
+        cols = slice(at * n + parity * h, at * n + (parity + 1) * h)
+        for turned, mixed in enumerate((first + second, first - second)):
+            high, low = halves(mixed)
+            rhs_high[turned, :h, cols] = high[:, :h]
+            rhs_high[turned, h:, cols] = high[:, h:]
+            rhs_low[turned, :h, cols] = low[:, :h]
+            rhs_low[turned, h:, cols] = low[:, h:]
+    yield
+    outer = [
         product(
             tables[which ^ 1, turned, 0], tables[which ^ 1, turned, 1],
-            rhs_high[turned], rhs_low[turned],
+            rhs_high[turned, :, rows], rhs_low[turned, :, rows],
         )
         for turned in range(2)
     ]
-    results = []
-    for at in range(len(fields)):
-        pair = []
-        for part in range(2):
-            e = even[part * h : (part + 1) * h, at * n : (at + 1) * n]
-            o = odd[part * h : (part + 1) * h, at * n : (at + 1) * n]
-            value = jnp.concatenate([e + o, e - o], axis=0)
-            first, second = value[:, :h], value[:, h:]
-            pair.append(jnp.concatenate([first + second, first - second], axis=1))
-        results.append(pair)
+    yield
+    pair = []
+    for part in range(2):
+        e = outer[0][part * h : (part + 1) * h]
+        o = outer[1][part * h : (part + 1) * h]
+        value = jnp.concatenate([e + o, e - o], axis=0)
+        first, second = value[:, :h], value[:, h:]
+        pair.append(jnp.concatenate([first + second, first - second], axis=1))
+    return pair
+
+
+def staggered(chains):
+    results = [None] * len(chains)
+    running = set(range(len(chains)))
+    step = 0
+    while running:
+        for at in sorted(running):
+            if step >= at * STAGGER:
+                try:
+                    next(chains[at])
+                except StopIteration as end:
+                    results[at] = end.value
+                    running.discard(at)
+        step += 1
     return results
 
 
@@ -138,7 +158,7 @@
     ]
 
 
-def prepare_kernel(probe_in, blocks, probe, tables):
+def prepare_kernel(probe_in, measured_in, blocks, probe, measured, tables):
     h = blocks.shape[-1]
     for field in range(2):
         for parity in range(2):
@@ -159,28 +179,31 @@
         return carry
 
     lax.fori_loop(0, 2, fold, 0)
-
-
-def prepared(probe, blocks):
+    for at, plane in enumerate(folded([measured_in[at] for at in range(measured.shape[0])])):
+        measured[at] = plane
+
+
+def prepared(probe, measured, blocks):
     n = probe.shape[-1]
     return pl.pallas_call(
         prepare_kernel,
         out_shape=(
             jax.ShapeDtypeStruct(probe.shape, F32),
+            jax.ShapeDtypeStruct(measured.shape, F32),
             jax.ShapeDtypeStruct((4, 2, 2, n, n), BF),
         ),
-        in_specs=[VMEM] * 2,
-        out_specs=(VMEM,) * 2,
+        in_specs=[VMEM] * 3,
+        out_specs=(VMEM,) * 3,
         compiler_params=pltpu.CompilerParams(vmem_limit_bytes=24 << 20),
         cost_estimate=pl.CostEstimate(flops=3 << 30, bytes_accessed=6 << 20, transcendentals=0),
         name="prepare",
-    )(probe, blocks)
+    )(probe, measured, blocks)
 
 
 def forward_kernel(
-    offsets, left, left_edges, middle, middle_edges, right, right_edges, probe, tables, phase,
-    window, moved, far, intensity,
-    lhs_high, lhs_low, rhs_high, rhs_low, wide, sems,
+    left, left_edges, middle, middle_edges, right, right_edges, probe, tables, phase,
+    window, moved, far, intensity, offsets,
+    lhs_high, lhs_low, rhs_high, rhs_low, wide, numbers, sems,
 ):
     n, modes = probe.shape[-1], probe.shape[1]
     rows, tile = wide.shape[2], wide.shape[3] // 3
@@ -188,16 +211,22 @@
     for across, (own, edges) in enumerate(
         ((left, left_edges), (middle, middle_edges), (right, right_edges))
     ):
-        sources = (edges.at[:, :, :tile], own, edges.at[:, :, tile:])
+        sources = (edges.at[:, :, :tile], own, edges.at[:, :, tile + 8 :])
         for down, source in enumerate(sources):
             place = wide.at[
                 :, :, down * tile : (down + 1) * tile, across * tile : (across + 1) * tile
             ]
             pieces.append(pltpu.make_async_copy(source, place, sems.at[len(pieces)]))
+    pieces.append(
+        pltpu.make_async_copy(left_edges.at[:, :, tile : tile + 8], numbers, sems.at[len(pieces)])
+    )
     for piece in pieces:
         piece.start()
     for piece in pieces:
         piece.wait()
+    for position in range(window.shape[0]):
+        for axis in range(2):
+            offsets[position, axis] = numbers[position, axis, 0, 0].astype(jnp.int32)
     buffers = (tables, lhs_high, lhs_low, rhs_high, rhs_low)
 
     def visit(position, carry):
@@ -211,23 +240,22 @@
         window[position, 0, 0], window[position, 1, 0] = planes[0], planes[1]
         window[position, 0, 1] = planes[2] * phase[0] - planes[3] * phase[1]
         window[position, 1, 1] = planes[2] * phase[1] + planes[3] * phase[0]
+
         top_re, top_im = window[position, 0, 0], window[position, 1, 0]
-        fields = []
+        chains = []
         for mode in range(modes):
             probe_re, probe_im = probe[0, mode], probe[1, mode]
-            fields.append(
-                (probe_re * top_re - probe_im * top_im, probe_re * top_im + probe_im * top_re)
-            )
-        fields = sandwich(fields, PROP, *buffers)
+            field = (probe_re * top_re - probe_im * top_im, probe_re * top_im + probe_im * top_re)
+            chains.append(sandwich(field, PROP, mode, *buffers))
         low_re, low_im = window[position, 0, 1], window[position, 1, 1]
-        exits = []
-        for mode, (re, im) in enumerate(fields):
+        following = []
+        for mode, (re, im) in enumerate(staggered(chains)):
             moved[position, 0, mode] = re
             moved[position, 1, mode] = im
-            exits.append((re * low_re - im * low_im, re * low_im + im * low_re))
-        fields = sandwich(exits, FOUR, *buffers)
+            field = (re * low_re - im * low_im, re * low_im + im * low_re)
+            following.append(sandwich(field, FOUR, mode, *buffers))
         total = jnp.zeros((n, n), F32)
-        for mode, (re, im) in enumerate(fields):
+        for mode, (re, im) in enumerate(staggered(following)):
             far[position, 0, mode] = re
             far[position, 1, mode] = im
             total = total + (re * re + im * im)
@@ -237,7 +265,7 @@
     lax.fori_loop(0, window.shape[0], visit, 0)
 
 
-def forward(count, offsets, tiles, probe, tables, phase):
+def forward(count, tiles, probe, tables, phase):
     n, modes = probe.shape[-1], probe.shape[1]
     tile = tiles[0].shape[-1]
     fields = jax.ShapeDtypeStruct((count,) + probe.shape, F32)
@@ -248,69 +276,64 @@
             fields,
             fields,
             jax.ShapeDtypeStruct((count, n, n), F32),
+            jax.ShapeDtypeStruct((count, 2), jnp.int32),
         ),
-        in_specs=[SMEM] + [ANY] * 6 + [VMEM] * 3,
-        out_specs=(VMEM,) * 4,
+        in_specs=[ANY] * 6 + [VMEM] * 3,
+        out_specs=(VMEM,) * 4 + (SMEM,),
         scratch_shapes=sandwich_scratch(n, modes)
-        + [pltpu.VMEM((2, 2, 3 * tile, 3 * tile), F32), pltpu.SemaphoreType.DMA((9,))],
+        + [
+            pltpu.VMEM((2, 2, 3 * tile, 3 * tile), F32),
+            pltpu.SMEM((2, 2, 8, tile), F32),
+            pltpu.SemaphoreType.DMA((10,)),
+        ],
         compiler_params=pltpu.CompilerParams(vmem_limit_bytes=SCOPED_F << 20),
         cost_estimate=pl.CostEstimate(
             flops=count * modes * 8 * 12 * n**3, bytes_accessed=18 << 20, transcendentals=0
         ),
         name="forward",
-    )(offsets, *tiles, probe, tables, phase)
+    )(*tiles, probe, tables, phase)
 
 
 def backward_kernel(
     core, window, moved, far, intensity, measured, probe, tables, phase,
     totals, kept, sent,
-    lhs_high, lhs_low, rhs_high, rhs_low, probe_grad, amplitude, sems,
+    lhs_high, lhs_low, rhs_high, rhs_low, probe_grad, sems,
 ):
     n, modes = probe.shape[-1], probe.shape[1]
     buffers = (tables, lhs_high, lhs_low, rhs_high, rhs_low)
-    count = measured.shape[0]
-    for at, plane in enumerate(folded([measured[at] for at in range(count)])):
-        amplitude[at] = plane
 
     def visit(position, carry):
-        scaling = 1.0 - amplitude[position] / jnp.sqrt(intensity[position] + 1.0)
-        fields = [
-            (scaling * far[position, 0, mode], scaling * far[position, 1, mode])
-            for mode in range(modes)
-        ]
-        fields = sandwich(fields, FOUR_CONJ, *buffers)
-        low_re, low_im = window[position, 0, 1], window[position, 1, 1]
-        total_re = total_im = jnp.zeros((n, n), F32)
-        behinds = []
-        for mode, (re, im) in enumerate(fields):
+        scaling = 1.0 - measured[position] / jnp.sqrt(intensity[position] + 1.0)
+
+        def chain(mode):
+            field = (scaling * far[position, 0, mode], scaling * far[position, 1, mode])
+            re, im = yield from sandwich(field, FOUR_CONJ, mode, *buffers)
             moved_re, moved_im = moved[position, 0, mode], moved[position, 1, mode]
-            total_re = total_re + (moved_re * re + moved_im * im)
-            total_im = total_im + (moved_re * im - moved_im * re)
-            behinds.append((low_re * re + low_im * im, low_re * im - low_im * re))
-        totals[position, 0, 1] = total_re * phase[0] + total_im * phase[1]
-        totals[position, 1, 1] = total_im * phase[0] - total_re * phase[1]
-        fields = sandwich(behinds, PROP_CONJ, *buffers)
-        top_re, top_im = window[position, 0, 0], window[position, 1, 0]
-        total_re = total_im = jnp.zeros((n, n), F32)
-        for mode, (re, im) in enumerate(fields):
+            low_terms = (moved_re * re + moved_im * im, moved_re * im - moved_im * re)
+            for part in range(2):
+                if mode == 0:
+                    totals[position, part, 1] = low_terms[part]
+                else:
+                    totals[position, part, 1] += low_terms[part]
+            low_re, low_im = window[position, 0, 1], window[position, 1, 1]
+            field = (low_re * re + low_im * im, low_re * im - low_im * re)
+            re, im = yield from sandwich(field, PROP_CONJ, mode, *buffers)
             probe_re, probe_im = probe[0, mode], probe[1, mode]
-            total_re = total_re + (probe_re * re + probe_im * im)
-            total_im = total_im + (probe_re * im - probe_im * re)
-            term_re = top_re * re + top_im * im
-            term_im = top_re * im - top_im * re
-
-            @pl.when(position == 0)
-            def _():
-                probe_grad[0, mode] = term_re
-                probe_grad[1, mode] = term_im
-
-            @pl.when(position != 0)
-            def _():
-                probe_grad[0, mode] += term_re
-                probe_grad[1, mode] += term_im
-
-        totals[position, 0, 0] = total_re
-        totals[position, 1, 0] = total_im
+            top_terms = (probe_re * re + probe_im * im, probe_re * im - probe_im * re)
+            top_re, top_im = window[position, 0, 0], window[position, 1, 0]
+            terms = (top_re * re + top_im * im, top_re * im - top_im * re)
+            for part in range(2):
+                if mode == 0:
+                    totals[position, part, 0] = top_terms[part]
+                else:
+                    totals[position, part, 0] += top_terms[part]
+                before = jnp.where(position == 0, 0.0, probe_grad[part, mode])
+                probe_grad[part, mode] = before + terms[part]
+
+        staggered([chain(mode) for mode in range(modes)])
+        low_re, low_im = totals[position, 0, 1], totals[position, 1, 1]
+        totals[position, 0, 1] = low_re * phase[0] + low_im * phase[1]
+        totals[position, 1, 1] = low_im * phase[0] - low_re * phase[1]
         return carry
 
     lax.fori_loop(0, window.shape[0], visit, 0)
@@ -344,7 +367,6 @@
         scratch_shapes=sandwich_scratch(n, modes)
         + [
             pltpu.VMEM(probe.shape, F32),
-            pltpu.VMEM(measured.shape, F32),
             pltpu.SemaphoreType.DMA((2,)),
         ],
         compiler_params=pltpu.CompilerParams(vmem_limit_bytes=SCOPED_B << 20),
@@ -437,22 +459,23 @@
         for t in range(tiles)
     ]
     corner = jnp.stack([lax.axis_index("strip"), lax.axis_index("tile")]).astype(jnp.int32) * tile
-    wrap = jnp.array([strips * tile, tiles * tile], jnp.int32)
-    scalars = lax.ppermute((offsets - corner) % wrap, both, diagonal)
-    above = around(object_field, "strip", 1)
+    local = (offsets - corner).astype(F32)[:, :, None, None]
+    sent_down = jnp.concatenate(
+        [object_field, jnp.broadcast_to(local, local.shape[:2] + (8, tile))], axis=2
+    )
+    above = around(sent_down, "strip", 1)
     below = around(object_field, "strip", -1)
     left = around(object_field, "tile", 1)
     right = around(object_field, "tile", -1)
-    above, below, left, right, scalars, measured = lax.optimization_barrier(
-        (above, below, left, right, scalars, measured)
-    )
-    probe, tables = prepared(probe_modes, jnp.asarray(blocks))
+    probe, measured, tables = prepared(probe_modes, measured, jnp.asarray(blocks))
+    above, below, left, right = lax.optimization_barrier((above, below, left, right))
     edges = jnp.concatenate([above, below], axis=2)
     left_edges = around(edges, "tile", 1)
     right_edges = around(edges, "tile", -1)
+    edges, measured = lax.optimization_barrier((edges, measured))
     measured = lax.ppermute(measured, both, diagonal)
     pieces = (left, left_edges, object_field, edges, right, right_edges)
-    state = forward(measured.shape[0], scalars, pieces, probe, tables, phase)
+    *state, scalars = forward(measured.shape[0], pieces, probe, tables, phase)
     core = (lax.axis_index("tile") % 2).astype(jnp.int32)
     totals, kept, sent = backward(core.reshape(1), state, measured, probe, tables, phase)
 
@@ -475,7 +498,7 @@
     upper, lower = column[:, :, :tile], column[:, :, 2 * tile :]
     from_below = around(upper, "strip", -1)
     from_above = around(lower, "strip", 1)
-    shares, from_below, from_above = lax.optimization_barrier((shares, from_below, from_above))
+    shares, column, upper, lower = lax.optimization_barrier((shares, column, upper, lower))
 
     def across(value, distance):
         step = [
@@ -489,6 +512,7 @@
         lax.dynamic_index_in_dim(shares, 1 - mine, 0, False), 1
     )
     distance = pairs
+    share, from_below, from_above = lax.optimization_barrier((share, from_below, from_above))
     while distance < levels:
         share = share + across(share, distance)
         distance *= 2

time: 139 us -> 132 us (0.950)
  waiting for transfers between devices: 42.7 us -> 33.2 us
  Pallas kernels: 35.9 us -> 33 us
  blocking collectives: 19.5 us -> 21.5 us
  starting transfers between devices: 31 us -> 32.7 us
    ppermute x1 -> x0, waiting for transfers between devices: 9.85 us -> none  [per_device(): scalars = lax.ppermute((offsets - corner) % wrap, both, diagonal)]
    ppermute x1, waiting for transfers between devices: 0.01 us -> 3.24 us  [per_device(): measured = lax.ppermute(measured, both, diagonal)]
    ppermute x2, starting transfers between devices: 8.74 us -> 5.74 us  [swapped(): lax.ppermute(value, 'tile', [(at, at ^ 1) for at in range(lax.axis_size('...]
    ppermute x3, starting transfers between devices: 1.72 us -> 4.64 us  [across(): return lax.ppermute(value, 'tile', step)]
    pallas_call x1, Pallas kernels: 15.8 us -> 13.4 us  [backward(): pl.pallas_call(backward_kernel, out_shape=(jax.ShapeDtypeStruct((count, 2...]
    ppermute x3, waiting for transfers between devices: 11.5 us -> 9.18 us  [across(): return lax.ppermute(value, 'tile', step)]
    all_to_all x1, blocking collectives: 19.5 us -> 21.5 us  [exchanged(): lax.all_to_all(value, axis, 0, 0, tiled=True, axis_index_groups=groups)]
    all_to_all x1, waiting for transfers between devices: 6.87 us -> 5.28 us  [exchanged(): lax.all_to_all(value, axis, 0, 0, tiled=True, axis_index_groups=groups)]
  transfers between devices with their start and end apart: 18 -> 17, of which waited for: 10 -> 11; matrix products, arithmetic and copies ran while one was open for 3% -> 3% of each run, Pallas kernels for 14% -> 15%
where the time goes in v6:
time: 132 us
  waiting for transfers between devices  33.2 us (25%)
  Pallas kernels  33 us (25%)
  starting transfers between devices  32.7 us (25%)
  blocking collectives  21.5 us (16%)
  other arithmetic  6.74 us (5%)
  local copies, waits for them, and re-layouts  3.95 us (3%)
    all_to_all x1, blocking collectives, exchanged(): lax.all_to_all(value, axis, 0, 0, tiled=True, axis_index_groups=groups)  21.5 us
    ppermute x10, starting transfers between devices, around(): lax.ppermute(value, axis, [(at, (at + steps) % count) for at in range(cou...  17.2 us
    pallas_call x1, Pallas kernels, forward(): pl.pallas_call(forward_kernel, out_shape=(jax.ShapeDtypeStruct((count, 2,...  14.2 us
    ppermute x10, waiting for transfers between devices, around(): lax.ppermute(value, axis, [(at, (at + steps) % count) for at in range(cou...  14 us
    pallas_call x1, Pallas kernels, backward(): pl.pallas_call(backward_kernel, out_shape=(jax.ShapeDtypeStruct((count, 2...  13.4 us
    ppermute x3, waiting for transfers between devices, across(): return lax.ppermute(value, 'tile', step)  9.18 us
    ppermute x2, starting transfers between devices, swapped(): lax.ppermute(value, 'tile', [(at, at ^ 1) for at in range(lax.axis_size('...  5.74 us
    all_to_all x1, waiting for transfers between devices, exchanged(): lax.all_to_all(value, axis, 0, 0, tiled=True, axis_index_groups=groups)  5.28 us
  transfers between devices with their start and end apart: 17, of which 11 were waited for; matrix products, arithmetic and copies ran while one was open for 3% of the time, Pallas kernels for 15%

profile of v6, /device:TPU:1, one launch (start us, length us, event | category | flops | bytes accessed | tf_op | source)
XLA Modules:
  0.0 131.9 jit_solution(9870593453445510208)
XLA Ops:
  2.4 2.2 %collective-permute-start = (f32[2,2,136,128]{3,2,1,0:T(8,128)S(1)}, f32[2,2,136,128]{3,2,1,0:T(8,128)S(1)}, u32[]{:S(2)}, u32[]{:S(2)}) collective-permute-start(f32[2,2,136,128]{3,2,1,0:T(8,128)S(1)} %pad_maximum_fusion), channel_id=1, source_target_pairs={{0,16},{16,32},{32,48},{48,64},{64,80},{80,96},{96,112},{112,128},... | collective-permute-start | bytes 835592 | tf_op jit(solution)/shard_map/ppermute | solution.py:434
  4.6 2.5 %collective-permute-start.2 = (f32[2,2,128,128]{3,2,1,0:T(8,128)}, f32[2,2,128,128]{3,2,1,0:T(8,128)S(1)}, u32[]{:S(2)}, u32[]{:S(2)}) collective-permute-start(f32[2,2,128,128]{3,2,1,0:T(8,128)} %middle.1), channel_id=1, source_target_pairs={{0,1},{1,2},{2,3},{3,4},{4,5},{5,6},{6,7},{7,8},{8,9},{9,10},{10,1... | collective-permute-start | bytes 786440 | tf_op jit(solution)/shard_map/ppermute | solution.py:434
  7.1 3.5 %collective-permute-start.1 = (f32[2,2,128,128]{3,2,1,0:T(8,128)}, f32[2,2,128,128]{3,2,1,0:T(8,128)S(1)}, u32[]{:S(2)}, u32[]{:S(2)}) collective-permute-start(f32[2,2,128,128]{3,2,1,0:T(8,128)} %middle.1), channel_id=1, source_target_pairs={{0,240},{16,0},{32,16},{48,32},{64,48},{80,64},{96,80},{112,96},{1... | collective-permute-start | bytes 786440 | tf_op jit(solution)/shard_map/ppermute | solution.py:434
  11.1 5.3 %collective-permute-done.1 = f32[2,2,128,128]{3,2,1,0:T(8,128)S(1)} collective-permute-done((f32[2,2,128,128]{3,2,1,0:T(8,128)}, f32[2,2,128,128]{3,2,1,0:T(8,128)S(1)}, u32[]{:S(2)}, u32[]{:S(2)}) %collective-permute-start.1) | collective-permute-done | bytes 262176 | tf_op jit(solution)/shard_map/ppermute | solution.py:434
  16.7 2.0 %collective-permute-start.5 = (f32[2,2,264,128]{3,2,1,0:T(8,128)S(1)}, f32[2,2,264,128]{3,2,1,0:T(8,128)S(1)}, u32[]{:S(2)}, u32[]{:S(2)}) collective-permute-start(f32[2,2,264,128]{3,2,1,0:T(8,128)S(1)} %constant_dynamic-update-slice_fusion.middle_edges), channel_id=1, source_target_pairs={{0,15},{1,0},{2,1},{3,2},{4,3},{5,4},{6,5},{7,6},{8,7},{9,8},{10,9... | collective-permute-start | bytes 1622024 | tf_op jit(solution)/shard_map/ppermute | solution.py:434
  22.3 1.8 %prepare.1 = (f32[2,4,256,256]{3,2,1,0:T(8,128)S(1)}, f32[2,256,256]{2,1,0:T(8,128)S(1)}, bf16[4,2,2,256,256]{4,3,2,1,0:T(8,128)(2,1)S(1)}) custom-call(f32[2,4,256,256]{3,2,1,0:T(8,128)S(1)} %copy-done.1, f32[2,256,256]{2,1,0:T(8,128)S(1)} %copy-done.2, bf16[2,2,2,2,128,128]{5,4,3,2,1,0:T(8,128)(2,1)S(1)} %copy-done.4), custom_call_target="tpu_custom_call" | custom-call | flops 3221225472 | bytes 6291456 | tf_op jit(solution)/shard_map/prepare/pallas_call | solution.py:188
  25.8 14.2 %forward.1 = (f32[2,2,2,256,256]{4,3,2,1,0:T(8,128)S(1)}, f32[2,2,4,256,256]{4,3,2,1,0:T(8,128)S(1)}, f32[2,2,4,256,256]{4,3,2,1,0:T(8,128)S(1)}, f32[2,256,256]{2,1,0:T(8,128)S(1)}, s32[2,2]{1,0:T(2,128)S(1)}) custom-call(f32[2,2,128,128]{3,2,1,0:T(8,128)S(1)} %collective-permute-done.2.left, f32[2,2,264,128]{3,2,1,0:T(8,128)S(1)} %collective-permute-done.4.left_edges, ...), custom_call_target="tpu_custom_call" | custom-call | flops 12884901888 | bytes 18874368 | tf_op jit(solution)/shard_map/forward/pallas_call | solution.py:272
  40.0 3.2 %collective-permute-done.6.measured = f32[2,256,256]{2,1,0:T(8,128)S(1)} collective-permute-done((f32[2,256,256]{2,1,0:T(8,128)S(1)}, f32[2,256,256]{2,1,0:T(8,128)S(1)}, u32[]{:S(2)}, u32[]{:S(2)}) %collective-permute-start.6) | collective-permute-done | bytes 524320 | tf_op jit(solution)/shard_map/ppermute | solution.py:476
  43.2 13.4 %backward.1 = (f32[2,2,2,256,256]{4,3,2,1,0:T(8,128)S(1)}, f32[4,256,256]{2,1,0:T(8,128)S(1)}, f32[4,256,256]{2,1,0:T(8,128)S(1)}) custom-call(s32[1]{0:T(128)} %bitcast.core, f32[2,2,2,256,256]{4,3,2,1,0:T(8,128)S(1)} %get-tuple-element.39.window, f32[2,2,4,256,256]{4,3,2,1,0:T(8,128)S(1)} %get-tuple-element.40.moved, ...), custom_call_target="tpu_custom_call" | custom-call | flops 12884901888 | bytes 18874368 | tf_op jit(solution)/shard_map/backward/pallas_call | solution.py:362
  56.6 2.9 %collective-permute-start.7 = (f32[4,256,256]{2,1,0:T(8,128)S(1)}, f32[4,256,256]{2,1,0:T(8,128)S(1)}, u32[]{:S(2)}, u32[]{:S(2)}) collective-permute-start(f32[4,256,256]{2,1,0:T(8,128)S(1)} %get-tuple-element.45), channel_id=1, source_target_pairs={{0,1},{1,0},{2,3},{3,2},{4,5},{5,4},{6,7},{7,6},{8,9},{9,8},{10,11... | collective-permute-start | bytes 3145736 | tf_op jit(solution)/shard_map/ppermute | solution.py:446
  59.5 3.6 %place.1 = (f32[2,2,384,128]{3,2,1,0:T(8,128)S(1)}, f32[2,2,384,128]{3,2,1,0:T(8,128)S(1)}, f32[2,2,384,128]{3,2,1,0:T(8,128)S(1)}) custom-call(s32[2,2]{1,0:T(2,128)S(1)} %get-tuple-element.46.scalars, f32[2,2,2,256,256]{4,3,2,1,0:T(8,128)S(1)} %get-tuple-element.47.totals), custom_call_target="tpu_custom_call" | custom-call | flops 2147483648 | bytes 8388608 | tf_op jit(solution)/shard_map/place/pallas_call | solution.py:417
  63.2 1.7 %collective-permute-start.9 = (f32[2,2,384,128]{3,2,1,0:T(8,128)S(1)}, f32[2,2,384,128]{3,2,1,0:T(8,128)}, u32[]{:S(2)}, u32[]{:S(2)}) collective-permute-start(f32[2,2,384,128]{3,2,1,0:T(8,128)S(1)} %get-tuple-element.54), channel_id=1, source_target_pairs={{0,1},{1,2},{2,3},{3,4},{4,5},{5,6},{6,7},{7,8},{8,9},{9,10},{10,1... | collective-permute-start | bytes 2359304 | tf_op jit(solution)/shard_map/ppermute | solution.py:434
  66.1 4.8 %all-to-all-start = ((f32[16,64,256]{2,1,0:T(8,128)}), f32[16,64,256]{2,1,0:T(8,128)S(1)}, u32[]{:S(2)}, u32[]{:S(2)}) async-start(f32[16,64,256]{2,1,0:T(8,128)} %bitcast.3), calls=%async_computation | async-start | bytes 2097152 | tf_op jit(solution)/shard_map/all_to_all | solution.py:438
  70.9 4.1 %collective-permute-done.8 = f32[2,2,384,128]{3,2,1,0:T(8,128)} collective-permute-done((f32[2,2,384,128]{3,2,1,0:T(8,128)S(1)}, f32[2,2,384,128]{3,2,1,0:T(8,128)}, u32[]{:S(2)}, u32[]{:S(2)}) %collective-permute-start.8) | collective-permute-done | bytes 786464 | tf_op jit(solution)/shard_map/ppermute | solution.py:434
  76.6 4.8 %collective-permute-start.11 = (f32[2,2,128,128]{3,2,1,0:T(8,128)S(1)}, f32[2,2,128,128]{3,2,1,0:T(8,128)S(1)}, u32[]{:S(2)}, u32[]{:S(2)}) collective-permute-start(f32[2,2,128,128]{3,2,1,0:T(8,128)S(1)} %get-tuple-element.61), channel_id=1, source_target_pairs={{0,240},{16,0},{32,16},{48,32},{64,48},{80,64},{96,80},{112,96},{1... | collective-permute-start | bytes 786440 | tf_op jit(solution)/shard_map/ppermute | solution.py:434
  81.4 5.3 %all-to-all-done = f32[16,64,256]{2,1,0:T(8,128)S(1)} async-done(((f32[16,64,256]{2,1,0:T(8,128)}), f32[16,64,256]{2,1,0:T(8,128)S(1)}, u32[]{:S(2)}, u32[]{:S(2)}) %all-to-all-start) | async-done | bytes 1048608 | tf_op jit(solution)/shard_map/all_to_all | solution.py:438
  86.9 3.0 %collective-permute-done.10 = f32[32,256]{1,0:T(8,128)S(1)} collective-permute-done((f32[32,256]{1,0:T(8,128)S(1)}, f32[32,256]{1,0:T(8,128)S(1)}, u32[]{:S(2)}, u32[]{:S(2)}) %collective-permute-start.10) | collective-permute-done | bytes 32800 | tf_op jit(solution)/shard_map/ppermute | solution.py:507
  89.9 3.0 %collective-permute-done.12 = f32[2,2,128,128]{3,2,1,0:T(8,128)S(1)} collective-permute-done((f32[2,2,128,128]{3,2,1,0:T(8,128)S(1)}, f32[2,2,128,128]{3,2,1,0:T(8,128)S(1)}, u32[]{:S(2)}, u32[]{:S(2)}) %collective-permute-start.12) | collective-permute-done | bytes 262176 | tf_op jit(solution)/shard_map/ppermute | solution.py:434
  93.0 3.9 %collective-permute-done.13 = f32[32,256]{1,0:T(8,128)S(1)} collective-permute-done((f32[32,256]{1,0:T(8,128)S(1)}, f32[32,256]{1,0:T(8,128)S(1)}, u32[]{:S(2)}, u32[]{:S(2)}) %collective-permute-start.13) | collective-permute-done | bytes 32800 | tf_op jit(solution)/shard_map/ppermute | solution.py:507
  96.9 4.4 %collective-permute-start.14 = (f32[32,256]{1,0:T(8,128)S(1)}, f32[32,256]{1,0:T(8,128)S(1)}, u32[]{:S(2)}, u32[]{:S(2)}) collective-permute-start(f32[32,256]{1,0:T(8,128)S(1)} %add.51), channel_id=1, source_target_pairs={{0,8},{1,9},{2,10},{3,11},{4,12},{5,13},{6,14},{7,15},{8,0},{9,1},... | collective-permute-start | bytes 98312 | tf_op jit(solution)/shard_map/ppermute | solution.py:507
  101.4 2.2 %collective-permute-done.14 = f32[32,256]{1,0:T(8,128)S(1)} collective-permute-done((f32[32,256]{1,0:T(8,128)S(1)}, f32[32,256]{1,0:T(8,128)S(1)}, u32[]{:S(2)}, u32[]{:S(2)}) %collective-permute-start.14) | collective-permute-done | bytes 32800 | tf_op jit(solution)/shard_map/ppermute | solution.py:507
  103.7 21.5 %all_to_all.10 = f32[32,32,256]{2,1,0:T(8,128)S(1)} all-to-all(f32[32,32,256]{2,1,0:T(8,128)S(1)} %broadcast_in_dim.45), channel_id=1, replica_groups={{0,2,16,18,32,34,48,50,64,66,80,82,96,98,112,114,128,130,144,146,160,16..., dimensions={0} | all-to-all | bytes 2097152 | tf_op jit(solution)/shard_map/all_to_all | solution.py:438
  125.2 2.8 %collective-permute-start.15 = (f32[32,32,256]{2,1,0:T(8,128)S(1)}, f32[32,32,256]{2,1,0:T(8,128)S(1)}, u32[]{:S(2)}, u32[]{:S(2)}) collective-permute-start(f32[32,32,256]{2,1,0:T(8,128)S(1)} %all_to_all.10), channel_id=1, source_target_pairs={{0,1},{1,0},{2,3},{3,2},{4,5},{5,4},{6,7},{7,6},{8,9},{9,8},{10,11... | collective-permute-start | bytes 3145736 | tf_op jit(solution)/shard_map/ppermute | solution.py:446
  130.3 1.6 %broadcast_select_fusion = f32[2,4,256,256]{3,2,1,0:T(8,128)} fusion(f32[4,256,256]{2,1,0:T(8,128)S(1)} %bitcast.12, f32[4,256,256]{2,1,0:T(8,128)S(1)} %bitcast.11, pred[2]{0:T(512)(128)(4,1)S(1)} %iota_compare_fusion), kind=kLoop, calls=%fused_computation | loop fusion | flops 524288 | bytes 4194306 | tf_op jit(solution)/shard_map/jit(_where)/select_n | solution.py:523
  (43 shorter events, 13.3 us)
Async XLA Ops:
  2.4 14.2 %collective-permute-start = (f32[2,2,136,128]{3,2,1,0:T(8,128)S(1)}, f32[2,2,136,128]{3,2,1,0:T(8,128)S(1)}, u32[]{:S(2)}, u32[]{:S(2)}) collective-permute-start(f32[2,2,136,128]{3,2,1,0:T(8,128)S(1)} %pad_maximum_fusion), channel_id=1, source_target_pairs={{0,16},{16,32},{32,48},{48,64},{64,80},{80,96},{96,112},{112,128},... | collective-permute-start | bytes 835592 | tf_op jit(solution)/shard_map/ppermute | solution.py:434
  4.6 6.5 %collective-permute-start.2 = (f32[2,2,128,128]{3,2,1,0:T(8,128)}, f32[2,2,128,128]{3,2,1,0:T(8,128)S(1)}, u32[]{:S(2)}, u32[]{:S(2)}) collective-permute-start(f32[2,2,128,128]{3,2,1,0:T(8,128)} %middle.1), channel_id=1, source_target_pairs={{0,1},{1,2},{2,3},{3,4},{4,5},{5,6},{6,7},{7,8},{8,9},{9,10},{10,1... | collective-permute-start | bytes 786440 | tf_op jit(solution)/shard_map/ppermute | solution.py:434
  7.1 9.3 %collective-permute-start.1 = (f32[2,2,128,128]{3,2,1,0:T(8,128)}, f32[2,2,128,128]{3,2,1,0:T(8,128)S(1)}, u32[]{:S(2)}, u32[]{:S(2)}) collective-permute-start(f32[2,2,128,128]{3,2,1,0:T(8,128)} %middle.1), channel_id=1, source_target_pairs={{0,240},{16,0},{32,16},{48,32},{64,48},{80,64},{96,80},{112,96},{1... | collective-permute-start | bytes 786440 | tf_op jit(solution)/shard_map/ppermute | solution.py:434
  10.6 6.0 %collective-permute-start.3 = (f32[2,2,128,128]{3,2,1,0:T(8,128)}, f32[2,2,128,128]{3,2,1,0:T(8,128)S(1)}, u32[]{:S(2)}, u32[]{:S(2)}) collective-permute-start(f32[2,2,128,128]{3,2,1,0:T(8,128)} %middle.1), channel_id=1, source_target_pairs={{0,15},{1,0},{2,1},{3,2},{4,3},{5,4},{6,5},{7,6},{8,7},{9,8},{10,9... | collective-permute-start | bytes 786440 | tf_op jit(solution)/shard_map/ppermute | solution.py:434
  16.7 9.1 %collective-permute-start.5 = (f32[2,2,264,128]{3,2,1,0:T(8,128)S(1)}, f32[2,2,264,128]{3,2,1,0:T(8,128)S(1)}, u32[]{:S(2)}, u32[]{:S(2)}) collective-permute-start(f32[2,2,264,128]{3,2,1,0:T(8,128)S(1)} %constant_dynamic-update-slice_fusion.middle_edges), channel_id=1, source_target_pairs={{0,15},{1,0},{2,1},{3,2},{4,3},{5,4},{6,5},{7,6},{8,7},{9,8},{10,9... | collective-permute-start | bytes 1622024 | tf_op jit(solution)/shard_map/ppermute | solution.py:434
  18.6 7.1 %collective-permute-start.4 = (f32[2,2,264,128]{3,2,1,0:T(8,128)S(1)}, f32[2,2,264,128]{3,2,1,0:T(8,128)S(1)}, u32[]{:S(2)}, u32[]{:S(2)}) collective-permute-start(f32[2,2,264,128]{3,2,1,0:T(8,128)S(1)} %constant_dynamic-update-slice_fusion.middle_edges), channel_id=1, source_target_pairs={{0,1},{1,2},{2,3},{3,4},{4,5},{5,6},{6,7},{7,8},{8,9},{9,10},{10,1... | collective-permute-start | bytes 1622024 | tf_op jit(solution)/shard_map/ppermute | solution.py:434
  18.6 1.6 %copy-start.1 = (f32[2,4,256,256]{3,2,1,0:T(8,128)S(1)}, f32[2,4,256,256]{3,2,1,0:T(8,128)}, u32[]{:S(2)}) copy-start(f32[2,4,256,256]{3,2,1,0:T(8,128)} %probe_in.1) | copy-start | bytes 6291460
  20.2 1.0 copy-start.2
  21.3 1.0 copy-start.4
  22.3 3.5 %copy-start = (f32[2,2,128,128]{3,2,1,0:T(8,128)S(1)}, f32[2,2,128,128]{3,2,1,0:T(8,128)}, u32[]{:S(2)}) copy-start(f32[2,2,128,128]{3,2,1,0:T(8,128)} %middle.1) | copy-start | bytes 786436
  22.3 3.5 %copy-start.3 = (f32[2,256,256]{2,1,0:T(8,128)S(1)}, f32[2,256,256]{2,1,0:T(8,128)}, u32[]{:S(2)}) copy-start(f32[2,256,256]{2,1,0:T(8,128)} %constant.54.clone.phase) | copy-start | bytes 1572868
  24.1 19.1 %collective-permute-start.6 = (f32[2,256,256]{2,1,0:T(8,128)S(1)}, f32[2,256,256]{2,1,0:T(8,128)S(1)}, u32[]{:S(2)}, u32[]{:S(2)}) collective-permute-start(f32[2,256,256]{2,1,0:T(8,128)S(1)} %get-tuple-element.43), channel_id=1, source_target_pairs={{0,17},{1,18},{2,19},{3,20},{4,21},{5,22},{6,23},{7,24},{8,25},{9,... | collective-permute-start | bytes 1572872 | tf_op jit(solution)/shard_map/ppermute | solution.py:476
  56.6 6.6 %collective-permute-start.7 = (f32[4,256,256]{2,1,0:T(8,128)S(1)}, f32[4,256,256]{2,1,0:T(8,128)S(1)}, u32[]{:S(2)}, u32[]{:S(2)}) collective-permute-start(f32[4,256,256]{2,1,0:T(8,128)S(1)} %get-tuple-element.45), channel_id=1, source_target_pairs={{0,1},{1,0},{2,3},{3,2},{4,5},{5,4},{6,7},{7,6},{8,9},{9,8},{10,11... | collective-permute-start | bytes 3145736 | tf_op jit(solution)/shard_map/ppermute | solution.py:446
  63.2 11.8 %collective-permute-start.8 = (f32[2,2,384,128]{3,2,1,0:T(8,128)S(1)}, f32[2,2,384,128]{3,2,1,0:T(8,128)}, u32[]{:S(2)}, u32[]{:S(2)}) collective-permute-start(f32[2,2,384,128]{3,2,1,0:T(8,128)S(1)} %get-tuple-element.53), channel_id=1, source_target_pairs={{0,15},{1,0},{2,1},{3,2},{4,3},{5,4},{6,5},{7,6},{8,7},{9,8},{10,9... | collective-permute-start | bytes 2359304 | tf_op jit(solution)/shard_map/ppermute | solution.py:434
  63.2 11.8 %collective-permute-start.9 = (f32[2,2,384,128]{3,2,1,0:T(8,128)S(1)}, f32[2,2,384,128]{3,2,1,0:T(8,128)}, u32[]{:S(2)}, u32[]{:S(2)}) collective-permute-start(f32[2,2,384,128]{3,2,1,0:T(8,128)S(1)} %get-tuple-element.54), channel_id=1, source_target_pairs={{0,1},{1,2},{2,3},{3,4},{4,5},{5,6},{6,7},{7,8},{8,9},{9,10},{10,1... | collective-permute-start | bytes 2359304 | tf_op jit(solution)/shard_map/ppermute | solution.py:434
  66.1 20.6 %all-to-all-start = ((f32[16,64,256]{2,1,0:T(8,128)}), f32[16,64,256]{2,1,0:T(8,128)S(1)}, u32[]{:S(2)}, u32[]{:S(2)}) async-start(f32[16,64,256]{2,1,0:T(8,128)} %bitcast.3), calls=%async_computation | async-start | bytes 2097152 | tf_op jit(solution)/shard_map/all_to_all | solution.py:438
  76.6 16.4 %collective-permute-start.12 = (f32[2,2,128,128]{3,2,1,0:T(8,128)S(1)}, f32[2,2,128,128]{3,2,1,0:T(8,128)S(1)}, u32[]{:S(2)}, u32[]{:S(2)}) collective-permute-start(f32[2,2,128,128]{3,2,1,0:T(8,128)S(1)} %get-tuple-element.60), channel_id=1, source_target_pairs={{0,16},{16,32},{32,48},{48,64},{64,80},{80,96},{96,112},{112,128},... | collective-permute-start | bytes 786440 | tf_op jit(solution)/shard_map/ppermute | solution.py:434
  76.6 16.3 %collective-permute-start.11 = (f32[2,2,128,128]{3,2,1,0:T(8,128)S(1)}, f32[2,2,128,128]{3,2,1,0:T(8,128)S(1)}, u32[]{:S(2)}, u32[]{:S(2)}) collective-permute-start(f32[2,2,128,128]{3,2,1,0:T(8,128)S(1)} %get-tuple-element.61), channel_id=1, source_target_pairs={{0,240},{16,0},{32,16},{48,32},{64,48},{80,64},{96,80},{112,96},{1... | collective-permute-start | bytes 786440 | tf_op jit(solution)/shard_map/ppermute | solution.py:434
  86.8 3.1 %collective-permute-start.10 = (f32[32,256]{1,0:T(8,128)S(1)}, f32[32,256]{1,0:T(8,128)S(1)}, u32[]{:S(2)}, u32[]{:S(2)}) collective-permute-start(f32[32,256]{1,0:T(8,128)S(1)} %dynamic-slice_bitcast_fusion), channel_id=1, source_target_pairs={{0,2},{1,3},{2,0},{3,1},{4,6},{5,7},{6,4},{7,5},{8,10},{9,11},{10,... | collective-permute-start | bytes 98312 | tf_op jit(solution)/shard_map/ppermute | solution.py:507
  92.9 4.0 %collective-permute-start.13 = (f32[32,256]{1,0:T(8,128)S(1)}, f32[32,256]{1,0:T(8,128)S(1)}, u32[]{:S(2)}, u32[]{:S(2)}) collective-permute-start(f32[32,256]{1,0:T(8,128)S(1)} %bitcast_add_fusion), channel_id=1, source_target_pairs={{0,4},{1,5},{2,6},{3,7},{4,0},{5,1},{6,2},{7,3},{8,12},{9,13},{10,... | collective-permute-start | bytes 98312 | tf_op jit(solution)/shard_map/ppermute | solution.py:507
  96.9 6.7 %collective-permute-start.14 = (f32[32,256]{1,0:T(8,128)S(1)}, f32[32,256]{1,0:T(8,128)S(1)}, u32[]{:S(2)}, u32[]{:S(2)}) collective-permute-start(f32[32,256]{1,0:T(8,128)S(1)} %add.51), channel_id=1, source_target_pairs={{0,8},{1,9},{2,10},{3,11},{4,12},{5,13},{6,14},{7,15},{8,0},{9,1},... | collective-permute-start | bytes 98312 | tf_op jit(solution)/shard_map/ppermute | solution.py:507
  125.2 5.1 %collective-permute-start.15 = (f32[32,32,256]{2,1,0:T(8,128)S(1)}, f32[32,32,256]{2,1,0:T(8,128)S(1)}, u32[]{:S(2)}, u32[]{:S(2)}) collective-permute-start(f32[32,32,256]{2,1,0:T(8,128)S(1)} %all_to_all.10), channel_id=1, source_target_pairs={{0,1},{1,0},{2,3},{3,2},{4,5},{5,4},{6,7},{7,6},{8,9},{9,8},{10,11... | collective-permute-start | bytes 3145736 | tf_op jit(solution)/shard_map/ppermute | solution.py:446

commit v7 on v6

--- a/solution.py
+++ b/solution.py
@@ -234,8 +234,8 @@
         planes = []
         for layer in range(2):
             for part in range(2):
-                plane = pltpu.roll(wide[part, layer], 3 * tile - col, 1)[:, :n]
-                planes.append(pltpu.roll(plane, rows - row, 0)[:n])
+                plane = pltpu.roll(wide[part, layer], rows - row, 0)[:n]
+                planes.append(pltpu.roll(plane, 3 * tile - col, 1)[:, :n])
         planes = folded(planes)
         window[position, 0, 0], window[position, 1, 0] = planes[0], planes[1]
         window[position, 0, 1] = planes[2] * phase[0] - planes[3] * phase[1]
@@ -386,10 +386,10 @@
         at = [(part, layer) for layer in range(2) for part in range(2)]
         planes = folded([totals[position, part, layer] for part, layer in at])
         for (part, layer), plane in zip(at, planes):
-            plane = jnp.concatenate([plane, jnp.zeros((rows - n, n), F32)], axis=0)
+            plane = jnp.concatenate([plane, jnp.zeros((n, 3 * tile - n), F32)], axis=1)
+            plane = pltpu.roll(plane, col, 1)
+            plane = jnp.concatenate([plane, jnp.zeros((rows - n, 3 * tile), F32)], axis=0)
             plane = pltpu.roll(plane, row, 0)
-            plane = jnp.concatenate([plane, jnp.zeros((rows, 3 * tile - n), F32)], axis=1)
-            plane = pltpu.roll(plane, col, 1)
 
             @pl.when(position == 0)
             def _():

time: 132 us -> 134 us (1.015)
  transfers between devices with their start and end apart: 17 -> 17, of which waited for: 11 -> 11; matrix products, arithmetic and copies ran while one was open for 3% -> 3% of each run, Pallas kernels for 15% -> 16%
where the time goes in v7:
time: 134 us; the launch traced here: 133 us
  Pallas kernels  34.2 us (26%)
  starting transfers between devices  33.1 us (25%)
  waiting for transfers between devices  32.9 us (25%)
  blocking collectives  21.5 us (16%)
  other arithmetic  6.74 us (5%)
  local copies, waits for them, and re-layouts  3.95 us (3%)
    all_to_all x1, blocking collectives, exchanged(): lax.all_to_all(value, axis, 0, 0, tiled=True, axis_index_groups=groups)  21.5 us
    ppermute x10, starting transfers between devices, around(): lax.ppermute(value, axis, [(at, (at + steps) % count) for at in range(cou...  17.2 us
    pallas_call x1, Pallas kernels, forward(): pl.pallas_call(forward_kernel, out_shape=(jax.ShapeDtypeStruct((count, 2,...  14.5 us
    ppermute x10, waiting for transfers between devices, around(): lax.ppermute(value, axis, [(at, (at + steps) % count) for at in range(cou...  14 us
    pallas_call x1, Pallas kernels, backward(): pl.pallas_call(backward_kernel, out_shape=(jax.ShapeDtypeStruct((count, 2...  13.4 us
    ppermute x3, waiting for transfers between devices, across(): return lax.ppermute(value, 'tile', step)  9.16 us
    ppermute x2, starting transfers between devices, swapped(): lax.ppermute(value, 'tile', [(at, at ^ 1) for at in range(lax.axis_size('...  6.07 us
    all_to_all x1, waiting for transfers between devices, exchanged(): lax.all_to_all(value, axis, 0, 0, tiled=True, axis_index_groups=groups)  5.29 us
  transfers between devices with their start and end apart: 17, of which 11 were waited for; matrix products, arithmetic and copies ran while one was open for 3% of the time, Pallas kernels for 16%

profile of v7, /device:TPU:1, one launch (start us, length us, event | category | flops | bytes accessed | tf_op | source)
XLA Modules:
  0.0 133.1 jit_solution(4432241138399098503)
XLA Ops:
  2.4 2.2 %collective-permute-start = (f32[2,2,136,128]{3,2,1,0:T(8,128)S(1)}, f32[2,2,136,128]{3,2,1,0:T(8,128)S(1)}, u32[]{:S(2)}, u32[]{:S(2)}) collective-permute-start(f32[2,2,136,128]{3,2,1,0:T(8,128)S(1)} %pad_maximum_fusion), channel_id=1, source_target_pairs={{0,16},{16,32},{32,48},{48,64},{64,80},{80,96},{96,112},{112,128},... | collective-permute-start | bytes 835592 | tf_op jit(solution)/shard_map/ppermute | solution.py:434
  4.6 2.5 %collective-permute-start.2 = (f32[2,2,128,128]{3,2,1,0:T(8,128)}, f32[2,2,128,128]{3,2,1,0:T(8,128)S(1)}, u32[]{:S(2)}, u32[]{:S(2)}) collective-permute-start(f32[2,2,128,128]{3,2,1,0:T(8,128)} %middle.1), channel_id=1, source_target_pairs={{0,1},{1,2},{2,3},{3,4},{4,5},{5,6},{6,7},{7,8},{8,9},{9,10},{10,1... | collective-permute-start | bytes 786440 | tf_op jit(solution)/shard_map/ppermute | solution.py:434
  7.1 3.5 %collective-permute-start.1 = (f32[2,2,128,128]{3,2,1,0:T(8,128)}, f32[2,2,128,128]{3,2,1,0:T(8,128)S(1)}, u32[]{:S(2)}, u32[]{:S(2)}) collective-permute-start(f32[2,2,128,128]{3,2,1,0:T(8,128)} %middle.1), channel_id=1, source_target_pairs={{0,240},{16,0},{32,16},{48,32},{64,48},{80,64},{96,80},{112,96},{1... | collective-permute-start | bytes 786440 | tf_op jit(solution)/shard_map/ppermute | solution.py:434
  11.1 5.3 %collective-permute-done.1 = f32[2,2,128,128]{3,2,1,0:T(8,128)S(1)} collective-permute-done((f32[2,2,128,128]{3,2,1,0:T(8,128)}, f32[2,2,128,128]{3,2,1,0:T(8,128)S(1)}, u32[]{:S(2)}, u32[]{:S(2)}) %collective-permute-start.1) | collective-permute-done | bytes 262176 | tf_op jit(solution)/shard_map/ppermute | solution.py:434
  16.7 2.0 %collective-permute-start.5 = (f32[2,2,264,128]{3,2,1,0:T(8,128)S(1)}, f32[2,2,264,128]{3,2,1,0:T(8,128)S(1)}, u32[]{:S(2)}, u32[]{:S(2)}) collective-permute-start(f32[2,2,264,128]{3,2,1,0:T(8,128)S(1)} %constant_dynamic-update-slice_fusion.middle_edges), channel_id=1, source_target_pairs={{0,15},{1,0},{2,1},{3,2},{4,3},{5,4},{6,5},{7,6},{8,7},{9,8},{10,9... | collective-permute-start | bytes 1622024 | tf_op jit(solution)/shard_map/ppermute | solution.py:434
  22.3 1.8 %prepare.1 = (f32[2,4,256,256]{3,2,1,0:T(8,128)S(1)}, f32[2,256,256]{2,1,0:T(8,128)S(1)}, bf16[4,2,2,256,256]{4,3,2,1,0:T(8,128)(2,1)S(1)}) custom-call(f32[2,4,256,256]{3,2,1,0:T(8,128)S(1)} %copy-done.1, f32[2,256,256]{2,1,0:T(8,128)S(1)} %copy-done.2, bf16[2,2,2,2,128,128]{5,4,3,2,1,0:T(8,128)(2,1)S(1)} %copy-done.4), custom_call_target="tpu_custom_call" | custom-call | flops 3221225472 | bytes 6291456 | tf_op jit(solution)/shard_map/prepare/pallas_call | solution.py:188
  25.8 14.5 %forward.1 = (f32[2,2,2,256,256]{4,3,2,1,0:T(8,128)S(1)}, f32[2,2,4,256,256]{4,3,2,1,0:T(8,128)S(1)}, f32[2,2,4,256,256]{4,3,2,1,0:T(8,128)S(1)}, f32[2,256,256]{2,1,0:T(8,128)S(1)}, s32[2,2]{1,0:T(2,128)S(1)}) custom-call(f32[2,2,128,128]{3,2,1,0:T(8,128)S(1)} %collective-permute-done.2.left, f32[2,2,264,128]{3,2,1,0:T(8,128)S(1)} %collective-permute-done.4.left_edges, ...), custom_call_target="tpu_custom_call" | custom-call | flops 12884901888 | bytes 18874368 | tf_op jit(solution)/shard_map/forward/pallas_call | solution.py:272
  40.3 2.9 %collective-permute-done.6.measured = f32[2,256,256]{2,1,0:T(8,128)S(1)} collective-permute-done((f32[2,256,256]{2,1,0:T(8,128)S(1)}, f32[2,256,256]{2,1,0:T(8,128)S(1)}, u32[]{:S(2)}, u32[]{:S(2)}) %collective-permute-start.6) | collective-permute-done | bytes 524320 | tf_op jit(solution)/shard_map/ppermute | solution.py:476
  43.2 13.4 %backward.1 = (f32[2,2,2,256,256]{4,3,2,1,0:T(8,128)S(1)}, f32[4,256,256]{2,1,0:T(8,128)S(1)}, f32[4,256,256]{2,1,0:T(8,128)S(1)}) custom-call(s32[1]{0:T(128)} %bitcast.core, f32[2,2,2,256,256]{4,3,2,1,0:T(8,128)S(1)} %get-tuple-element.39.window, f32[2,2,4,256,256]{4,3,2,1,0:T(8,128)S(1)} %get-tuple-element.40.moved, ...), custom_call_target="tpu_custom_call" | custom-call | flops 12884901888 | bytes 18874368 | tf_op jit(solution)/shard_map/backward/pallas_call | solution.py:362
  56.6 3.3 %collective-permute-start.7 = (f32[4,256,256]{2,1,0:T(8,128)S(1)}, f32[4,256,256]{2,1,0:T(8,128)S(1)}, u32[]{:S(2)}, u32[]{:S(2)}) collective-permute-start(f32[4,256,256]{2,1,0:T(8,128)S(1)} %get-tuple-element.45), channel_id=1, source_target_pairs={{0,1},{1,0},{2,3},{3,2},{4,5},{5,4},{6,7},{7,6},{8,9},{9,8},{10,11... | collective-permute-start | bytes 3145736 | tf_op jit(solution)/shard_map/ppermute | solution.py:446
  59.9 4.5 %place.1 = (f32[2,2,384,128]{3,2,1,0:T(8,128)S(1)}, f32[2,2,384,128]{3,2,1,0:T(8,128)S(1)}, f32[2,2,384,128]{3,2,1,0:T(8,128)S(1)}) custom-call(s32[2,2]{1,0:T(2,128)S(1)} %get-tuple-element.46.scalars, f32[2,2,2,256,256]{4,3,2,1,0:T(8,128)S(1)} %get-tuple-element.47.totals), custom_call_target="tpu_custom_call" | custom-call | flops 2147483648 | bytes 8388608 | tf_op jit(solution)/shard_map/place/pallas_call | solution.py:417
  64.4 1.7 %collective-permute-start.9 = (f32[2,2,384,128]{3,2,1,0:T(8,128)S(1)}, f32[2,2,384,128]{3,2,1,0:T(8,128)}, u32[]{:S(2)}, u32[]{:S(2)}) collective-permute-start(f32[2,2,384,128]{3,2,1,0:T(8,128)S(1)} %get-tuple-element.54), channel_id=1, source_target_pairs={{0,1},{1,2},{2,3},{3,4},{4,5},{5,6},{6,7},{7,8},{8,9},{9,10},{10,1... | collective-permute-start | bytes 2359304 | tf_op jit(solution)/shard_map/ppermute | solution.py:434
  67.3 4.8 %all-to-all-start = ((f32[16,64,256]{2,1,0:T(8,128)}), f32[16,64,256]{2,1,0:T(8,128)S(1)}, u32[]{:S(2)}, u32[]{:S(2)}) async-start(f32[16,64,256]{2,1,0:T(8,128)} %bitcast.3), calls=%async_computation | async-start | bytes 2097152 | tf_op jit(solution)/shard_map/all_to_all | solution.py:438
  72.1 4.1 %collective-permute-done.8 = f32[2,2,384,128]{3,2,1,0:T(8,128)} collective-permute-done((f32[2,2,384,128]{3,2,1,0:T(8,128)S(1)}, f32[2,2,384,128]{3,2,1,0:T(8,128)}, u32[]{:S(2)}, u32[]{:S(2)}) %collective-permute-start.8) | collective-permute-done | bytes 786464 | tf_op jit(solution)/shard_map/ppermute | solution.py:434
  77.8 4.8 %collective-permute-start.11 = (f32[2,2,128,128]{3,2,1,0:T(8,128)S(1)}, f32[2,2,128,128]{3,2,1,0:T(8,128)S(1)}, u32[]{:S(2)}, u32[]{:S(2)}) collective-permute-start(f32[2,2,128,128]{3,2,1,0:T(8,128)S(1)} %get-tuple-element.61), channel_id=1, source_target_pairs={{0,240},{16,0},{32,16},{48,32},{64,48},{80,64},{96,80},{112,96},{1... | collective-permute-start | bytes 786440 | tf_op jit(solution)/shard_map/ppermute | solution.py:434
  82.6 5.3 %all-to-all-done = f32[16,64,256]{2,1,0:T(8,128)S(1)} async-done(((f32[16,64,256]{2,1,0:T(8,128)}), f32[16,64,256]{2,1,0:T(8,128)S(1)}, u32[]{:S(2)}, u32[]{:S(2)}) %all-to-all-start) | async-done | bytes 1048608 | tf_op jit(solution)/shard_map/all_to_all | solution.py:438
  88.1 3.0 %collective-permute-done.10 = f32[32,256]{1,0:T(8,128)S(1)} collective-permute-done((f32[32,256]{1,0:T(8,128)S(1)}, f32[32,256]{1,0:T(8,128)S(1)}, u32[]{:S(2)}, u32[]{:S(2)}) %collective-permute-start.10) | collective-permute-done | bytes 32800 | tf_op jit(solution)/shard_map/ppermute | solution.py:507
  91.2 3.0 %collective-permute-done.12 = f32[2,2,128,128]{3,2,1,0:T(8,128)S(1)} collective-permute-done((f32[2,2,128,128]{3,2,1,0:T(8,128)S(1)}, f32[2,2,128,128]{3,2,1,0:T(8,128)S(1)}, u32[]{:S(2)}, u32[]{:S(2)}) %collective-permute-start.12) | collective-permute-done | bytes 262176 | tf_op jit(solution)/shard_map/ppermute | solution.py:434
  94.2 3.9 %collective-permute-done.13 = f32[32,256]{1,0:T(8,128)S(1)} collective-permute-done((f32[32,256]{1,0:T(8,128)S(1)}, f32[32,256]{1,0:T(8,128)S(1)}, u32[]{:S(2)}, u32[]{:S(2)}) %collective-permute-start.13) | collective-permute-done | bytes 32800 | tf_op jit(solution)/shard_map/ppermute | solution.py:507
  98.1 4.5 %collective-permute-start.14 = (f32[32,256]{1,0:T(8,128)S(1)}, f32[32,256]{1,0:T(8,128)S(1)}, u32[]{:S(2)}, u32[]{:S(2)}) collective-permute-start(f32[32,256]{1,0:T(8,128)S(1)} %add.51), channel_id=1, source_target_pairs={{0,8},{1,9},{2,10},{3,11},{4,12},{5,13},{6,14},{7,15},{8,0},{9,1},... | collective-permute-start | bytes 98312 | tf_op jit(solution)/shard_map/ppermute | solution.py:507
  102.6 2.2 %collective-permute-done.14 = f32[32,256]{1,0:T(8,128)S(1)} collective-permute-done((f32[32,256]{1,0:T(8,128)S(1)}, f32[32,256]{1,0:T(8,128)S(1)}, u32[]{:S(2)}, u32[]{:S(2)}) %collective-permute-start.14) | collective-permute-done | bytes 32800 | tf_op jit(solution)/shard_map/ppermute | solution.py:507
  104.9 21.5 %all_to_all.10 = f32[32,32,256]{2,1,0:T(8,128)S(1)} all-to-all(f32[32,32,256]{2,1,0:T(8,128)S(1)} %broadcast_in_dim.45), channel_id=1, replica_groups={{0,2,16,18,32,34,48,50,64,66,80,82,96,98,112,114,128,130,144,146,160,16..., dimensions={0} | all-to-all | bytes 2097152 | tf_op jit(solution)/shard_map/all_to_all | solution.py:438
  126.4 2.8 %collective-permute-start.15 = (f32[32,32,256]{2,1,0:T(8,128)S(1)}, f32[32,32,256]{2,1,0:T(8,128)S(1)}, u32[]{:S(2)}, u32[]{:S(2)}) collective-permute-start(f32[32,32,256]{2,1,0:T(8,128)S(1)} %all_to_all.10), channel_id=1, source_target_pairs={{0,1},{1,0},{2,3},{3,2},{4,5},{5,4},{6,7},{7,6},{8,9},{9,8},{10,11... | collective-permute-start | bytes 3145736 | tf_op jit(solution)/shard_map/ppermute | solution.py:446
  131.5 1.6 %broadcast_select_fusion = f32[2,4,256,256]{3,2,1,0:T(8,128)} fusion(f32[4,256,256]{2,1,0:T(8,128)S(1)} %bitcast.12, f32[4,256,256]{2,1,0:T(8,128)S(1)} %bitcast.11, pred[2]{0:T(512)(128)(4,1)S(1)} %iota_compare_fusion), kind=kLoop, calls=%fused_computation | loop fusion | flops 524288 | bytes 4194306 | tf_op jit(solution)/shard_map/jit(_where)/select_n | solution.py:523
  (43 shorter events, 13.3 us)
Async XLA Ops:
  2.4 14.2 %collective-permute-start = (f32[2,2,136,128]{3,2,1,0:T(8,128)S(1)}, f32[2,2,136,128]{3,2,1,0:T(8,128)S(1)}, u32[]{:S(2)}, u32[]{:S(2)}) collective-permute-start(f32[2,2,136,128]{3,2,1,0:T(8,128)S(1)} %pad_maximum_fusion), channel_id=1, source_target_pairs={{0,16},{16,32},{32,48},{48,64},{64,80},{80,96},{96,112},{112,128},... | collective-permute-start | bytes 835592 | tf_op jit(solution)/shard_map/ppermute | solution.py:434
  4.6 6.5 %collective-permute-start.2 = (f32[2,2,128,128]{3,2,1,0:T(8,128)}, f32[2,2,128,128]{3,2,1,0:T(8,128)S(1)}, u32[]{:S(2)}, u32[]{:S(2)}) collective-permute-start(f32[2,2,128,128]{3,2,1,0:T(8,128)} %middle.1), channel_id=1, source_target_pairs={{0,1},{1,2},{2,3},{3,4},{4,5},{5,6},{6,7},{7,8},{8,9},{9,10},{10,1... | collective-permute-start | bytes 786440 | tf_op jit(solution)/shard_map/ppermute | solution.py:434
  7.1 9.3 %collective-permute-start.1 = (f32[2,2,128,128]{3,2,1,0:T(8,128)}, f32[2,2,128,128]{3,2,1,0:T(8,128)S(1)}, u32[]{:S(2)}, u32[]{:S(2)}) collective-permute-start(f32[2,2,128,128]{3,2,1,0:T(8,128)} %middle.1), channel_id=1, source_target_pairs={{0,240},{16,0},{32,16},{48,32},{64,48},{80,64},{96,80},{112,96},{1... | collective-permute-start | bytes 786440 | tf_op jit(solution)/shard_map/ppermute | solution.py:434
  10.6 6.0 %collective-permute-start.3 = (f32[2,2,128,128]{3,2,1,0:T(8,128)}, f32[2,2,128,128]{3,2,1,0:T(8,128)S(1)}, u32[]{:S(2)}, u32[]{:S(2)}) collective-permute-start(f32[2,2,128,128]{3,2,1,0:T(8,128)} %middle.1), channel_id=1, source_target_pairs={{0,15},{1,0},{2,1},{3,2},{4,3},{5,4},{6,5},{7,6},{8,7},{9,8},{10,9... | collective-permute-start | bytes 786440 | tf_op jit(solution)/shard_map/ppermute | solution.py:434
  16.7 9.1 %collective-permute-start.5 = (f32[2,2,264,128]{3,2,1,0:T(8,128)S(1)}, f32[2,2,264,128]{3,2,1,0:T(8,128)S(1)}, u32[]{:S(2)}, u32[]{:S(2)}) collective-permute-start(f32[2,2,264,128]{3,2,1,0:T(8,128)S(1)} %constant_dynamic-update-slice_fusion.middle_edges), channel_id=1, source_target_pairs={{0,15},{1,0},{2,1},{3,2},{4,3},{5,4},{6,5},{7,6},{8,7},{9,8},{10,9... | collective-permute-start | bytes 1622024 | tf_op jit(solution)/shard_map/ppermute | solution.py:434
  18.6 7.1 %collective-permute-start.4 = (f32[2,2,264,128]{3,2,1,0:T(8,128)S(1)}, f32[2,2,264,128]{3,2,1,0:T(8,128)S(1)}, u32[]{:S(2)}, u32[]{:S(2)}) collective-permute-start(f32[2,2,264,128]{3,2,1,0:T(8,128)S(1)} %constant_dynamic-update-slice_fusion.middle_edges), channel_id=1, source_target_pairs={{0,1},{1,2},{2,3},{3,4},{4,5},{5,6},{6,7},{7,8},{8,9},{9,10},{10,1... | collective-permute-start | bytes 1622024 | tf_op jit(solution)/shard_map/ppermute | solution.py:434
  18.6 1.6 %copy-start.1 = (f32[2,4,256,256]{3,2,1,0:T(8,128)S(1)}, f32[2,4,256,256]{3,2,1,0:T(8,128)}, u32[]{:S(2)}) copy-start(f32[2,4,256,256]{3,2,1,0:T(8,128)} %probe_in.1) | copy-start | bytes 6291460
  20.2 1.0 copy-start.2
  21.3 1.0 copy-start.4
  22.3 3.5 %copy-start = (f32[2,2,128,128]{3,2,1,0:T(8,128)S(1)}, f32[2,2,128,128]{3,2,1,0:T(8,128)}, u32[]{:S(2)}) copy-start(f32[2,2,128,128]{3,2,1,0:T(8,128)} %middle.1) | copy-start | bytes 786436
  22.3 3.5 %copy-start.3 = (f32[2,256,256]{2,1,0:T(8,128)S(1)}, f32[2,256,256]{2,1,0:T(8,128)}, u32[]{:S(2)}) copy-start(f32[2,256,256]{2,1,0:T(8,128)} %constant.54.clone.phase) | copy-start | bytes 1572868
  24.1 19.1 %collective-permute-start.6 = (f32[2,256,256]{2,1,0:T(8,128)S(1)}, f32[2,256,256]{2,1,0:T(8,128)S(1)}, u32[]{:S(2)}, u32[]{:S(2)}) collective-permute-start(f32[2,256,256]{2,1,0:T(8,128)S(1)} %get-tuple-element.43), channel_id=1, source_target_pairs={{0,17},{1,18},{2,19},{3,20},{4,21},{5,22},{6,23},{7,24},{8,25},{9,... | collective-permute-start | bytes 1572872 | tf_op jit(solution)/shard_map/ppermute | solution.py:476
  56.6 7.8 %collective-permute-start.7 = (f32[4,256,256]{2,1,0:T(8,128)S(1)}, f32[4,256,256]{2,1,0:T(8,128)S(1)}, u32[]{:S(2)}, u32[]{:S(2)}) collective-permute-start(f32[4,256,256]{2,1,0:T(8,128)S(1)} %get-tuple-element.45), channel_id=1, source_target_pairs={{0,1},{1,0},{2,3},{3,2},{4,5},{5,4},{6,7},{7,6},{8,9},{9,8},{10,11... | collective-permute-start | bytes 3145736 | tf_op jit(solution)/shard_map/ppermute | solution.py:446
  64.4 11.8 %collective-permute-start.8 = (f32[2,2,384,128]{3,2,1,0:T(8,128)S(1)}, f32[2,2,384,128]{3,2,1,0:T(8,128)}, u32[]{:S(2)}, u32[]{:S(2)}) collective-permute-start(f32[2,2,384,128]{3,2,1,0:T(8,128)S(1)} %get-tuple-element.53), channel_id=1, source_target_pairs={{0,15},{1,0},{2,1},{3,2},{4,3},{5,4},{6,5},{7,6},{8,7},{9,8},{10,9... | collective-permute-start | bytes 2359304 | tf_op jit(solution)/shard_map/ppermute | solution.py:434
  64.4 11.8 %collective-permute-start.9 = (f32[2,2,384,128]{3,2,1,0:T(8,128)S(1)}, f32[2,2,384,128]{3,2,1,0:T(8,128)}, u32[]{:S(2)}, u32[]{:S(2)}) collective-permute-start(f32[2,2,384,128]{3,2,1,0:T(8,128)S(1)} %get-tuple-element.54), channel_id=1, source_target_pairs={{0,1},{1,2},{2,3},{3,4},{4,5},{5,6},{6,7},{7,8},{8,9},{9,10},{10,1... | collective-permute-start | bytes 2359304 | tf_op jit(solution)/shard_map/ppermute | solution.py:434
  67.3 20.6 %all-to-all-start = ((f32[16,64,256]{2,1,0:T(8,128)}), f32[16,64,256]{2,1,0:T(8,128)S(1)}, u32[]{:S(2)}, u32[]{:S(2)}) async-start(f32[16,64,256]{2,1,0:T(8,128)} %bitcast.3), calls=%async_computation | async-start | bytes 2097152 | tf_op jit(solution)/shard_map/all_to_all | solution.py:438
  77.8 16.4 %collective-permute-start.12 = (f32[2,2,128,128]{3,2,1,0:T(8,128)S(1)}, f32[2,2,128,128]{3,2,1,0:T(8,128)S(1)}, u32[]{:S(2)}, u32[]{:S(2)}) collective-permute-start(f32[2,2,128,128]{3,2,1,0:T(8,128)S(1)} %get-tuple-element.60), channel_id=1, source_target_pairs={{0,16},{16,32},{32,48},{48,64},{64,80},{80,96},{96,112},{112,128},... | collective-permute-start | bytes 786440 | tf_op jit(solution)/shard_map/ppermute | solution.py:434
  77.8 16.3 %collective-permute-start.11 = (f32[2,2,128,128]{3,2,1,0:T(8,128)S(1)}, f32[2,2,128,128]{3,2,1,0:T(8,128)S(1)}, u32[]{:S(2)}, u32[]{:S(2)}) collective-permute-start(f32[2,2,128,128]{3,2,1,0:T(8,128)S(1)} %get-tuple-element.61), channel_id=1, source_target_pairs={{0,240},{16,0},{32,16},{48,32},{64,48},{80,64},{96,80},{112,96},{1... | collective-permute-start | bytes 786440 | tf_op jit(solution)/shard_map/ppermute | solution.py:434
  88.0 3.1 %collective-permute-start.10 = (f32[32,256]{1,0:T(8,128)S(1)}, f32[32,256]{1,0:T(8,128)S(1)}, u32[]{:S(2)}, u32[]{:S(2)}) collective-permute-start(f32[32,256]{1,0:T(8,128)S(1)} %dynamic-slice_bitcast_fusion), channel_id=1, source_target_pairs={{0,2},{1,3},{2,0},{3,1},{4,6},{5,7},{6,4},{7,5},{8,10},{9,11},{10,... | collective-permute-start | bytes 98312 | tf_op jit(solution)/shard_map/ppermute | solution.py:507
  94.1 4.0 %collective-permute-start.13 = (f32[32,256]{1,0:T(8,128)S(1)}, f32[32,256]{1,0:T(8,128)S(1)}, u32[]{:S(2)}, u32[]{:S(2)}) collective-permute-start(f32[32,256]{1,0:T(8,128)S(1)} %bitcast_add_fusion), channel_id=1, source_target_pairs={{0,4},{1,5},{2,6},{3,7},{4,0},{5,1},{6,2},{7,3},{8,12},{9,13},{10,... | collective-permute-start | bytes 98312 | tf_op jit(solution)/shard_map/ppermute | solution.py:507
  98.1 6.7 %collective-permute-start.14 = (f32[32,256]{1,0:T(8,128)S(1)}, f32[32,256]{1,0:T(8,128)S(1)}, u32[]{:S(2)}, u32[]{:S(2)}) collective-permute-start(f32[32,256]{1,0:T(8,128)S(1)} %add.51), channel_id=1, source_target_pairs={{0,8},{1,9},{2,10},{3,11},{4,12},{5,13},{6,14},{7,15},{8,0},{9,1},... | collective-permute-start | bytes 98312 | tf_op jit(solution)/shard_map/ppermute | solution.py:507
  126.4 5.1 %collective-permute-start.15 = (f32[32,32,256]{2,1,0:T(8,128)S(1)}, f32[32,32,256]{2,1,0:T(8,128)S(1)}, u32[]{:S(2)}, u32[]{:S(2)}) collective-permute-start(f32[32,32,256]{2,1,0:T(8,128)S(1)} %all_to_all.10), channel_id=1, source_target_pairs={{0,1},{1,0},{2,3},{3,2},{4,5},{5,4},{6,7},{7,6},{8,9},{9,8},{10,11... | collective-permute-start | bytes 3145736 | tf_op jit(solution)/shard_map/ppermute | solution.py:446
